TPU v7x, 32 devices: a whole 2x2x4 slice. The times are simulated.
32 devices in a mesh: dp: 16 (over z, y, core), fsdp: 2 (over x).
Axes of the slice: x: 2, y: 2, z: 4, core: 2. Of those that a mesh axis runs over, the one named last changes fastest.
Arguments:
- activations: bfloat16 [32, 768, 960], P(('dp', 'fsdp')), may hold values from -6 to 6
- doc_ids: int32 [32, 768], P(('dp', 'fsdp')), may hold values from 0 to 2, never falling along the last dimension, each value on 1 to 384 neighbouring positions
- w_query: bfloat16 [960, 960], P('fsdp'), may hold values from -0.1875 to 0.1875
- key_projection: bfloat16 [960, 320], P('fsdp'), may hold values from -0.1875 to 0.1875
- value_projection: bfloat16 [960, 320], P('fsdp'), may hold values from -0.1875 to 0.1875
- w_out: bfloat16 [960, 960], P('fsdp'), may hold values from -0.75 to 0.75
- gain_attn: bfloat16 [960], P('fsdp'), may hold values from 0.5 to 1.5
- gain_ffn: bfloat16 [960], P('fsdp'), may hold values from 0.5 to 1.5
- w_gate: bfloat16 [960, 2560], P('fsdp'), may hold values from -0.1875 to 0.1875
- w_up: bfloat16 [960, 2560], P('fsdp'), may hold values from -0.1875 to 0.1875
- w_down: bfloat16 [2560, 960], P('fsdp'), may hold values from -0.15625 to 0.15625
- cotangent: bfloat16 [32, 768, 960], P(('dp', 'fsdp')), may hold values from -6 to 6
Outputs:
- block_out: bfloat16 [32, 768, 960], P(('dp', 'fsdp'))
- grad_in: bfloat16 [32, 768, 960], P(('dp', 'fsdp'))
- grad_query: float32 [960, 960], P('fsdp')
- grad_key: float32 [960, 320], P('fsdp')
- grad_value: float32 [960, 320], P('fsdp')
- grad_out: float32 [960, 960], P('fsdp')
- grad_gain_attn: float32 [960], P('fsdp')
- grad_gain_ffn: float32 [960], P('fsdp')
- grad_gate: float32 [960, 2560], P('fsdp')
- grad_up: float32 [960, 2560], P('fsdp')
- grad_down: float32 [2560, 960], P('fsdp')
Inputs may be any that keep to these rules, and one draw needn't show every extreme that they name: `doc_ids`: document numbers never fall along a sequence; a document holds at most 384 tokens, and some document holds exactly that many.
All inputs are finite; a program needn't handle non-finite values.
Results may differ from a plain program's by a relative error of at most 0.03.
Values may be sent and summed in bfloat16 or wider, within the bound.
No kernel may reach another device: no remote copies, remote signals or barrier semaphores. Data moves between devices by JAX's collectives and lax.ppermute only.
A program may use at most 192 MiB of HBM per device.

v0:
```python
from functools import partial

import jax
import jax.numpy as jnp
from jax import lax
from jax.sharding import PartitionSpec as P

QUERY_HEADS = 15
KEY_VALUE_HEADS = 5
HEAD_SIZE = 64


EPSILON = 1e-05
ROPE_BASE = 10000.0
NEGATIVE = -1e30


def matrix_product(left_mat, right_mat):
    return jnp.dot(left_mat, right_mat, preferred_element_type=jnp.float32)


def left_contract(left_mat, right_mat):
    return lax.dot_general(
        left_mat, right_mat, (((0,), (0,)), ((), ())), preferred_element_type=jnp.float32
    )


def right_contract(left_mat, right_mat):
    return lax.dot_general(
        left_mat, right_mat, (((1,), (1,)), ((), ())), preferred_element_type=jnp.float32
    )


def doc_tables(doc_row):
    token_index = jnp.arange(doc_row.shape[0])
    same_doc = doc_row[:, None] == doc_row[None, :]
    earlier = token_index[None, :] < token_index[:, None]
    places = jnp.sum(jnp.where(same_doc & earlier, 1.0, 0.0).astype(jnp.float32), axis=1)
    halves = HEAD_SIZE // 2
    frequency = ROPE_BASE ** (-2.0 * jnp.arange(halves, dtype=jnp.float32) / HEAD_SIZE)
    angles = places[:, None] * frequency[None, :]
    allowed = same_doc & (token_index[None, :] <= token_index[:, None])
    return (jnp.cos(angles), jnp.sin(angles), allowed)


def apply_rotation(inputs, cosine_table, sine_table):
    halves = inputs.shape[-1] // 2
    first_half = inputs[..., :halves]
    second_half = inputs[..., halves:]
    cosine_row = cosine_table[:, None, :]
    sine_row = sine_table[:, None, :]
    return jnp.concatenate(
        [
            first_half * cosine_row - second_half * sine_row,
            second_half * cosine_row + first_half * sine_row,
        ],
        axis=-1,
    )


def norm_forward(inputs, gain_vec):
    inverse = lax.rsqrt(jnp.mean(inputs * inputs, axis=-1, keepdims=True) + EPSILON)
    return ((inputs * inverse * gain_vec.astype(jnp.float32)).astype(jnp.bfloat16), inverse)


def norm_backward(inputs, inverse, gain_vec, incoming_gradient):
    scaled = gain_vec.astype(jnp.float32) * incoming_gradient
    inner_mean = jnp.mean(scaled * inputs, axis=-1, keepdims=True)
    grad_inputs = inverse * scaled - inputs * inverse**3 * inner_mean
    grad_gain = jnp.sum(incoming_gradient * inputs * inverse, axis=0)
    return (grad_inputs, grad_gain)


def head_scores(query_rows, rotated_keys, allowed):
    scores = jnp.einsum(
        "qgd,sd->gqs", query_rows, rotated_keys, preferred_element_type=jnp.float32
    ) * HEAD_SIZE ** (-0.5)
    return jnp.where(allowed[None], scores, NEGATIVE)


def head_forward(pieces, allowed):
    query_rows, rotated_keys, value_rows = pieces
    scores = head_scores(query_rows, rotated_keys, allowed)
    row_max = jnp.max(scores, axis=-1, keepdims=True)
    exp_scores = jnp.exp(scores - row_max)
    row_sum = jnp.sum(exp_scores, axis=-1, keepdims=True)
    attn_probs = (exp_scores / row_sum).astype(jnp.bfloat16)
    attn_mix = jnp.einsum("gqs,sd->qgd", attn_probs, value_rows, preferred_element_type=jnp.float32)
    return (attn_mix, (row_max + jnp.log(row_sum))[..., 0])


def head_backward(pieces, allowed):
    query_rows, rotated_keys, value_rows, logsum, incoming_gradient = pieces
    scores = head_scores(query_rows, rotated_keys, allowed)
    attn_probs = jnp.where(allowed[None], jnp.exp(scores - logsum[..., None]), 0.0)
    grad_probs = jnp.einsum(
        "qgd,sd->gqs", incoming_gradient, value_rows, preferred_element_type=jnp.float32
    )
    value_gradient_rows = jnp.einsum(
        "gqs,qgd->sd",
        attn_probs.astype(jnp.bfloat16),
        incoming_gradient,
        preferred_element_type=jnp.float32,
    )
    grad_scores = attn_probs * (
        grad_probs - jnp.sum(attn_probs * grad_probs, axis=-1, keepdims=True)
    )
    grad_scores = grad_scores.astype(jnp.bfloat16)
    score_scale = HEAD_SIZE ** (-0.5)
    grad_queries = (
        jnp.einsum("gqs,sd->qgd", grad_scores, rotated_keys, preferred_element_type=jnp.float32)
        * score_scale
    )
    key_gradient_rows = (
        jnp.einsum("gqs,qgd->sd", grad_scores, query_rows, preferred_element_type=jnp.float32)
        * score_scale
    )
    return (grad_queries, key_gradient_rows, value_gradient_rows)


def attend(query_rows, rotated_keys, value_rows, allowed):
    sequence_length = query_rows.shape[0]
    grouped_rows = jnp.moveaxis(
        query_rows.reshape(
            sequence_length, KEY_VALUE_HEADS, QUERY_HEADS // KEY_VALUE_HEADS, HEAD_SIZE
        ),
        1,
        0,
    )
    attn_mix, logsum = lax.map(
        partial(head_forward, allowed=allowed),
        (grouped_rows, jnp.moveaxis(rotated_keys, 1, 0), jnp.moveaxis(value_rows, 1, 0)),
    )
    return (
        jnp.moveaxis(attn_mix, 0, 1)
        .reshape(sequence_length, QUERY_HEADS * HEAD_SIZE)
        .astype(jnp.bfloat16),
        logsum,
    )


def attend_back(query_rows, rotated_keys, value_rows, logsum, incoming_gradient, allowed):
    sequence_length = query_rows.shape[0]
    grouped_rows = jnp.moveaxis(
        query_rows.reshape(
            sequence_length, KEY_VALUE_HEADS, QUERY_HEADS // KEY_VALUE_HEADS, HEAD_SIZE
        ),
        1,
        0,
    )
    incoming_head_gradient = jnp.moveaxis(
        incoming_gradient.reshape(
            sequence_length, KEY_VALUE_HEADS, QUERY_HEADS // KEY_VALUE_HEADS, HEAD_SIZE
        ),
        1,
        0,
    )
    grad_queries, key_gradient_rows, value_gradient_rows = lax.map(
        partial(head_backward, allowed=allowed),
        (
            grouped_rows,
            jnp.moveaxis(rotated_keys, 1, 0),
            jnp.moveaxis(value_rows, 1, 0),
            logsum,
            incoming_head_gradient,
        ),
    )
    grad_queries = jnp.moveaxis(grad_queries, 0, 1).reshape(sequence_length, QUERY_HEADS, HEAD_SIZE)
    return (
        grad_queries,
        jnp.moveaxis(key_gradient_rows, 0, 1),
        jnp.moveaxis(value_gradient_rows, 0, 1),
    )


def layer_forward(inputs, params, tables):
    w_query, key_projection, value_projection, w_out, gain_attn, gain_ffn, w_gate, w_up, w_down = (
        params
    )
    cosine_table, sine_table, allowed = tables
    sequence_length = inputs.shape[0]
    normalized_input, inverse_attn = norm_forward(inputs, gain_attn)
    query_rows = apply_rotation(
        matrix_product(normalized_input, w_query).reshape(sequence_length, QUERY_HEADS, HEAD_SIZE),
        cosine_table,
        sine_table,
    ).astype(jnp.bfloat16)
    rotated_keys = apply_rotation(
        matrix_product(normalized_input, key_projection).reshape(
            sequence_length, KEY_VALUE_HEADS, HEAD_SIZE
        ),
        cosine_table,
        sine_table,
    ).astype(jnp.bfloat16)
    value_rows = (
        matrix_product(normalized_input, value_projection)
        .astype(jnp.bfloat16)
        .reshape(sequence_length, KEY_VALUE_HEADS, HEAD_SIZE)
    )
    attn_mix, logsum = attend(query_rows, rotated_keys, value_rows, allowed)
    middle = inputs + matrix_product(attn_mix, w_out)
    normed_ffn, inverse_ffn = norm_forward(middle, gain_ffn)
    gate_pre = matrix_product(normed_ffn, w_gate)
    up_pre = matrix_product(normed_ffn, w_up)
    activated = (jax.nn.silu(gate_pre) * up_pre).astype(jnp.bfloat16)
    outputs = middle + matrix_product(activated, w_down)
    stored = (
        inputs,
        inverse_attn,
        normalized_input,
        query_rows,
        rotated_keys,
        value_rows,
        logsum,
        attn_mix,
        middle,
        inverse_ffn,
        normed_ffn,
        gate_pre,
        up_pre,
        activated,
    )
    return (outputs, stored)


def layer_backward(stored, incoming_gradient, params, tables):
    w_query, key_projection, value_projection, w_out, gain_attn, gain_ffn, w_gate, w_up, w_down = (
        params
    )
    cosine_table, sine_table, allowed = tables
    (
        inputs,
        inverse_attn,
        normalized_input,
        query_rows,
        rotated_keys,
        value_rows,
        logsum,
        attn_mix,
        middle,
        inverse_ffn,
        normed_ffn,
        gate_pre,
        up_pre,
        activated,
    ) = stored
    sequence_length = inputs.shape[0]
    grad_branch = incoming_gradient.astype(jnp.bfloat16)
    grad_down = left_contract(activated, grad_branch)
    grad_act = right_contract(grad_branch, w_down)
    sigmoid = jax.nn.sigmoid(gate_pre)
    grad_up_pre = (grad_act * gate_pre * sigmoid).astype(jnp.bfloat16)
    grad_gate_pre = (grad_act * up_pre * sigmoid * (1.0 + gate_pre * (1.0 - sigmoid))).astype(
        jnp.bfloat16
    )
    grad_gate = left_contract(normed_ffn, grad_gate_pre)
    grad_up = left_contract(normed_ffn, grad_up_pre)
    grad_normed_ffn = right_contract(grad_gate_pre, w_gate) + right_contract(grad_up_pre, w_up)
    grad_middle, grad_gain_ffn = norm_backward(middle, inverse_ffn, gain_ffn, grad_normed_ffn)
    grad_middle = grad_middle + incoming_gradient
    grad_attn_out = grad_middle.astype(jnp.bfloat16)
    grad_out = left_contract(attn_mix, grad_attn_out)
    grad_mix = right_contract(grad_attn_out, w_out).astype(jnp.bfloat16)
    grad_queries, key_gradient_rows, value_gradient_rows = attend_back(
        query_rows, rotated_keys, value_rows, logsum, grad_mix, allowed
    )
    grad_q_raw = (
        apply_rotation(grad_queries, cosine_table, -sine_table)
        .reshape(sequence_length, QUERY_HEADS * HEAD_SIZE)
        .astype(jnp.bfloat16)
    )
    grad_k_raw = (
        apply_rotation(key_gradient_rows, cosine_table, -sine_table)
        .reshape(sequence_length, KEY_VALUE_HEADS * HEAD_SIZE)
        .astype(jnp.bfloat16)
    )
    value_gradient_unsummed = value_gradient_rows.reshape(
        sequence_length, KEY_VALUE_HEADS * HEAD_SIZE
    ).astype(jnp.bfloat16)
    grad_query = left_contract(normalized_input, grad_q_raw)
    grad_key = left_contract(normalized_input, grad_k_raw)
    grad_value = left_contract(normalized_input, value_gradient_unsummed)
    grad_normed = (
        right_contract(grad_q_raw, w_query)
        + right_contract(grad_k_raw, key_projection)
        + right_contract(value_gradient_unsummed, value_projection)
    )
    grad_inputs, grad_gain_attn = norm_backward(inputs, inverse_attn, gain_attn, grad_normed)
    layer_grads = (
        grad_query,
        grad_key,
        grad_value,
        grad_out,
        grad_gain_attn,
        grad_gain_ffn,
        grad_gate,
        grad_up,
        grad_down,
    )
    return (grad_inputs + grad_middle, layer_grads)


def body(
    activations,
    doc_ids,
    w_query,
    key_projection,
    value_projection,
    w_out,
    gain_attn,
    gain_ffn,
    w_gate,
    w_up,
    w_down,
    cotangent,
):
    params = (
        lax.all_gather(w_query, "fsdp", axis=0, tiled=True),
        lax.all_gather(key_projection, "fsdp", axis=0, tiled=True),
        lax.all_gather(value_projection, "fsdp", axis=0, tiled=True),
        lax.all_gather(w_out, "fsdp", axis=0, tiled=True),
        lax.all_gather(gain_attn, "fsdp", axis=0, tiled=True),
        lax.all_gather(gain_ffn, "fsdp", axis=0, tiled=True),
        lax.all_gather(w_gate, "fsdp", axis=0, tiled=True),
        lax.all_gather(w_up, "fsdp", axis=0, tiled=True),
        lax.all_gather(w_down, "fsdp", axis=0, tiled=True),
    )

    def forward_one(unused_carry, seq_item):
        inputs, doc_row = seq_item
        tables = doc_tables(doc_row)
        first_out, first_stored = layer_forward(inputs.astype(jnp.float32), params, tables)
        second_out, second_stored = layer_forward(first_out, params, tables)
        return (unused_carry, (second_out.astype(jnp.bfloat16), first_stored, second_stored))

    unused, (block_out, first_kept, second_kept) = lax.scan(
        forward_one, jnp.zeros((), jnp.float32), (activations, doc_ids)
    )

    def backward_one(totals, seq_item):
        stored, incoming_gradient, doc_row = seq_item
        grad_inputs, layer_grads = layer_backward(
            stored, incoming_gradient, params, doc_tables(doc_row)
        )
        return (
            tuple((running + update for running, update in zip(totals, layer_grads))),
            grad_inputs,
        )

    zero_grads = tuple((jnp.zeros(weight.shape, jnp.float32) for weight in params))
    second_totals, grad_mid = lax.scan(
        backward_one, zero_grads, (second_kept, cotangent.astype(jnp.float32), doc_ids)
    )
    first_totals, grad_first = lax.scan(
        backward_one, second_totals, (first_kept, grad_mid, doc_ids)
    )
    (
        sum_query,
        sum_key,
        sum_value,
        sum_out,
        sum_gain_attn,
        sum_gain_ffn,
        sum_gate,
        sum_up,
        sum_down,
    ) = first_totals
    shard_grads = (
        lax.psum_scatter(
            sum_query.astype(jnp.bfloat16), "fsdp", scatter_dimension=0, tiled=True
        ).astype(jnp.float32),
        lax.psum_scatter(
            sum_key.astype(jnp.bfloat16), "fsdp", scatter_dimension=0, tiled=True
        ).astype(jnp.float32),
        lax.psum_scatter(
            sum_value.astype(jnp.bfloat16), "fsdp", scatter_dimension=0, tiled=True
        ).astype(jnp.float32),
        lax.psum_scatter(
            sum_out.astype(jnp.bfloat16), "fsdp", scatter_dimension=0, tiled=True
        ).astype(jnp.float32),
        lax.psum_scatter(
            sum_gain_attn.astype(jnp.bfloat16), "fsdp", scatter_dimension=0, tiled=True
        ).astype(jnp.float32),
        lax.psum_scatter(
            sum_gain_ffn.astype(jnp.bfloat16), "fsdp", scatter_dimension=0, tiled=True
        ).astype(jnp.float32),
        lax.psum_scatter(
            sum_gate.astype(jnp.bfloat16), "fsdp", scatter_dimension=0, tiled=True
        ).astype(jnp.float32),
        lax.psum_scatter(
            sum_up.astype(jnp.bfloat16), "fsdp", scatter_dimension=0, tiled=True
        ).astype(jnp.float32),
        lax.psum_scatter(
            sum_down.astype(jnp.bfloat16), "fsdp", scatter_dimension=0, tiled=True
        ).astype(jnp.float32),
    )
    (
        part_query,
        part_key,
        part_value,
        part_out,
        part_gain_attn,
        part_gain_ffn,
        part_gate,
        part_up,
        part_down,
    ) = shard_grads
    (
        grad_query,
        grad_key,
        grad_value,
        grad_out,
        grad_gain_attn,
        grad_gain_ffn,
        grad_gate,
        grad_up,
        grad_down,
    ) = (
        lax.psum(part_query.astype(jnp.bfloat16), "dp").astype(jnp.float32),
        lax.psum(part_key.astype(jnp.bfloat16), "dp").astype(jnp.float32),
        lax.psum(part_value.astype(jnp.bfloat16), "dp").astype(jnp.float32),
        lax.psum(part_out.astype(jnp.bfloat16), "dp").astype(jnp.float32),
        lax.psum(part_gain_attn.astype(jnp.bfloat16), "dp").astype(jnp.float32),
        lax.psum(part_gain_ffn.astype(jnp.bfloat16), "dp").astype(jnp.float32),
        lax.psum(part_gate.astype(jnp.bfloat16), "dp").astype(jnp.float32),
        lax.psum(part_up.astype(jnp.bfloat16), "dp").astype(jnp.float32),
        lax.psum(part_down.astype(jnp.bfloat16), "dp").astype(jnp.float32),
    )
    return (
        block_out,
        grad_first.astype(jnp.bfloat16),
        grad_query,
        grad_key,
        grad_value,
        grad_out,
        grad_gain_attn,
        grad_gain_ffn,
        grad_gate,
        grad_up,
        grad_down,
    )


def solution(mesh):
    in_specs = (
        P(("dp", "fsdp"), None, None),
        P(("dp", "fsdp"), None),
        P("fsdp", None),
        P("fsdp", None),
        P("fsdp", None),
        P("fsdp", None),
        P("fsdp"),
        P("fsdp"),
        P("fsdp", None),
        P("fsdp", None),
        P("fsdp", None),
        P(("dp", "fsdp"), None, None),
    )
    out_specs = (
        P(("dp", "fsdp"), None, None),
        P(("dp", "fsdp"), None, None),
        P("fsdp", None),
        P("fsdp", None),
        P("fsdp", None),
        P("fsdp", None),
        P("fsdp"),
        P("fsdp"),
        P("fsdp", None),
        P("fsdp", None),
        P("fsdp", None),
    )
    return jax.shard_map(body, mesh=mesh, in_specs=in_specs, out_specs=out_specs, check_vma=False)
```

profile of v0, /device:TPU:0, one launch (start us, length us, event | category | flops | bytes accessed | tf_op | source)
XLA Modules:
  0.0 1155.3 jit_solution(16352493970026803649)
XLA Ops:
  12.0 14.5 %all-gather = bf16[2,480,320]{1,2,0:T(8,128)(2,1)S(1)} all-gather(bf16[1,480,320]{1,2,0:T(8,128)(2,1)} %bitcast.543), channel_id=1, replica_groups=mesh['dp'=16,'fsdp'=2] {'fsdp'}, dimensions={0}, use_global_device_ids=true | all-gather | bytes 921600 | tf_op jit(solution)/shard_map/all_gather | solution.py:320
  38.8 13.1 %all-gather.1 = bf16[2,480,320]{1,2,0:T(8,128)(2,1)S(1)} all-gather(bf16[1,480,320]{1,2,0:T(8,128)(2,1)} %bitcast.544), channel_id=1, replica_groups=mesh['dp'=16,'fsdp'=2] {'fsdp'}, dimensions={0}, use_global_device_ids=true | all-gather | bytes 921600 | tf_op jit(solution)/shard_map/all_gather | solution.py:319
  70.9 41.3 %while.68 = (s32[]{:T(128)}, bf16[5,768,3,64]{1,3,2,0:T(8,128)(2,1)}, f32[5,3,768]{2,1,0:T(4,128)S(1)}, bf16[5,768,64]{1,2,0:T(8,128)(2,1)}, bf16[5,768,64]{1,2,...) while((s32[]{:T(128)}, ...), condition=%wide.region_5.6_spmd.clone, body=%wide.region_2.0_spmd.clone.sunk | while | flops 475985664 | bytes 24762464 | solution.py:130
  118.6 31.6 %all-gather.12.cloned.1.call-done = bf16[960,2560]{1,0:T(8,128)(2,1)} async-done(((bf16[480,2560]{1,0:T(8,128)(2,1)}), bf16[960,2560]{1,0:T(8,128)(2,1)}) %all-gather.12.cloned.1.call-update) | async-done | bytes 4915216 | tf_op jit(solution)/shard_map/all_gather | solution.py:324
  150.2 8.8 fusion.192
  159.0 57.5 %all-gather.14.cloned.1.call-done = bf16[960,2560]{1,0:T(8,128)(2,1)} async-done(((bf16[480,2560]{1,0:T(8,128)(2,1)}), bf16[960,2560]{1,0:T(8,128)(2,1)}) %all-gather.14.cloned.1.call-update) | async-done | bytes 4915216 | tf_op jit(solution)/shard_map/all_gather | solution.py:325
  216.5 12.1 %multiply_convert_fusion.5 = (bf16[768,2560]{1,0:T(8,128)(2,1)}, f32[768,2560]{1,0:T(8,128)}) fusion(f32[768,2560]{1,0:T(8,128)} %fusion.192, bf16[768,960]{0,1:T(8,128)(2,1)S(1)} %multiply_convert_fusion.8, bf16[960,2560]{1,0:T(8,128)(2,1)} %all-gather.14.cloned.1.call-done), kind=kOutput, calls=%fused_computation.143 | convolution fusion | flops 3786670080 | bytes 26050560 | tf_op jit(solution)/shard_map/while/body/eval_jaxpr/dot_general | solution.py:19
  228.6 54.2 %all-gather.16.cloned.1.call-done = bf16[2560,960]{0,1:T(8,128)(2,1)} async-done(((bf16[1280,960]{0,1:T(8,128)(2,1)}), bf16[2560,960]{0,1:T(8,128)(2,1)}) %all-gather.16.cloned.1.call-update) | async-done | bytes 4915216 | tf_op jit(solution)/shard_map/all_gather | solution.py:326
  282.8 8.4 multiply_reduce_fusion.7
  299.5 41.8 %while.69 = (s32[]{:T(128)}, bf16[5,768,3,64]{1,3,2,0:T(8,128)(2,1)}, f32[5,3,768]{2,1,0:T(4,128)S(1)}, bf16[5,768,64]{1,2,0:T(8,128)(2,1)}, bf16[5,768,64]{1,2,...) while((s32[]{:T(128)}, ...), condition=%wide.region_11.12_spmd.clone, body=%wide.region_8.11_spmd.clone.sunk | while | flops 475985664 | bytes 24762464 | solution.py:130
  346.0 6.6 fusion.194
  352.6 6.5 fusion.195
  359.1 13.8 %multiply_convert_fusion.2 = (bf16[768,2560]{1,0:T(8,128)(2,1)}, bf16[768,2560]{1,0:T(8,128)(2,1)}, bf16[768,2560]{1,0:T(8,128)(2,1)}) fusion(f32[768,2560]{1,0:T(8,128)} %fusion.194, f32[768,2560]{1,0:T(8,128)} %fusion.195, bf16[2560,960]{0,1:T(8,128)(2,1)S(1)} %bitcast.546, bf16[1,768,960]{1,2,0:T(8,128)(2,1)S(1)} %copy-done.47), kind=kOutput, calls=%fused_computation.139 | convolution fusion | flops 3806330880 | bytes 33914880 | tf_op jit(solution)/shard_map/while/body/eval_jaxpr/dot_general | solution.py:29
  373.0 6.3 fusion.196
  379.3 7.5 multiply_reduce_fusion.1
  392.5 90.9 %while.70 = (s32[]{:T(128)}, f32[5,768,3,64]{1,3,2,0:T(8,128)S(1)}, f32[5,768,64]{1,2,0:T(8,128)}, bf16[5,768,64]{1,2,0:T(8,128)(2,1)S(1)}, bf16[5,768,64]{1,2,0...) while((s32[]{:T(128)}, f32[5,768,3,64]{1,3,2,0:T(8,128)S(1)}, ...), condition=%wide.region_16.17_spmd.clone, body=%wide.region_14.16_spmd.clone.sunk | while | flops 1152120576 | bytes 85087376 | solution.py:158
  496.6 13.5 %multiply_convert_fusion = (bf16[768,2560]{1,0:T(8,128)(2,1)S(1)}, bf16[768,2560]{1,0:T(8,128)(2,1)}) fusion(f32[768,2560]{1,0:T(8,128)} %fusion.192, f32[768,2560]{1,0:T(8,128)} %get-tuple-element.762, bf16[2560,960]{0,1:T(8,128)(2,1)S(1)} %bitcast.548, f32[768,960]{0,1:T(8,128)S(1)} %subtract_add_fusion.1), kind=kOutput, calls=%fused_computation.137 | convolution fusion | flops 3801169920 | bytes 31457280 | tf_op jit(solution)/shard_map/while/body/eval_jaxpr/dot_general | solution.py:29
  510.2 7.5 fusion.198
  517.8 7.4 multiply_reduce_fusion
  532.5 95.1 %while.71 = (s32[]{:T(128)}, f32[5,768,3,64]{1,3,2,0:T(8,128)}, f32[5,768,64]{1,2,0:T(8,128)}, bf16[5,768,64]{1,2,0:T(8,128)(2,1)S(1)}, bf16[5,768,64]{1,2,0:T(8...) while((s32[]{:T(128)}, f32[5,768,3,64]{1,3,2,0:T(8,128)}, ...), condition=%wide.region_21.22_spmd.clone, body=%wide.region_19.21_spmd.clone.sunk | while | flops 1152120576 | bytes 85087376 | solution.py:158
  655.0 6.7 fusion.203
  661.7 5.7 add_convert_fusion.2
  667.7 6.7 fusion.204
  681.7 6.2 fusion.144
  697.4 7.1 reduce-scatter.12.cloned.1.call-done
  704.5 33.4 %reduce-scatter.14.cloned.1.call-done = bf16[480,960]{1,0:T(8,128)(2,1)} async-done(((bf16[960,960]{1,0:T(8,128)(2,1)}), bf16[480,960]{1,0:T(8,128)(2,1)}) %reduce-scatter.14.cloned.1.call-update) | async-done | bytes 921616 | tf_op jit(solution)/shard_map/reduce_scatter | solution.py:378
  737.9 64.9 %reduce-scatter.16.cloned.1.call-done = bf16[480,2560]{1,0:T(8,128)(2,1)} async-done(((bf16[960,2560]{1,0:T(8,128)(2,1)}), bf16[480,2560]{1,0:T(8,128)(2,1)}) %reduce-scatter.16.cloned.1.call-update) | async-done | bytes 2457616 | tf_op jit(solution)/shard_map/reduce_scatter | solution.py:387
  802.8 65.1 %reduce-scatter.18.cloned.1.call-done = bf16[480,2560]{1,0:T(8,128)(2,1)} async-done(((bf16[960,2560]{1,0:T(8,128)(2,1)}), bf16[480,2560]{1,0:T(8,128)(2,1)}) %reduce-scatter.18.cloned.1.call-update) | async-done | bytes 2457616 | tf_op jit(solution)/shard_map/reduce_scatter | solution.py:390
  867.9 64.9 %reduce-scatter.20.cloned.1.call-done = bf16[1280,960]{0,1:T(8,128)(2,1)} async-done(((bf16[2560,960]{0,1:T(8,128)(2,1)}), bf16[1280,960]{0,1:T(8,128)(2,1)}) %reduce-scatter.20.cloned.1.call-update) | async-done | bytes 2457616 | tf_op jit(solution)/shard_map/reduce_scatter | solution.py:393
  946.1 34.6 %all-reduce.4 = (bf16[480]{0:T(512)(128)(2,1)S(1)}, bf16[480]{0:T(512)(128)(2,1)S(1)}) all-reduce(bf16[480]{0:T(512)(128)(2,1)S(1)} %dynamic-slice.30, bf16[480]{0:T(512)(128)(2,1)S(1)} %dynamic-slice.32), channel_id=1, replica_groups=mesh['dp'=16,'fsdp'=2] {'dp'}, use_global_device_ids=true, to_apply=%region_34.35 | all-reduce | flops 960 | bytes 3840 | tf_op jit(solution)/shard_map/psum | solution.py:423
  987.1 7.6 fusion.159
  994.7 139.2 %all-reduce.10.cloned.1.call-done = (bf16[480,960]{1,0:T(8,128)(2,1)}, bf16[480,320]{0,1:T(8,128)(2,1)}, bf16[480,320]{0,1:T(8,128)(2,1)}, bf16[480,960]{1,0:T(8...) async-done(((bf16[480,960]{1,0:T(8,128)(2,1)}, bf16[480,320]{0,1:T(8,128)(2,1)}, bf16[480,320]{0,1:T(8,128)(2,1)}, ...) | async-done | bytes 9830416 | tf_op jit(solution)/shard_map/psum | solution.py:419
  (484 shorter events, 425.3 us)
Async XLA Ops:
  7.2 55.9 %all-gather.8.cloned.1.call-start = ((), (), s32[]{:S(2)}) async-start(), calls=%async_computation.7 | async-start | bytes 2949120 | tf_op jit(solution)/shard_map/all_gather | solution.py:318
  7.9 104.3 %all-gather.10.cloned.1.call-start = ((), (), s32[]{:S(2)}) async-start(), calls=%async_computation.8 | async-start | bytes 2949120 | tf_op jit(solution)/shard_map/all_gather | solution.py:321
  8.7 141.5 %all-gather.12.cloned.1.call-start = ((), (), s32[]{:S(2)}) async-start(), calls=%async_computation.9 | async-start | bytes 7372800 | tf_op jit(solution)/shard_map/all_gather | solution.py:324
  9.4 207.1 %all-gather.14.cloned.1.call-start = ((), (), s32[]{:S(2)}) async-start(), calls=%async_computation.10 | async-start | bytes 7372800 | tf_op jit(solution)/shard_map/all_gather | solution.py:325
  10.0 272.9 %all-gather.16.cloned.1.call-start = ((), (), s32[]{:S(2)}) async-start(), calls=%async_computation.11 | async-start | bytes 7372800 | tf_op jit(solution)/shard_map/all_gather | solution.py:326
  10.6 683.1 %reduce-scatter.22.cloned.1.call-start = ((), (), s32[]{:S(2)}) async-start(), calls=%async_computation.17 | async-start | bytes 1105920
  10.8 48.9 %copy-start.33 = (bf16[5,768,64]{1,2,0:T(8,128)(2,1)}, bf16[5,768,64]{1,2,0:T(8,128)(2,1)S(1)}, u32[]{:S(2)}) copy-start(bf16[5,768,64]{1,2,0:T(8,128)(2,1)S(1)} %fusion.190) | copy-start | bytes 1474564
  10.8 19.8 %copy-start.77 = (u32[32]{0:T(128)S(1)}, u32[32]{0:T(128)}, u32[]{:S(2)}) copy-start(u32[32]{0:T(128)} %constant.266) | copy-start | bytes 388
  10.9 21.2 %copy-start.78 = (bf16[480]{0:T(512)(128)(2,1)S(1)}, bf16[480]{0:T(512)(128)(2,1)}, u32[]{:S(2)}) copy-start(bf16[480]{0:T(512)(128)(2,1)} %param.26) | copy-start | bytes 2884
  10.9 21.4 %copy-start.79 = (bf16[480]{0:T(512)(128)(2,1)S(1)}, bf16[480]{0:T(512)(128)(2,1)}, u32[]{:S(2)}) copy-start(bf16[480]{0:T(512)(128)(2,1)} %param.27) | copy-start | bytes 2884
  10.9 27.0 %copy-start.6 = (bf16[1,768,960]{1,2,0:T(8,128)(2,1)S(1)}, bf16[1,768,960]{1,2,0:T(8,128)(2,1)}, u32[]{:S(2)}) copy-start(bf16[1,768,960]{1,2,0:T(8,128)(2,1)} %param.20) | copy-start | bytes 4423684
  30.6 26.9 %copy-start.22 = (bf16[960,320]{0,1:T(8,128)(2,1)}, bf16[960,320]{0,1:T(8,128)(2,1)S(1)}, u32[]{:S(2)}) copy-start(bf16[960,320]{0,1:T(8,128)(2,1)S(1)} %reshape.469) | copy-start | bytes 1843204
  37.9 254.0 %copy-start.62 = (f32[960]{0:T(1024)}, f32[960]{0:T(1024)S(1)}, u32[]{:S(2)}) copy-start(f32[960]{0:T(1024)S(1)} %convert_element_type.308) | copy-start | bytes 11524
  38.8 28.1 %copy-start.66 = (f32[768]{0:T(1024)}, f32[768]{0:T(1024)S(1)}, u32[]{:S(2)}) copy-start(f32[768]{0:T(1024)S(1)} %get-tuple-element.750) | copy-start | bytes 9220
  60.8 237.0 %copy-start.20 = (f32[768,32]{0,1:T(8,128)}, f32[768,32]{0,1:T(8,128)S(1)}, u32[]{:S(2)}) copy-start(f32[768,32]{0,1:T(8,128)S(1)} %get-tuple-element.748) | copy-start | bytes 294916
  117.4 41.7 %copy-start.68 = (f32[768]{0:T(1024)}, f32[768]{0:T(1024)S(1)}, u32[]{:S(2)}) copy-start(f32[768]{0:T(1024)S(1)} %get-tuple-element.752) | copy-start | bytes 9220
  118.6 97.9 %copy-start.49 = (bf16[768,960]{0,1:T(8,128)(2,1)}, bf16[768,960]{0,1:T(8,128)(2,1)S(1)}, u32[]{:S(2)}) copy-start(bf16[768,960]{0,1:T(8,128)(2,1)S(1)} %multiply_convert_fusion.8) | copy-start | bytes 4423684
  291.3 50.1 %copy-start.4 = (f32[768,960]{0,1:T(8,128)}, f32[768,960]{0,1:T(8,128)S(1)}, u32[]{:S(2)}) copy-start(f32[768,960]{0,1:T(8,128)S(1)} %get-tuple-element.764) | copy-start | bytes 8847364
  345.6 41.2 %copy-start.8 = (f32[768,960]{0,1:T(8,128)}, f32[768,960]{0,1:T(8,128)S(1)}, u32[]{:S(2)}) copy-start(f32[768,960]{0,1:T(8,128)S(1)} %get-tuple-element.766) | copy-start | bytes 8847364
  352.6 20.4 %slice-start.6 = ((s8[4915200]{0:T(1024)(128)(4,1)}), s8[4194304]{0:T(1024)(128)(4,1)S(1)}, s32[]{:S(2)}) async-start(s8[4915200]{0:T(1024)(128)(4,1)} %bitcast.551), calls=%async_computation.26 | async-start | bytes 8388608
  392.5 92.6 %copy-start.21 = (f32[768,32]{0,1:T(8,128)S(1)}, f32[768,32]{0,1:T(8,128)}, u32[]{:S(2)}) copy-start(f32[768,32]{0,1:T(8,128)} %copy-done.20) | copy-start | bytes 294916
  496.6 28.6 %copy-start.16 = (f32[768,960]{0,1:T(8,128)}, f32[768,960]{0,1:T(8,128)S(1)}, u32[]{:S(2)}) copy-start(f32[768,960]{0,1:T(8,128)S(1)} %subtract_add_fusion.1) | copy-start | bytes 8847364
  532.5 97.3 %copy-start.7 = (bf16[1,768,960]{1,2,0:T(8,128)(2,1)S(1)}, bf16[1,768,960]{1,2,0:T(8,128)(2,1)}, u32[]{:S(2)}) copy-start(bf16[1,768,960]{1,2,0:T(8,128)(2,1)} %param.20) | copy-start | bytes 4423684
  532.5 97.3 %copy-start.67 = (f32[768]{0:T(1024)S(1)}, f32[768]{0:T(1024)}, u32[]{:S(2)}) copy-start(f32[768]{0:T(1024)} %copy-done.66) | copy-start | bytes 9220
  635.0 60.5 %reduce-scatter.24.cloned.1.call-start = ((), (), s32[]{:S(2)}) async-start(), calls=%async_computation.18 | async-start | bytes 1105920
  640.8 63.8 %reduce-scatter.12.cloned.1.call-start = ((), (), s32[]{:S(2)}) async-start(), calls=%async_computation.12 | async-start | bytes 2949120 | tf_op jit(solution)/shard_map/reduce_scatter | solution.py:369
  648.1 89.8 %reduce-scatter.14.cloned.1.call-start = ((), (), s32[]{:S(2)}) async-start(), calls=%async_computation.13 | async-start | bytes 2949120 | tf_op jit(solution)/shard_map/reduce_scatter | solution.py:378
  655.0 147.8 %reduce-scatter.16.cloned.1.call-start = ((), (), s32[]{:S(2)}) async-start(), calls=%async_computation.14 | async-start | bytes 7372800 | tf_op jit(solution)/shard_map/reduce_scatter | solution.py:387
  667.5 200.4 %reduce-scatter.18.cloned.1.call-start = ((), (), s32[]{:S(2)}) async-start(), calls=%async_computation.15 | async-start | bytes 7372800 | tf_op jit(solution)/shard_map/reduce_scatter | solution.py:390
  680.2 252.6 %reduce-scatter.20.cloned.1.call-start = ((), (), s32[]{:S(2)}) async-start(), calls=%async_computation.16 | async-start | bytes 7372800 | tf_op jit(solution)/shard_map/reduce_scatter | solution.py:393
  693.6 440.3 %all-reduce.10.cloned.1.call-start = ((), (), s32[]{:S(2)}) async-start(), calls=%async_computation.19 | async-start | bytes 19988480 | tf_op jit(solution)/shard_map/psum | solution.py:419
  937.7 44.1 %copy-start.71 = (f32[768]{0:T(1024)S(1)}, f32[768]{0:T(1024)}, u32[]{:S(2)}) copy-start(f32[768]{0:T(1024)} %get-tuple-element.749) | copy-start | bytes 9220
  (89 other events, 391.5 us)
Sparse Core Ops, SparseCore 0:
  9.6 39.6 all-gather.7
  50.8 32.9 all-gather.9
  85.3 64.8 all-gather.11
  151.6 64.8 all-gather.13
  217.9 64.8 all-gather.15
  635.2 16.8 reduce-scatter.21
  654.3 16.8 reduce-scatter.23
  674.1 30.3 reduce-scatter.11
  707.4 30.3 reduce-scatter.13
  740.6 62.1 reduce-scatter.15
  805.7 62.1 reduce-scatter.17
  870.6 62.1 reduce-scatter.19
  937.5 196.3 all-reduce.9
where the time goes:
time: 1160 us
  waiting for transfers between devices  521 us (45%)
  matrix products  395 us (34%)
  other arithmetic  101 us (9%)
  blocking collectives  72.4 us (6%)
  local copies, waits for them, and re-layouts  46.6 us (4%)
  between operations  16.9 us (1%)
    psum x1, waiting for transfers between devices, body(): lax.psum(part_query.astype(jnp.bfloat16), 'dp').astype(jnp.float32)  139 us
    dot_general x14, matrix products, right_contract(): lax.dot_general(left_mat, right_mat, (((1,), (1,)), ((), ())), preferred_...  72.6 us
    dot_general x14, matrix products, matrix_product(): return jnp.dot(left_mat, right_mat, preferred_element_type=jnp.float32)  69.3 us
    dot_general x20, matrix products, head_scores(): jnp.einsum('qgd,sd->gqs', query_rows, rotated_keys, preferred_element_typ...  65.5 us
    reduce_scatter x1, waiting for transfers between devices, body(): lax.psum_scatter(sum_up.astype(jnp.bfloat16), 'fsdp', scatter_dimension=0...  65.1 us
    reduce_scatter x1, waiting for transfers between devices, body(): lax.psum_scatter(sum_down.astype(jnp.bfloat16), 'fsdp', scatter_dimension...  64.9 us
    reduce_scatter x1, waiting for transfers between devices, body(): lax.psum_scatter(sum_gate.astype(jnp.bfloat16), 'fsdp', scatter_dimension...  64.9 us
    all_gather x1, waiting for transfers between devices, body(): lax.all_gather(w_up, 'fsdp', axis=0, tiled=True)  57.5 us
  transfers between devices with their start and end apart: 13, of which 9 were waited for; matrix products, arithmetic and copies ran while one was open for 15% of the time, Pallas kernels for 0%

commit v1 on v0

v1 whole, which is shorter than its diff:
```python
import jax
import jax.numpy as jnp
from jax import lax
from jax.experimental import pallas as pl
from jax.experimental.pallas import tpu as pltpu
from jax.sharding import PartitionSpec as P

QUERY_HEADS = 15
KEY_VALUE_HEADS = 5
GROUP = QUERY_HEADS // KEY_VALUE_HEADS
HEAD_SIZE = 64
HALF = HEAD_SIZE // 2
LONGEST_DOC = 384
EPSILON = 1e-05
ROPE_BASE = 10000.0
NEGATIVE = -1e30
SCALE = HEAD_SIZE ** (-0.5)
QUERY_BLOCK = 128
BF16 = jnp.bfloat16
F32 = jnp.float32


def dot(left, right, contract):
    return lax.dot_general(left, right, ((contract[:1], contract[1:]), ((), ())), preferred_element_type=F32)


def key_window(block):
    return (max(0, block * QUERY_BLOCK - LONGEST_DOC), (block + 1) * QUERY_BLOCK)


def fill_mask(start_ref, mask_ref):
    for block in range(mask_ref.shape[0] // QUERY_BLOCK):
        low, high = key_window(block)
        cols = slice(block * QUERY_BLOCK, high)
        shape = (high - low, QUERY_BLOCK)
        key = low + lax.broadcasted_iota(jnp.int32, shape, 0)
        query = block * QUERY_BLOCK + lax.broadcasted_iota(jnp.int32, shape, 1)
        allowed = (key >= start_ref[:, cols]) & (key <= query)
        mask_ref[low:high, cols] = jnp.where(allowed, 0.0, NEGATIVE)


def side_by_side(ref, cols):
    return jnp.concatenate([ref[j * HEAD_SIZE : (j + 1) * HEAD_SIZE, cols] for j in range(GROUP)], axis=1)


def attention_kernel(start_ref, query_ref, key_ref, value_ref, mix_ref, logsum_ref, mask_ref, key_rows_ref):
    @pl.when(pl.program_id(0) == 0)
    def _():
        fill_mask(start_ref, mask_ref)

    key_rows_ref[...] = key_ref[...].T
    for block in range(query_ref.shape[1] // QUERY_BLOCK):
        low, high = key_window(block)
        cols = slice(block * QUERY_BLOCK, high)
        queries = side_by_side(query_ref, cols)
        mask = jnp.concatenate([mask_ref[low:high, cols]] * GROUP, axis=1)
        scores = dot(key_rows_ref[low:high, :], queries, (1, 0)) * SCALE + mask
        top = jnp.max(scores, axis=0, keepdims=True)
        weights = jnp.exp(scores - top)
        total = jnp.sum(weights, axis=0, keepdims=True)
        mix = dot(value_ref[:, low:high], weights.astype(BF16), (1, 0))
        mix = (mix / total).astype(BF16)
        logsum = top + jnp.log(total)
        for j in range(GROUP):
            part = slice(j * QUERY_BLOCK, (j + 1) * QUERY_BLOCK)
            mix_ref[j * HEAD_SIZE : (j + 1) * HEAD_SIZE, cols] = mix[:, part]
            logsum_ref[0, j : j + 1, cols] = logsum[:, part]


def attention(start, qkv):
    length = qkv.shape[1]
    rows = GROUP * HEAD_SIZE
    return pl.pallas_call(
        attention_kernel,
        grid=(KEY_VALUE_HEADS,),
        in_specs=[
            pl.BlockSpec((1, length), lambda g: (0, 0)),
            pl.BlockSpec((rows, length), lambda g: (g, 0)),
            pl.BlockSpec((HEAD_SIZE, length), lambda g: (QUERY_HEADS + g, 0)),
            pl.BlockSpec((HEAD_SIZE, length), lambda g: (QUERY_HEADS + KEY_VALUE_HEADS + g, 0)),
        ],
        out_specs=[
            pl.BlockSpec((rows, length), lambda g: (g, 0)),
            pl.BlockSpec((1, 8, length), lambda g: (g, 0, 0)),
        ],
        out_shape=[
            jax.ShapeDtypeStruct((QUERY_HEADS * HEAD_SIZE, length), BF16),
            jax.ShapeDtypeStruct((KEY_VALUE_HEADS, 8, length), F32),
        ],
        scratch_shapes=[pltpu.VMEM((length, length), F32), pltpu.VMEM((length, HEAD_SIZE), BF16)],
        compiler_params=pltpu.CompilerParams(vmem_limit_bytes=32 << 20),
        cost_estimate=pl.CostEstimate(flops=6_000_000_000, bytes_accessed=4_000_000, transcendentals=4_500_000),
        name="attention",
    )(start, qkv, qkv, qkv)


def unrotate(rows, cosine, sine):
    first = rows[:HALF]
    second = rows[HALF:]
    return (first * cosine + second * sine, second * cosine - first * sine)


def attention_back_kernel(
    start_ref, cosine_ref, sine_ref, query_ref, key_ref, value_ref, mix_ref, logsum_ref, mix_grad_ref,
    out_ref, mask_ref, key_rows_ref, value_rows_ref, key_grad_ref, value_grad_ref,
):
    group = pl.program_id(0)

    @pl.when(group == 0)
    def _():
        fill_mask(start_ref, mask_ref)

    key_rows_ref[...] = key_ref[...].T
    value_rows_ref[...] = value_ref[...].T
    key_grad_ref[...] = jnp.zeros_like(key_grad_ref)
    value_grad_ref[...] = jnp.zeros_like(value_grad_ref)
    for block in range(query_ref.shape[1] // QUERY_BLOCK):
        low, high = key_window(block)
        cols = slice(block * QUERY_BLOCK, high)
        queries = side_by_side(query_ref, cols)
        mix_grads = side_by_side(mix_grad_ref, cols)
        mixes = side_by_side(mix_ref, cols)
        inner = jnp.sum(mix_grads.astype(F32) * mixes.astype(F32), axis=0, keepdims=True)
        logsum = jnp.concatenate([logsum_ref[0, j : j + 1, cols] for j in range(GROUP)], axis=1)
        mask = jnp.concatenate([mask_ref[low:high, cols]] * GROUP, axis=1)
        scores = dot(key_rows_ref[low:high, :], queries, (1, 0)) * SCALE + mask
        weights = jnp.exp(scores - logsum)
        weight_grads = dot(value_rows_ref[low:high, :], mix_grads, (1, 0))
        score_grads = (weights * (weight_grads - inner)).astype(BF16)
        value_grad_ref[:, low:high] += dot(mix_grads, weights.astype(BF16), (1, 1))
        key_grad_ref[:, low:high] += dot(queries, score_grads, (1, 1))
        query_grads = dot(key_ref[:, low:high], score_grads, (1, 0)) * SCALE
        cosine = cosine_ref[:, cols]
        sine = sine_ref[:, cols]
        for j in range(GROUP):
            first, second = unrotate(query_grads[:, j * QUERY_BLOCK : (j + 1) * QUERY_BLOCK], cosine, sine)
            base = group * (GROUP * HEAD_SIZE) + j * HEAD_SIZE
            out_ref[pl.ds(pl.multiple_of(base, HALF), HALF), cols] = first.astype(BF16)
            out_ref[pl.ds(pl.multiple_of(base + HALF, HALF), HALF), cols] = second.astype(BF16)
    first, second = unrotate(key_grad_ref[...] * SCALE, cosine_ref[...], sine_ref[...])
    base = (QUERY_HEADS + group) * HEAD_SIZE
    out_ref[pl.ds(pl.multiple_of(base, HALF), HALF), :] = first.astype(BF16)
    out_ref[pl.ds(pl.multiple_of(base + HALF, HALF), HALF), :] = second.astype(BF16)
    base = (QUERY_HEADS + KEY_VALUE_HEADS + group) * HEAD_SIZE
    out_ref[pl.ds(pl.multiple_of(base, HEAD_SIZE), HEAD_SIZE), :] = value_grad_ref[...].astype(BF16)


def attention_back(start, cosine, sine, qkv, mix, logsum, mix_grad):
    length = qkv.shape[1]
    rows = GROUP * HEAD_SIZE
    return pl.pallas_call(
        attention_back_kernel,
        grid=(KEY_VALUE_HEADS,),
        in_specs=[
            pl.BlockSpec((1, length), lambda g: (0, 0)),
            pl.BlockSpec((HALF, length), lambda g: (0, 0)),
            pl.BlockSpec((HALF, length), lambda g: (0, 0)),
            pl.BlockSpec((rows, length), lambda g: (g, 0)),
            pl.BlockSpec((HEAD_SIZE, length), lambda g: (QUERY_HEADS + g, 0)),
            pl.BlockSpec((HEAD_SIZE, length), lambda g: (QUERY_HEADS + KEY_VALUE_HEADS + g, 0)),
            pl.BlockSpec((rows, length), lambda g: (g, 0)),
            pl.BlockSpec((1, 8, length), lambda g: (g, 0, 0)),
            pl.BlockSpec((rows, length), lambda g: (g, 0)),
        ],
        out_specs=pl.BlockSpec(qkv.shape, lambda g: (0, 0)),
        out_shape=jax.ShapeDtypeStruct(qkv.shape, BF16),
        scratch_shapes=[
            pltpu.VMEM((length, length), F32),
            pltpu.VMEM((length, HEAD_SIZE), BF16),
            pltpu.VMEM((length, HEAD_SIZE), BF16),
            pltpu.VMEM((HEAD_SIZE, length), F32),
            pltpu.VMEM((HEAD_SIZE, length), F32),
        ],
        compiler_params=pltpu.CompilerParams(vmem_limit_bytes=32 << 20),
        cost_estimate=pl.CostEstimate(flops=9_000_000_000, bytes_accessed=9_000_000, transcendentals=4_500_000),
        name="attention_back",
    )(start, cosine, sine, qkv, qkv, qkv, mix, logsum, mix_grad)


def doc_tables(doc_row):
    token_index = jnp.arange(doc_row.shape[0])
    start = jnp.sum((doc_row[:, None] < doc_row[None, :]).astype(jnp.int32), axis=0)
    places = (token_index - start).astype(F32)
    frequency = ROPE_BASE ** (-2.0 * jnp.arange(HALF, dtype=F32) / HEAD_SIZE)
    angles = frequency[:, None] * places[None, :]
    return (start[None, :], jnp.cos(angles), jnp.sin(angles))


def norm_forward(inputs, gain):
    inverse = lax.rsqrt(jnp.mean(inputs * inputs, axis=-1, keepdims=True) + EPSILON)
    return ((inputs * inverse * gain).astype(BF16), inverse)


def norm_backward(inputs, inverse, gain, grad):
    scaled = gain * grad
    inner = jnp.mean(scaled * inputs, axis=-1, keepdims=True)
    return (inverse * scaled - inputs * inverse**3 * inner, jnp.sum(grad * inputs * inverse, axis=0))


def layer_forward(inputs, weights, gains, tables):
    w_qkv, w_out, w_gate, w_up, w_down = weights
    start, cosine, sine = tables
    length = inputs.shape[0]
    normed, inverse = norm_forward(inputs, gains[0])
    raw = dot(w_qkv, normed, (0, 1))
    heads = QUERY_HEADS + KEY_VALUE_HEADS
    pairs = raw[: heads * HEAD_SIZE].reshape(heads, 2, HALF, length)
    first, second = pairs[:, 0], pairs[:, 1]
    rotated = jnp.stack([first * cosine - second * sine, second * cosine + first * sine], axis=1)
    qkv = jnp.concatenate(
        [rotated.reshape(heads * HEAD_SIZE, length).astype(BF16), raw[heads * HEAD_SIZE :].astype(BF16)], axis=0
    )
    mix, logsum = attention(start, qkv)
    middle = inputs + dot(mix, w_out, (0, 0))
    normed_ffn, inverse_ffn = norm_forward(middle, gains[1])
    gate = dot(normed_ffn, w_gate, (1, 0))
    up = dot(normed_ffn, w_up, (1, 0))
    hidden = (jax.nn.silu(gate) * up).astype(BF16)
    outputs = middle + dot(hidden, w_down, (1, 0))
    kept = (inputs, inverse, normed, qkv, logsum, mix, middle, inverse_ffn, normed_ffn, gate, up, hidden)
    return (outputs, kept)


def layer_backward(kept, grad, weights, gains, tables):
    w_qkv, w_out, w_gate, w_up, w_down = weights
    start, cosine, sine = tables
    inputs, inverse, normed, qkv, logsum, mix, middle, inverse_ffn, normed_ffn, gate, up, hidden = kept
    branch = grad.astype(BF16)
    hidden_grad = dot(branch, w_down, (1, 1))
    sigmoid = jax.nn.sigmoid(gate)
    up_grad = (hidden_grad * gate * sigmoid).astype(BF16)
    gate_grad = (hidden_grad * up * sigmoid * (1.0 + gate * (1.0 - sigmoid))).astype(BF16)
    normed_ffn_grad = dot(gate_grad, w_gate, (1, 1)) + dot(up_grad, w_up, (1, 1))
    middle_grad, gain_ffn_grad = norm_backward(middle, inverse_ffn, gains[1], normed_ffn_grad)
    middle_grad = middle_grad + grad
    attn_grad = middle_grad.astype(BF16)
    mix_grad = dot(w_out, attn_grad, (1, 1)).astype(BF16)
    qkv_grad = attention_back(start, cosine, sine, qkv, mix, logsum, mix_grad)
    normed_grad = dot(qkv_grad, w_qkv, (0, 1))
    inputs_grad, gain_attn_grad = norm_backward(inputs, inverse, gains[0], normed_grad)
    products = (
        (hidden, branch),
        (normed_ffn, gate_grad),
        (normed_ffn, up_grad),
        (mix, attn_grad),
        (normed, qkv_grad),
    )
    return (inputs_grad + middle_grad, (gain_attn_grad, gain_ffn_grad), products)


def swap_fsdp(value):
    return lax.ppermute(value, "fsdp", [(0, 1), (1, 0)])


def swap_dp(value, bit, size):
    return lax.ppermute(value, "dp", [(i, i ^ bit) for i in range(size)])


def gather_rows(shard, dp_size):
    count = shard.shape[0]
    quarter = count // 4
    fsdp = lax.axis_index("fsdp")
    place = lax.axis_index("dp") % 4
    mine = swap_fsdp(lax.dynamic_slice_in_dim(shard, place * quarter, quarter, 0))
    across = swap_dp(mine, 2, dp_size)
    beside = swap_dp(mine, 1, dp_size)
    corner = swap_dp(across, 1, dp_size)
    whole = jnp.zeros((2 * count,) + shard.shape[1:], shard.dtype)
    whole = lax.dynamic_update_slice_in_dim(whole, shard, fsdp * count, 0)
    other = (1 - fsdp) * count
    for flip, piece in ((0, mine), (2, across), (1, beside), (3, corner)):
        whole = lax.dynamic_update_slice_in_dim(whole, piece, other + (place ^ flip) * quarter, 0)
    return whole


def pick(parts, index):
    return lax.dynamic_index_in_dim(parts, index, 0, keepdims=False)


def add(left, right):
    return (left.astype(F32) + right.astype(F32)).astype(BF16)


def reduce_rows(grad, dp_size):
    count, width = grad.shape[0] // 2, grad.shape[1]
    fsdp = lax.axis_index("fsdp")
    place = lax.axis_index("dp")
    core, side = place % 2, (place // 2) % 2
    parts = grad.reshape(2, 2, count // 2, width)
    take = lambda which: lax.dynamic_index_in_dim(parts, which, 1, keepdims=False)
    parts = add(take(core), swap_dp(take(1 - core), 1, dp_size))
    parts = add(pick(parts, fsdp), swap_fsdp(pick(parts, 1 - fsdp)))
    parts = parts.reshape(2, count // 4, width)
    part = add(pick(parts, side), swap_dp(pick(parts, 1 - side), 2, dp_size))
    bit = 4
    while bit < dp_size:
        part = add(part, swap_dp(part, bit, dp_size))
        bit *= 2
    across = swap_dp(part, 2, dp_size)
    half = jnp.stack([jnp.where(side == 0, part, across), jnp.where(side == 0, across, part)]).reshape(
        count // 2, width
    )
    beside = swap_dp(half, 1, dp_size)
    whole = jnp.zeros((2, count // 2, width), F32)
    whole = lax.dynamic_update_slice_in_dim(whole, half.astype(F32)[None], core, 0)
    whole = lax.dynamic_update_slice_in_dim(whole, beside.astype(F32)[None], 1 - core, 0)
    return whole.reshape(count, width)


def reduce_vector(values, dp_size):
    total = values
    bit = 1
    while bit < dp_size:
        total = add(total, swap_dp(total, bit, dp_size))
        bit *= 2
    total = add(total, swap_fsdp(total))
    count = values.shape[1] // 2
    return lax.dynamic_slice_in_dim(total, lax.axis_index("fsdp") * count, count, 1)


def pair_transfers(dp_size):
    def gather_gains(gains):
        other = swap_fsdp(gains)
        first = lax.axis_index("fsdp") == 0
        return jnp.concatenate([jnp.where(first, gains, other), jnp.where(first, other, gains)], axis=1)

    return (
        lambda shard: gather_rows(shard, dp_size),
        gather_gains,
        lambda grad: reduce_rows(grad, dp_size),
        lambda grads: reduce_vector(grads, dp_size),
    )


def native_transfers():
    def reduce_over(axis):
        def reduce(grad):
            part = lax.psum_scatter(grad, "fsdp", scatter_dimension=axis, tiled=True)
            return lax.psum(part, "dp").astype(F32)

        return reduce

    return (
        lambda shard: lax.all_gather(shard, "fsdp", axis=0, tiled=True),
        lambda gains: lax.all_gather(gains, "fsdp", axis=1, tiled=True),
        reduce_over(0),
        reduce_over(1),
    )


def make_body(fsdp_size, dp_size):
    if fsdp_size == 2 and dp_size >= 4 and dp_size & (dp_size - 1) == 0:
        gather, gather_gains, reduce, reduce_gains = pair_transfers(dp_size)
    else:
        gather, gather_gains, reduce, reduce_gains = native_transfers()

    def body(
        activations, doc_ids, w_query, key_projection, value_projection, w_out,
        gain_attn, gain_ffn, w_gate, w_up, w_down, cotangent,
    ):
        gains = gather_gains(jnp.stack([gain_attn, gain_ffn])).astype(F32)
        weights = (
            gather(jnp.concatenate([w_query, key_projection, value_projection], axis=1)),
            gather(w_out),
            gather(w_gate),
            gather(w_up),
            gather(w_down),
        )
        tables = doc_tables(doc_ids[0])
        middle, first_kept = layer_forward(activations[0].astype(F32), weights, gains, tables)
        outputs, second_kept = layer_forward(middle, weights, gains, tables)
        grad, second_gains, second_products = layer_backward(
            second_kept, cotangent[0].astype(F32), weights, gains, tables
        )
        grad, first_gains, first_products = layer_backward(first_kept, grad, weights, gains, tables)
        axes = ((0, 0), (0, 0), (0, 0), (1, 0), (0, 1))
        reduced = []
        for contract, (left, right), (more_left, more_right) in zip(axes, second_products, first_products):
            total = dot(left, right, contract) + dot(more_left, more_right, contract)
            reduced.append(reduce(total.astype(BF16)))
        grad_down, grad_gate, grad_up, grad_out, grad_qkv = reduced
        gain_grads = jnp.stack([a + b for a, b in zip(second_gains, first_gains)]).astype(BF16)
        gain_grads = reduce_gains(gain_grads).astype(F32)
        width = w_query.shape[1]
        key_end = width + key_projection.shape[1]
        return (
            outputs.astype(BF16)[None],
            grad.astype(BF16)[None],
            grad_qkv[:, :width],
            grad_qkv[:, width:key_end],
            grad_qkv[:, key_end:],
            grad_out,
            gain_grads[0],
            gain_grads[1],
            grad_gate,
            grad_up,
            grad_down,
        )

    return body


def solution(mesh):
    sequences = P(("dp", "fsdp"), None, None)
    rows = P("fsdp", None)
    vector = P("fsdp")
    in_specs = (
        sequences, P(("dp", "fsdp"), None), rows, rows, rows, rows, vector, vector, rows, rows, rows, sequences,
    )
    out_specs = (sequences, sequences, rows, rows, rows, rows, vector, vector, rows, rows, rows)
    body = make_body(mesh.shape["fsdp"], mesh.shape["dp"])
    return jax.shard_map(body, mesh=mesh, in_specs=in_specs, out_specs=out_specs, check_vma=False)
```

time: 1160 us -> 788 us (0.68)
  waiting for transfers between devices: 521 us -> 216 us
  matrix products: 395 us -> 188 us
  local copies, waits for them, and re-layouts: 46.6 us -> 200 us
  blocking collectives: 72.4 us -> 0 us
  starting transfers between devices: 0.73 us -> 67.3 us
  other arithmetic: 101 us -> 46.3 us
  Pallas kernels: 0 us -> 52.2 us
  between operations: 16.9 us -> 2.77 us
    reduce_scatter x5 -> x0, waiting for transfers between devices: 235 us -> none  [the longest x1 65.1 us: body(): lax.psum_scatter(sum_up.astype(jnp.bfloat16), 'fsdp', scatter_dimension=0...]
    ppermute x0 -> x61, waiting for transfers between devices: none -> 216 us  [the longest x49 147 us: swap_dp(): return lax.ppermute(value, 'dp', [(i, i ^ bit) for i in range(size)])]
    dot_general x112 -> x30, matrix products: 395 us -> 188 us  [dot(): lax.dot_general(left, right, ((contract[:1], contract[1:]), ((), ())), pr...]
    all_gather x5 -> x0, waiting for transfers between devices: 143 us -> none  [the longest x1 57.5 us: body(): lax.all_gather(w_up, 'fsdp', axis=0, tiled=True)]
    psum x1 -> x0, waiting for transfers between devices: 139 us -> none  [body(): lax.psum(part_query.astype(jnp.bfloat16), 'dp').astype(jnp.float32)]
    dynamic_update_slice x0 -> x27, local copies, waits for them, and re-layouts: none -> 108 us  [the longest x1 44.3 us: reduce_rows(): lax.dynamic_update_slice_in_dim(whole, beside.astype(F32)[None], 1 - core...]
    ppermute x0 -> x61, starting transfers between devices: none -> 67.3 us  [the longest x49 52.3 us: swap_dp(): return lax.ppermute(value, 'dp', [(i, i ^ bit) for i in range(size)])]
    pallas_call x0 -> x4, Pallas kernels: none -> 52.2 us  [the longest x2 28.9 us: attention_back(): pl.pallas_call(attention_back_kernel, grid=(KEY_VALUE_HEADS,), in_specs=[...]
  transfers between devices with their start and end apart: 13 -> 61, of which waited for: 9 -> 22; matrix products, arithmetic and copies ran while one was open for 15% -> 35% of each run, Pallas kernels for 0% -> 1%
where the time goes in v1:
time: 788 us; the launch traced here: 773 us
  waiting for transfers between devices  216 us (27%)
  local copies, waits for them, and re-layouts  200 us (25%)
  matrix products  188 us (24%)
  starting transfers between devices  67.3 us (9%)
  Pallas kernels  52.2 us (7%)
  other arithmetic  46.3 us (6%)
    dot_general x30, matrix products, dot(): lax.dot_general(left, right, ((contract[:1], contract[1:]), ((), ())), pr...  188 us
    ppermute x49, waiting for transfers between devices, swap_dp(): return lax.ppermute(value, 'dp', [(i, i ^ bit) for i in range(size)])  147 us
    ppermute x12, waiting for transfers between devices, swap_fsdp(): return lax.ppermute(value, 'fsdp', [(0, 1), (1, 0)])  69.3 us
    ppermute x49, starting transfers between devices, swap_dp(): return lax.ppermute(value, 'dp', [(i, i ^ bit) for i in range(size)])  52.3 us
    dynamic_update_slice x1, local copies, waits for them, and re-layouts, reduce_rows(): lax.dynamic_update_slice_in_dim(whole, beside.astype(F32)[None], 1 - core...  44.3 us
    dynamic_update_slice x1, local copies, waits for them, and re-layouts, reduce_rows(): lax.dynamic_update_slice_in_dim(whole, half.astype(F32)[None], core, 0)  44.2 us
    pallas_call x2, Pallas kernels, attention_back(): pl.pallas_call(attention_back_kernel, grid=(KEY_VALUE_HEADS,), in_specs=[...  28.9 us
    unnamed x153, local copies, waits for them, and re-layouts  24.7 us
  transfers between devices with their start and end apart: 61, of which 22 were waited for; matrix products, arithmetic and copies ran while one was open for 35% of the time, Pallas kernels for 1%

profile of v1, /device:TPU:0, one launch (start us, length us, event | category | flops | bytes accessed | tf_op | source)
XLA Modules:
  0.0 772.7 jit_solution(15257237615715814233)
XLA Ops:
  56.4 8.9 %collective-permute-done.17 = bf16[320,960]{1,0:T(8,128)(2,1)S(1)} collective-permute-done((bf16[320,960]{1,0:T(8,128)(2,1)}, bf16[320,960]{1,0:T(8,128)(2,1)S(1)}, u32[]{:S(2)}, u32[]{:S(2)}) %collective-permute-start.17) | collective-permute-done | bytes 614432 | tf_op jit(solution)/shard_map/ppermute | solution.py:252
  75.2 11.5 %attention.2 = (bf16[960,768]{1,0:T(8,128)(2,1)S(1)}, f32[5,8,768]{2,1,0:T(8,128)S(1)}) custom-call(s32[1,768]{1,0:T(1,128)S(1)} %broadcast_in_dim.80.start_ref, bf16[1600,768]{1,0:T(8,128)(2,1)S(1)} %pad_maximum_fusion.query_ref.key_ref.value_ref, bf16[1600,768]{1,0:T(8,128)(2,1)S(1)} %pad_maximum_fusion.query_ref.key_ref.value_ref, ...), custom_call_target="tpu_custom_call" | custom-call | flops 6000000000 | bytes 4000000 | tf_op jit(solution)/shard_map/attention/pallas_call | solution.py:73
  91.8 7.0 collective-permute-done.18
  110.9 11.3 %multiply_convert_fusion.3 = (bf16[768,2560]{1,0:T(8,128)(2,1)S(1)}, f32[768,2560]{1,0:T(8,128)}) fusion(f32[768,2560]{1,0:T(8,128)} %fusion.53, bf16[768,960]{0,1:T(8,128)(2,1)S(1)} %multiply_convert_fusion.6, bf16[960,2560]{1,0:T(8,128)(2,1)} %constant_dynamic-update-slice_fusion.5), kind=kOutput, calls=%fused_computation.14 | convolution fusion | flops 3786670080 | bytes 26050560 | tf_op jit(solution)/shard_map/dot_general | solution.py:24
  123.2 7.5 multiply_reduce_fusion.7
  135.2 11.8 %attention.3 = (bf16[960,768]{1,0:T(8,128)(2,1)S(1)}, f32[5,8,768]{2,1,0:T(8,128)S(1)}) custom-call(s32[1,768]{1,0:T(1,128)S(1)} %broadcast_in_dim.80.start_ref, bf16[1600,768]{1,0:T(8,128)(2,1)S(1)} %pad_maximum_fusion.1.query_ref.key_ref.value_ref, bf16[1600,768]{1,0:T(8,128)(2,1)S(1)} %pad_maximum_fusion.1.query_ref.key_ref.value_ref, ...), custom_call_target="tpu_custom_call" | custom-call | flops 6000000000 | bytes 4000000 | tf_op jit(solution)/shard_map/attention/pallas_call | solution.py:73
  150.6 9.0 %fusion.27 = f32[2560,768]{0,1:T(8,128)} fusion(bf16[2560,960]{1,0:T(8,128)(2,1)} %constant_dynamic-update-slice_fusion, bf16[1,768,960]{1,2,0:T(8,128)(2,1)S(1)} %copy-done.36), kind=kOutput, calls=%fused_computation.97 | convolution fusion | flops 3774873600 | bytes 14254080 | tf_op jit(solution)/shard_map/dot_general | solution.py:24
  167.5 15.7 %fusion.2 = (bf16[768,2560]{1,0:T(8,128)(2,1)}, bf16[768,2560]{1,0:T(8,128)(2,1)}, bf16[768,2560]{1,0:T(8,128)(2,1)}) fusion(f32[2560,768]{0,1:T(8,128)} %fusion.27, f32[768,2560]{1,0:T(8,128)} %fusion.54, bf16[768,960]{0,1:T(8,128)(2,1)} %copy-done.40, bf16[960,2560]{1,0:T(8,128)(2,1)} %constant_dynamic-update-slice_fusion.5), kind=kOutput, calls=%fused_computation.7 | convolution fusion | flops 3806330880 | bytes 33914880 | tf_op jit(solution)/shard_map/dot_general | solution.py:24
  183.2 7.4 fusion.55
  199.3 14.4 %attention_back.2 = bf16[1600,768]{1,0:T(8,128)(2,1)S(1)} custom-call(s32[1,768]{1,0:T(1,128)S(1)} %broadcast_in_dim.80.start_ref, f32[32,768]{1,0:T(8,128)S(1)} %get-tuple-element.96.cosine_ref, f32[32,768]{1,0:T(8,128)S(1)} %get-tuple-element.97.sine_ref, bf16[1600,768]{1,0:T(8,128)(2,1)S(1)} %pad_maximum_fusion.1.query_ref.key_ref.value_ref, ...), custom_call_target="tpu_custom_call" | custom-call | flops 8999999488 | bytes 9000000 | tf_op jit(solution)/shard_map/attention_back/pallas_call | solution.py:151
  240.2 7.9 %fusion.29 = bf16[1,768,960]{1,2,0:T(8,128)(2,1)} fusion(f32[768,960]{0,1:T(8,128)S(1)} %get-tuple-element.117, bf16[768,2560]{1,0:T(8,128)(2,1)S(1)} %copy-done.56, bf16[2560,960]{1,0:T(8,128)(2,1)} %constant_dynamic-update-slice_fusion), kind=kOutput, calls=%fused_computation.99 | convolution fusion | flops 3776348160 | bytes 13271040 | tf_op jit(solution)/shard_map/dot_general | solution.py:24
  255.3 14.1 %multiply_convert_fusion.1 = (bf16[768,2560]{1,0:T(8,128)(2,1)}, bf16[768,2560]{1,0:T(8,128)(2,1)}) fusion(f32[768,2560]{1,0:T(8,128)} %fusion.53, f32[768,2560]{1,0:T(8,128)} %get-tuple-element.113, bf16[2560,960]{1,0:T(8,128)(2,1)} %constant_dynamic-update-slice_fusion, f32[768,960]{0,1:T(8,128)S(1)} %subtract_add_fusion.1), kind=kOutput, calls=%fused_computation.11 | convolution fusion | flops 3801169920 | bytes 31457280 | tf_op jit(solution)/shard_map/dot_general | solution.py:24
  269.4 7.2 fusion.56
  285.5 14.6 %attention_back.3 = bf16[1600,768]{1,0:T(8,128)(2,1)S(1)} custom-call(s32[1,768]{1,0:T(1,128)S(1)} %broadcast_in_dim.80.start_ref, f32[32,768]{1,0:T(8,128)S(1)} %get-tuple-element.96.cosine_ref, f32[32,768]{1,0:T(8,128)S(1)} %get-tuple-element.97.sine_ref, bf16[1600,768]{1,0:T(8,128)(2,1)S(1)} %copy-done.1, bf16[1600,768]{1,0:T(8,128)(2,1)S(1)} %copy-done.1, ...), custom_call_target="tpu_custom_call" | custom-call | flops 8999999488 | bytes 9000000 | tf_op jit(solution)/shard_map/attention_back/pallas_call | solution.py:151
  313.3 6.7 add_convert_fusion.2
  324.8 8.3 %add_convert_fusion = bf16[2560,960]{0,1:T(8,128)(2,1)} fusion(f32[2560,960]{0,1:T(8,128)} %fusion.25, bf16[768,2560]{1,0:T(8,128)(2,1)S(1)} %copy-done.60, f32[768,960]{0,1:T(8,128)S(1)} %subtract_add_fusion.1), kind=kOutput, calls=%fused_computation | convolution fusion | flops 3780526080 | bytes 21626880 | tf_op jit(solution)/shard_map/dot_general | solution.py:24
  333.1 8.1 %add_convert_fusion.1 = bf16[960,2560]{1,0:T(8,128)(2,1)} fusion(f32[960,2560]{1,0:T(8,128)} %fusion.58, bf16[768,960]{0,1:T(8,128)(2,1)S(1)} %copy-done.39, bf16[768,2560]{1,0:T(8,128)(2,1)S(1)} %copy-done.53), kind=kOutput, calls=%fused_computation.1 | convolution fusion | flops 3779788800 | bytes 20152320 | tf_op jit(solution)/shard_map/dot_general | solution.py:24
  341.3 11.0 %reshape.368 = bf16[2,2,640,960]{2,1,0,3:T(2,128)(2,1)} reshape(bf16[2560,960]{0,1:T(8,128)(2,1)} %add_convert_fusion) | data formatting | bytes 9830400 | tf_op jit(solution)/shard_map/reshape | solution.py:289
  353.2 12.5 %constant_dynamic-slice_fusion.2 = (bf16[2,1,640,960]{2,1,0,3:T(2,128)(2,1)S(1)}, bf16[2,1,640,960]{2,1,0,3:T(2,128)(2,1)S(1)}) fusion(bf16[2,2,640,960]{2,1,0,3:T(2,128)(2,1)} %reshape.368, s32[]{:T(128)S(6)} %select_n.254, s32[]{:T(128)S(6)} %select_n.255), kind=kLoop, calls=%fused_computation.167 | loop fusion | bytes 9830408 | tf_op jit(solution)/shard_map/jit(dynamic_index_in_dim)/dynamic_slice | solution.py:290
  373.3 8.3 %collective-permute-done.29 = bf16[240,960]{1,0:T(8,128)(2,1)S(1)} collective-permute-done((bf16[240,960]{1,0:T(8,128)(2,1)S(1)}, bf16[240,960]{1,0:T(8,128)(2,1)S(1)}, u32[]{:S(2)}, u32[]{:S(2)}) %collective-permute-start.29) | collective-permute-done | bytes 460832 | tf_op jit(solution)/shard_map/ppermute | solution.py:252
  399.3 6.8 collective-permute-done.32
  413.5 12.7 %collective-permute-done.22 = bf16[240,1600]{1,0:T(8,128)(2,1)S(1)} collective-permute-done((bf16[240,1600]{1,0:T(8,128)(2,1)S(1)}, bf16[240,1600]{1,0:T(8,128)(2,1)S(1)}, u32[]{:S(2)}, u32[]{:S(2)}) %collective-permute-start.22) | collective-permute-done | bytes 768032 | tf_op jit(solution)/shard_map/ppermute | solution.py:252
  451.3 13.5 %collective-permute-done.25 = bf16[120,1600]{1,0:T(8,128)(2,1)S(1)} collective-permute-done((bf16[120,1600]{1,0:T(8,128)(2,1)S(1)}, bf16[120,1600]{1,0:T(8,128)(2,1)S(1)}, u32[]{:S(2)}, u32[]{:S(2)}) %collective-permute-start.25) | collective-permute-done | bytes 384032 | tf_op jit(solution)/shard_map/ppermute | solution.py:256
  467.5 19.5 %collective-permute-done.48 = bf16[240,2560]{1,0:T(8,128)(2,1)S(1)} collective-permute-done((bf16[240,2560]{1,0:T(8,128)(2,1)S(1)}, bf16[240,2560]{1,0:T(8,128)(2,1)S(1)}, u32[]{:S(2)}, u32[]{:S(2)}) %collective-permute-start.48) | collective-permute-done | bytes 1228832 | tf_op jit(solution)/shard_map/ppermute | solution.py:252
  489.7 19.9 %collective-permute-done.55 = bf16[640,960]{0,1:T(8,128)(2,1)S(1)} collective-permute-done((bf16[640,960]{0,1:T(8,128)(2,1)S(1)}, bf16[640,960]{0,1:T(8,128)(2,1)S(1)}, u32[]{:S(2)}, u32[]{:S(2)}) %collective-permute-start.55) | collective-permute-done | bytes 1228832 | tf_op jit(solution)/shard_map/ppermute | solution.py:252
  540.0 21.7 %collective-permute-done.50 = bf16[120,2560]{1,0:T(8,128)(2,1)} collective-permute-done((bf16[120,2560]{1,0:T(8,128)(2,1)}, bf16[120,2560]{1,0:T(8,128)(2,1)}, u32[]{:S(2)}, u32[]{:S(2)}) %collective-permute-start.50) | collective-permute-done | bytes 614432 | tf_op jit(solution)/shard_map/ppermute | solution.py:256
  566.0 9.6 %collective-permute-done.57 = bf16[320,960]{1,0:T(8,128)(2,1)} collective-permute-done((bf16[320,960]{1,0:T(8,128)(2,1)S(1)}, bf16[320,960]{1,0:T(8,128)(2,1)}, u32[]{:S(2)}, u32[]{:S(2)}) %collective-permute-start.57) | collective-permute-done | bytes 614432 | tf_op jit(solution)/shard_map/ppermute | solution.py:256
  580.2 38.5 %collective-permute-done.51 = bf16[120,2560]{1,0:T(8,128)(2,1)S(1)} collective-permute-done((bf16[120,2560]{1,0:T(8,128)(2,1)S(1)}, bf16[120,2560]{1,0:T(8,128)(2,1)S(1)}, u32[]{:S(2)}, u32[]{:S(2)}) %collective-permute-start.51) | collective-permute-done | bytes 614432 | tf_op jit(solution)/shard_map/ppermute | solution.py:256
  619.4 13.3 %collective-permute-done.58 = bf16[320,960]{1,0:T(8,128)(2,1)S(1)} collective-permute-done((bf16[320,960]{1,0:T(8,128)(2,1)S(1)}, bf16[320,960]{1,0:T(8,128)(2,1)S(1)}, u32[]{:S(2)}, u32[]{:S(2)}) %collective-permute-start.58) | collective-permute-done | bytes 614432 | tf_op jit(solution)/shard_map/ppermute | solution.py:256
  636.6 13.1 %collective-permute-done.59 = bf16[320,960]{1,0:T(8,128)(2,1)S(1)} collective-permute-done((bf16[320,960]{1,0:T(8,128)(2,1)S(1)}, bf16[320,960]{1,0:T(8,128)(2,1)S(1)}, u32[]{:S(2)}, u32[]{:S(2)}) %collective-permute-start.59) | collective-permute-done | bytes 614432 | tf_op jit(solution)/shard_map/ppermute | solution.py:256
  669.2 44.2 %dynamic_update_slice.138 = f32[2,640,960]{1,0,2:T(2,128)} dynamic-update-slice(f32[2,640,960]{1,0,2:T(2,128)} %broadcast_in_dim.96, f32[1,640,960]{1,0,2:T(1,128)S(1)} %copy.62, s32[]{:T(128)S(6)} %select_n.254, s32[]{:T(128)} %constant.194.clone.1, s32[]{:T(128)} %constant.194.clone.1) | dynamic-update-slice | bytes 4915204 | tf_op jit(solution)/shard_map/dynamic_update_slice | solution.py:305
  717.4 44.3 %dynamic_update_slice.139 = f32[2,640,960]{1,0,2:T(2,128)} dynamic-update-slice(f32[2,640,960]{1,0,2:T(2,128)} %dynamic_update_slice.138, f32[1,640,960]{1,0,2:T(1,128)S(1)} %copy.64, s32[]{:T(128)S(6)} %select_n.255, s32[]{:T(128)} %constant.194.clone.1, s32[]{:T(128)} %constant.194.clone.1) | dynamic-update-slice | bytes 4915204 | tf_op jit(solution)/shard_map/dynamic_update_slice | solution.py:306
  (441 shorter events, 309.9 us)
Async XLA Ops:
  7.2 38.4 %collective-permute-start = (bf16[120,1600]{1,0:T(8,128)(2,1)}, bf16[120,1600]{1,0:T(8,128)(2,1)S(1)}, u32[]{:S(2)}, u32[]{:S(2)}) collective-permute-start(bf16[120,1600]{1,0:T(8,128)(2,1)} %constant_dynamic-slice_fusion.8), channel_id=1, source_target_pairs={{0,1},{1,0},{2,3},{3,2},{4,5},{5,4},{6,7},{7,6},{8,9},{9,8},{10,11... | collective-permute-start | bytes 1152008 | tf_op jit(solution)/shard_map/ppermute | solution.py:252
  10.2 31.5 %collective-permute-start.4 = (bf16[2,480]{1,0:T(2,128)(2,1)S(1)}, bf16[2,480]{1,0:T(2,128)(2,1)S(1)}, u32[]{:S(2)}, u32[]{:S(2)}) collective-permute-start(bf16[2,480]{1,0:T(2,128)(2,1)S(1)} %pad_maximum_fusion.10), channel_id=1, source_target_pairs={{0,1},{1,0},{2,3},{3,2},{4,5},{5,4},{6,7},{7,6},{8,9},{9,8},{10,11... | collective-permute-start | bytes 5768 | tf_op jit(solution)/shard_map/ppermute | solution.py:252
  11.9 29.9 %collective-permute-start.5 = (bf16[120,960]{1,0:T(8,128)(2,1)}, bf16[120,960]{1,0:T(8,128)(2,1)}, u32[]{:S(2)}, u32[]{:S(2)}) collective-permute-start(bf16[120,960]{1,0:T(8,128)(2,1)} %constant_dynamic-slice_fusion.7), channel_id=1, source_target_pairs={{0,1},{1,0},{2,3},{3,2},{4,5},{5,4},{6,7},{7,6},{8,9},{9,8},{10,11... | collective-permute-start | bytes 691208 | tf_op jit(solution)/shard_map/ppermute | solution.py:252
  15.9 35.9 %collective-permute-start.9 = (bf16[120,2560]{1,0:T(8,128)(2,1)}, bf16[120,2560]{1,0:T(8,128)(2,1)}, u32[]{:S(2)}, u32[]{:S(2)}) collective-permute-start(bf16[120,2560]{1,0:T(8,128)(2,1)} %constant_dynamic-slice_fusion.6), channel_id=1, source_target_pairs={{0,1},{1,0},{2,3},{3,2},{4,5},{5,4},{6,7},{7,6},{8,9},{9,8},{10,11... | collective-permute-start | bytes 1843208 | tf_op jit(solution)/shard_map/ppermute | solution.py:252
  17.8 36.4 %collective-permute-start.13 = (bf16[120,2560]{1,0:T(8,128)(2,1)}, bf16[120,2560]{1,0:T(8,128)(2,1)}, u32[]{:S(2)}, u32[]{:S(2)}) collective-permute-start(bf16[120,2560]{1,0:T(8,128)(2,1)} %constant_dynamic-slice_fusion.5), channel_id=1, source_target_pairs={{0,1},{1,0},{2,3},{3,2},{4,5},{5,4},{6,7},{7,6},{8,9},{9,8},{10,11... | collective-permute-start | bytes 1843208 | tf_op jit(solution)/shard_map/ppermute | solution.py:252
  54.3 45.3 %collective-permute-start.10 = (bf16[120,2560]{1,0:T(8,128)(2,1)}, bf16[120,2560]{1,0:T(8,128)(2,1)S(1)}, u32[]{:S(2)}, u32[]{:S(2)}) collective-permute-start(bf16[120,2560]{1,0:T(8,128)(2,1)} %collective-permute-done.9), channel_id=1, source_target_pairs={{0,4},{2,6},{4,0},{6,2},{8,12},{10,14},{12,8},{14,10},{16,20},{18,... | collective-permute-start | bytes 1843208 | tf_op jit(solution)/shard_map/ppermute | solution.py:256
  65.3 37.2 %collective-permute-start.11 = (bf16[120,2560]{1,0:T(8,128)(2,1)}, bf16[120,2560]{1,0:T(8,128)(2,1)S(1)}, u32[]{:S(2)}, u32[]{:S(2)}) collective-permute-start(bf16[120,2560]{1,0:T(8,128)(2,1)} %collective-permute-done.9), channel_id=1, source_target_pairs={{0,2},{2,0},{4,6},{6,4},{8,10},{10,8},{12,14},{14,12},{16,18},{18,... | collective-permute-start | bytes 1843208 | tf_op jit(solution)/shard_map/ppermute | solution.py:256
  66.2 34.0 %collective-permute-start.14 = (bf16[120,2560]{1,0:T(8,128)(2,1)}, bf16[120,2560]{1,0:T(8,128)(2,1)S(1)}, u32[]{:S(2)}, u32[]{:S(2)}) collective-permute-start(bf16[120,2560]{1,0:T(8,128)(2,1)} %collective-permute-done.13), channel_id=1, source_target_pairs={{0,4},{2,6},{4,0},{6,2},{8,12},{10,14},{12,8},{14,10},{16,20},{18,... | collective-permute-start | bytes 1843208 | tf_op jit(solution)/shard_map/ppermute | solution.py:256
  69.0 29.7 %collective-permute-start.18 = (bf16[320,960]{1,0:T(8,128)(2,1)S(1)}, bf16[320,960]{1,0:T(8,128)(2,1)S(1)}, u32[]{:S(2)}, u32[]{:S(2)}) collective-permute-start(bf16[320,960]{1,0:T(8,128)(2,1)S(1)} %collective-permute-done.17), channel_id=1, source_target_pairs={{0,4},{2,6},{4,0},{6,2},{8,12},{10,14},{12,8},{14,10},{16,20},{18,... | collective-permute-start | bytes 1843208 | tf_op jit(solution)/shard_map/ppermute | solution.py:256
  70.4 29.8 %collective-permute-start.19 = (bf16[320,960]{1,0:T(8,128)(2,1)S(1)}, bf16[320,960]{1,0:T(8,128)(2,1)S(1)}, u32[]{:S(2)}, u32[]{:S(2)}) collective-permute-start(bf16[320,960]{1,0:T(8,128)(2,1)S(1)} %collective-permute-done.17), channel_id=1, source_target_pairs={{0,2},{2,0},{4,6},{6,4},{8,10},{10,8},{12,14},{14,12},{16,18},{18,... | collective-permute-start | bytes 1843208 | tf_op jit(solution)/shard_map/ppermute | solution.py:256
  309.5 87.9 %collective-permute-start.21 = (bf16[2,240,1600]{2,1,0:T(8,128)(2,1)}, bf16[2,240,1600]{2,1,0:T(8,128)(2,1)}, u32[]{:S(2)}, u32[]{:S(2)}) collective-permute-start(bf16[2,240,1600]{2,1,0:T(8,128)(2,1)} %dynamic-slice_bitcast_fusion.2), channel_id=1, source_target_pairs={{0,2},{2,0},{4,6},{6,4},{8,10},{10,8},{12,14},{14,12},{16,18},{18,... | collective-permute-start | bytes 4608008 | tf_op jit(solution)/shard_map/ppermute | solution.py:256
  312.4 54.9 %collective-permute-start.28 = (bf16[2,240,960]{2,1,0:T(8,128)(2,1)}, bf16[2,240,960]{2,1,0:T(8,128)(2,1)}, u32[]{:S(2)}, u32[]{:S(2)}) collective-permute-start(bf16[2,240,960]{2,1,0:T(8,128)(2,1)} %dynamic-slice_bitcast_fusion.6), channel_id=1, source_target_pairs={{0,2},{2,0},{4,6},{6,4},{8,10},{10,8},{12,14},{14,12},{16,18},{18,... | collective-permute-start | bytes 2764808 | tf_op jit(solution)/shard_map/ppermute | solution.py:256
  312.9 39.3 %collective-permute-start.35 = (bf16[2,960]{1,0:T(2,128)(2,1)S(1)}, bf16[2,960]{1,0:T(2,128)(2,1)S(1)}, u32[]{:S(2)}, u32[]{:S(2)}) collective-permute-start(bf16[2,960]{1,0:T(2,128)(2,1)S(1)} %pad_maximum_fusion.9), channel_id=1, source_target_pairs={{0,2},{2,0},{4,6},{6,4},{8,10},{10,8},{12,14},{14,12},{16,18},{18,... | collective-permute-start | bytes 11528 | tf_op jit(solution)/shard_map/ppermute | solution.py:256
  321.7 105.3 %collective-permute-start.40 = (bf16[2,240,2560]{2,1,0:T(8,128)(2,1)}, bf16[2,240,2560]{2,1,0:T(8,128)(2,1)}, u32[]{:S(2)}, u32[]{:S(2)}) collective-permute-start(bf16[2,240,2560]{2,1,0:T(8,128)(2,1)} %dynamic-slice_bitcast_fusion.1), channel_id=1, source_target_pairs={{0,2},{2,0},{4,6},{6,4},{8,10},{10,8},{12,14},{14,12},{16,18},{18,... | collective-permute-start | bytes 7372808 | tf_op jit(solution)/shard_map/ppermute | solution.py:256
  383.3 48.5 %collective-permute-start.47 = (bf16[2,240,2560]{2,1,0:T(8,128)(2,1)S(1)}, bf16[2,240,2560]{2,1,0:T(8,128)(2,1)}, u32[]{:S(2)}, u32[]{:S(2)}) collective-permute-start(bf16[2,240,2560]{2,1,0:T(8,128)(2,1)S(1)} %dynamic-slice_bitcast_fusion), channel_id=1, source_target_pairs={{0,2},{2,0},{4,6},{6,4},{8,10},{10,8},{12,14},{14,12},{16,18},{18,... | collective-permute-start | bytes 7372808 | tf_op jit(solution)/shard_map/ppermute | solution.py:256
  391.3 47.3 %collective-permute-start.54 = (bf16[2,640,960]{1,2,0:T(8,128)(2,1)S(1)}, bf16[2,640,960]{1,2,0:T(8,128)(2,1)S(1)}, u32[]{:S(2)}, u32[]{:S(2)}) collective-permute-start(bf16[2,640,960]{1,2,0:T(8,128)(2,1)S(1)} %bitcast.284), channel_id=1, source_target_pairs={{0,2},{2,0},{4,6},{6,4},{8,10},{10,8},{12,14},{14,12},{16,18},{18,... | collective-permute-start | bytes 7372808 | tf_op jit(solution)/shard_map/ppermute | solution.py:256
  413.1 38.1 %collective-permute-start.34 = (bf16[240,960]{1,0:T(8,128)(2,1)S(1)}, bf16[240,960]{1,0:T(8,128)(2,1)S(1)}, u32[]{:S(2)}, u32[]{:S(2)}) collective-permute-start(bf16[240,960]{1,0:T(8,128)(2,1)S(1)} %bitcast.288), channel_id=1, source_target_pairs={{0,2},{2,0},{4,6},{6,4},{8,10},{10,8},{12,14},{14,12},{16,18},{18,... | collective-permute-start | bytes 1382408 | tf_op jit(solution)/shard_map/ppermute | solution.py:256
  430.5 34.9 %collective-permute-start.41 = (bf16[240,2560]{1,0:T(8,128)(2,1)}, bf16[240,2560]{1,0:T(8,128)(2,1)S(1)}, u32[]{:S(2)}, u32[]{:S(2)}) collective-permute-start(bf16[240,2560]{1,0:T(8,128)(2,1)} %dynamic-slice_bitcast_fusion.5), channel_id=1, source_target_pairs={{0,1},{1,0},{2,3},{3,2},{4,5},{5,4},{6,7},{7,6},{8,9},{9,8},{10,11... | collective-permute-start | bytes 3686408 | tf_op jit(solution)/shard_map/ppermute | solution.py:252
  434.2 52.8 %collective-permute-start.48 = (bf16[240,2560]{1,0:T(8,128)(2,1)S(1)}, bf16[240,2560]{1,0:T(8,128)(2,1)S(1)}, u32[]{:S(2)}, u32[]{:S(2)}) collective-permute-start(bf16[240,2560]{1,0:T(8,128)(2,1)S(1)} %dynamic-slice_bitcast_fusion.4), channel_id=1, source_target_pairs={{0,1},{1,0},{2,3},{3,2},{4,5},{5,4},{6,7},{7,6},{8,9},{9,8},{10,11... | collective-permute-start | bytes 3686408 | tf_op jit(solution)/shard_map/ppermute | solution.py:252
  449.8 59.9 %collective-permute-start.55 = (bf16[640,960]{0,1:T(8,128)(2,1)S(1)}, bf16[640,960]{0,1:T(8,128)(2,1)S(1)}, u32[]{:S(2)}, u32[]{:S(2)}) collective-permute-start(bf16[640,960]{0,1:T(8,128)(2,1)S(1)} %dynamic-slice_bitcast_fusion.3), channel_id=1, source_target_pairs={{0,1},{1,0},{2,3},{3,2},{4,5},{5,4},{6,7},{7,6},{8,9},{9,8},{10,11... | collective-permute-start | bytes 3686408 | tf_op jit(solution)/shard_map/ppermute | solution.py:252
  464.9 49.6 %collective-permute-start.26 = (bf16[120,1600]{1,0:T(8,128)(2,1)S(1)}, bf16[120,1600]{1,0:T(8,128)(2,1)}, u32[]{:S(2)}, u32[]{:S(2)}) collective-permute-start(bf16[120,1600]{1,0:T(8,128)(2,1)S(1)} %add_convert_fusion.14), channel_id=1, source_target_pairs={{0,4},{2,6},{4,0},{6,2},{8,12},{10,14},{12,8},{14,10},{16,20},{18,... | collective-permute-start | bytes 1152008 | tf_op jit(solution)/shard_map/ppermute | solution.py:256
  465.7 50.3 %collective-permute-start.42 = (bf16[120,2560]{1,0:T(8,128)(2,1)S(1)}, bf16[120,2560]{1,0:T(8,128)(2,1)}, u32[]{:S(2)}, u32[]{:S(2)}) collective-permute-start(bf16[120,2560]{1,0:T(8,128)(2,1)S(1)} %dynamic-slice_bitcast_fusion.10), channel_id=1, source_target_pairs={{0,4},{2,6},{4,0},{6,2},{8,12},{10,14},{12,8},{14,10},{16,20},{18,... | collective-permute-start | bytes 1843208 | tf_op jit(solution)/shard_map/ppermute | solution.py:256
  488.3 32.3 %collective-permute-start.49 = (bf16[120,2560]{1,0:T(8,128)(2,1)}, bf16[120,2560]{1,0:T(8,128)(2,1)}, u32[]{:S(2)}, u32[]{:S(2)}) collective-permute-start(bf16[120,2560]{1,0:T(8,128)(2,1)} %dynamic-slice_bitcast_fusion.9), channel_id=1, source_target_pairs={{0,4},{2,6},{4,0},{6,2},{8,12},{10,14},{12,8},{14,10},{16,20},{18,... | collective-permute-start | bytes 1843208 | tf_op jit(solution)/shard_map/ppermute | solution.py:256
  522.6 39.1 %collective-permute-start.50 = (bf16[120,2560]{1,0:T(8,128)(2,1)}, bf16[120,2560]{1,0:T(8,128)(2,1)}, u32[]{:S(2)}, u32[]{:S(2)}) collective-permute-start(bf16[120,2560]{1,0:T(8,128)(2,1)} %fusion.31), channel_id=1, source_target_pairs={{0,8},{2,10},{4,12},{6,14},{8,0},{10,2},{12,4},{14,6},{16,24},{18,... | collective-permute-start | bytes 1843208 | tf_op jit(solution)/shard_map/ppermute | solution.py:256
  526.4 49.3 %collective-permute-start.57 = (bf16[320,960]{1,0:T(8,128)(2,1)S(1)}, bf16[320,960]{1,0:T(8,128)(2,1)}, u32[]{:S(2)}, u32[]{:S(2)}) collective-permute-start(bf16[320,960]{1,0:T(8,128)(2,1)S(1)} %fusion.30), channel_id=1, source_target_pairs={{0,8},{2,10},{4,12},{6,14},{8,0},{10,2},{12,4},{14,6},{16,24},{18,... | collective-permute-start | bytes 1843208 | tf_op jit(solution)/shard_map/ppermute | solution.py:256
  536.6 43.0 %collective-permute-start.44 = (bf16[120,2560]{1,0:T(8,128)(2,1)S(1)}, bf16[120,2560]{1,0:T(8,128)(2,1)S(1)}, u32[]{:S(2)}, u32[]{:S(2)}) collective-permute-start(bf16[120,2560]{1,0:T(8,128)(2,1)S(1)} %add_convert_fusion.13), channel_id=1, source_target_pairs={{0,16},{2,18},{4,20},{6,22},{8,24},{10,26},{12,28},{14,30},{16,0},... | collective-permute-start | bytes 1843208 | tf_op jit(solution)/shard_map/ppermute | solution.py:256
  563.1 55.6 %collective-permute-start.51 = (bf16[120,2560]{1,0:T(8,128)(2,1)S(1)}, bf16[120,2560]{1,0:T(8,128)(2,1)S(1)}, u32[]{:S(2)}, u32[]{:S(2)}) collective-permute-start(bf16[120,2560]{1,0:T(8,128)(2,1)S(1)} %add_convert_fusion.11), channel_id=1, source_target_pairs={{0,16},{2,18},{4,20},{6,22},{8,24},{10,26},{12,28},{14,30},{16,0},... | collective-permute-start | bytes 1843208 | tf_op jit(solution)/shard_map/ppermute | solution.py:256
  577.0 55.7 %collective-permute-start.58 = (bf16[320,960]{1,0:T(8,128)(2,1)S(1)}, bf16[320,960]{1,0:T(8,128)(2,1)S(1)}, u32[]{:S(2)}, u32[]{:S(2)}) collective-permute-start(bf16[320,960]{1,0:T(8,128)(2,1)S(1)} %add_convert_fusion.9), channel_id=1, source_target_pairs={{0,16},{2,18},{4,20},{6,22},{8,24},{10,26},{12,28},{14,30},{16,0},... | collective-permute-start | bytes 1843208 | tf_op jit(solution)/shard_map/ppermute | solution.py:256
  579.7 53.7 %collective-permute-start.45 = (bf16[120,2560]{1,0:T(8,128)(2,1)S(1)}, bf16[120,2560]{1,0:T(8,128)(2,1)S(1)}, u32[]{:S(2)}, u32[]{:S(2)}) collective-permute-start(bf16[120,2560]{1,0:T(8,128)(2,1)S(1)} %add_convert_fusion.12), channel_id=1, source_target_pairs={{0,4},{2,6},{4,0},{6,2},{8,12},{10,14},{12,8},{14,10},{16,20},{18,... | collective-permute-start | bytes 1843208 | tf_op jit(solution)/shard_map/ppermute | solution.py:256
  634.7 132.0 %collective-permute-start.46 = (bf16[240,2560]{1,0:T(8,128)(2,1)}, bf16[240,2560]{1,0:T(8,128)(2,1)}, u32[]{:S(2)}, u32[]{:S(2)}) collective-permute-start(bf16[240,2560]{1,0:T(8,128)(2,1)} %bitcast.53), channel_id=1, source_target_pairs={{0,2},{2,0},{4,6},{6,4},{8,10},{10,8},{12,14},{14,12},{16,18},{18,... | collective-permute-start | bytes 3686408 | tf_op jit(solution)/shard_map/ppermute | solution.py:256
  636.1 132.3 %collective-permute-start.53 = (bf16[240,2560]{1,0:T(8,128)(2,1)}, bf16[240,2560]{1,0:T(8,128)(2,1)}, u32[]{:S(2)}, u32[]{:S(2)}) collective-permute-start(bf16[240,2560]{1,0:T(8,128)(2,1)} %bitcast.67), channel_id=1, source_target_pairs={{0,2},{2,0},{4,6},{6,4},{8,10},{10,8},{12,14},{14,12},{16,18},{18,... | collective-permute-start | bytes 3686408 | tf_op jit(solution)/shard_map/ppermute | solution.py:256
  651.3 62.1 %collective-permute-start.60 = (bf16[640,960]{0,1:T(8,128)(2,1)}, bf16[640,960]{0,1:T(8,128)(2,1)}, u32[]{:S(2)}, u32[]{:S(2)}) collective-permute-start(bf16[640,960]{0,1:T(8,128)(2,1)} %copy.63), channel_id=1, source_target_pairs={{0,2},{2,0},{4,6},{6,4},{8,10},{10,8},{12,14},{14,12},{16,18},{18,... | collective-permute-start | bytes 3686408 | tf_op jit(solution)/shard_map/ppermute | solution.py:256
  (102 other events, 1424.6 us)

commit v2 on v1

v2 whole, which is shorter than its diff:
```python
from functools import partial

import jax
import jax.numpy as jnp
from jax import lax
from jax.experimental import pallas as pl
from jax.experimental.pallas import tpu as pltpu
from jax.sharding import PartitionSpec as P

QUERY_HEADS = 15
KEY_VALUE_HEADS = 5
GROUP = QUERY_HEADS // KEY_VALUE_HEADS
HEAD_SIZE = 64
HALF = HEAD_SIZE // 2
LONGEST_DOC = 384
EPSILON = 1e-05
ROPE_BASE = 10000.0
NEGATIVE = -1e30
SCALE = HEAD_SIZE ** (-0.5)
QUERY_BLOCK = 128
BF16 = jnp.bfloat16
F32 = jnp.float32
HBM = pltpu.HBM
FFN_GRANT = 24 << 20
BACK_GRANT = 40 << 20
GRAD_GRANT = 24 << 20
MIXED_GRANT = 36 << 20


def dot(left, right, contract):
    return lax.dot_general(left, right, ((contract[:1], contract[1:]), ((), ())), preferred_element_type=F32)


def key_window(block):
    return (max(0, block * QUERY_BLOCK - LONGEST_DOC), (block + 1) * QUERY_BLOCK)


def fill_mask(start_ref, mask_ref):
    for block in range(mask_ref.shape[0] // QUERY_BLOCK):
        low, high = key_window(block)
        cols = slice(block * QUERY_BLOCK, high)
        shape = (high - low, QUERY_BLOCK)
        key = low + lax.broadcasted_iota(jnp.int32, shape, 0)
        query = block * QUERY_BLOCK + lax.broadcasted_iota(jnp.int32, shape, 1)
        allowed = (key >= start_ref[:, cols]) & (key <= query)
        mask_ref[low:high, cols] = jnp.where(allowed, 0.0, NEGATIVE)


def side_by_side(ref, cols):
    return jnp.concatenate([ref[j * HEAD_SIZE : (j + 1) * HEAD_SIZE, cols] for j in range(GROUP)], axis=1)


def attention_kernel(start_ref, query_ref, key_ref, value_ref, mix_ref, logsum_ref, mask_ref, key_rows_ref):
    @pl.when(pl.program_id(0) == 0)
    def _():
        fill_mask(start_ref, mask_ref)

    key_rows_ref[...] = key_ref[...].T
    for block in range(query_ref.shape[1] // QUERY_BLOCK):
        low, high = key_window(block)
        cols = slice(block * QUERY_BLOCK, high)
        queries = side_by_side(query_ref, cols)
        mask = jnp.concatenate([mask_ref[low:high, cols]] * GROUP, axis=1)
        scores = dot(key_rows_ref[low:high, :], queries, (1, 0)) * SCALE + mask
        top = jnp.max(scores, axis=0, keepdims=True)
        weights = jnp.exp(scores - top)
        total = jnp.sum(weights, axis=0, keepdims=True)
        mix = dot(value_ref[:, low:high], weights.astype(BF16), (1, 0))
        mix = (mix / total).astype(BF16)
        logsum = top + jnp.log(total)
        for j in range(GROUP):
            part = slice(j * QUERY_BLOCK, (j + 1) * QUERY_BLOCK)
            mix_ref[j * HEAD_SIZE : (j + 1) * HEAD_SIZE, cols] = mix[:, part]
            logsum_ref[0, j : j + 1, cols] = logsum[:, part]


def attention(start, qkv):
    length = qkv.shape[1]
    rows = GROUP * HEAD_SIZE
    return pl.pallas_call(
        attention_kernel,
        grid=(KEY_VALUE_HEADS,),
        in_specs=[
            pl.BlockSpec((1, length), lambda g: (0, 0)),
            pl.BlockSpec((rows, length), lambda g: (g, 0)),
            pl.BlockSpec((HEAD_SIZE, length), lambda g: (QUERY_HEADS + g, 0)),
            pl.BlockSpec((HEAD_SIZE, length), lambda g: (QUERY_HEADS + KEY_VALUE_HEADS + g, 0)),
        ],
        out_specs=[
            pl.BlockSpec((rows, length), lambda g: (g, 0)),
            pl.BlockSpec((1, 8, length), lambda g: (g, 0, 0)),
        ],
        out_shape=[
            jax.ShapeDtypeStruct((QUERY_HEADS * HEAD_SIZE, length), BF16),
            jax.ShapeDtypeStruct((KEY_VALUE_HEADS, 8, length), F32),
        ],
        scratch_shapes=[pltpu.VMEM((length, length), F32), pltpu.VMEM((length, HEAD_SIZE), BF16)],
        compiler_params=pltpu.CompilerParams(vmem_limit_bytes=8 << 20),
        cost_estimate=pl.CostEstimate(flops=6_000_000_000, bytes_accessed=4_000_000, transcendentals=4_500_000),
        name="attention",
    )(start, qkv, qkv, qkv)


def unrotate(rows, cosine, sine):
    first = rows[:HALF]
    second = rows[HALF:]
    return (first * cosine + second * sine, second * cosine - first * sine)


def attention_back_kernel(
    start_ref, cosine_ref, sine_ref, query_ref, key_ref, value_ref, mix_ref, logsum_ref, mix_grad_ref,
    out_ref, mask_ref, key_rows_ref, value_rows_ref, key_grad_ref, value_grad_ref,
):
    group = pl.program_id(0)

    @pl.when(group == 0)
    def _():
        fill_mask(start_ref, mask_ref)

    key_rows_ref[...] = key_ref[...].T
    value_rows_ref[...] = value_ref[...].T
    key_grad_ref[...] = jnp.zeros_like(key_grad_ref)
    value_grad_ref[...] = jnp.zeros_like(value_grad_ref)
    for block in range(query_ref.shape[1] // QUERY_BLOCK):
        low, high = key_window(block)
        cols = slice(block * QUERY_BLOCK, high)
        queries = side_by_side(query_ref, cols)
        mix_grads = side_by_side(mix_grad_ref, cols)
        mixes = side_by_side(mix_ref, cols)
        inner = jnp.sum(mix_grads.astype(F32) * mixes.astype(F32), axis=0, keepdims=True)
        logsum = jnp.concatenate([logsum_ref[0, j : j + 1, cols] for j in range(GROUP)], axis=1)
        mask = jnp.concatenate([mask_ref[low:high, cols]] * GROUP, axis=1)
        scores = dot(key_rows_ref[low:high, :], queries, (1, 0)) * SCALE + mask
        weights = jnp.exp(scores - logsum)
        weight_grads = dot(value_rows_ref[low:high, :], mix_grads, (1, 0))
        score_grads = (weights * (weight_grads - inner)).astype(BF16)
        value_grad_ref[:, low:high] += dot(mix_grads, weights.astype(BF16), (1, 1))
        key_grad_ref[:, low:high] += dot(queries, score_grads, (1, 1))
        query_grads = dot(key_ref[:, low:high], score_grads, (1, 0)) * SCALE
        cosine = cosine_ref[:, cols]
        sine = sine_ref[:, cols]
        for j in range(GROUP):
            first, second = unrotate(query_grads[:, j * QUERY_BLOCK : (j + 1) * QUERY_BLOCK], cosine, sine)
            base = group * (GROUP * HEAD_SIZE) + j * HEAD_SIZE
            out_ref[pl.ds(pl.multiple_of(base, HALF), HALF), cols] = first.astype(BF16)
            out_ref[pl.ds(pl.multiple_of(base + HALF, HALF), HALF), cols] = second.astype(BF16)
    first, second = unrotate(key_grad_ref[...] * SCALE, cosine_ref[...], sine_ref[...])
    base = (QUERY_HEADS + group) * HEAD_SIZE
    out_ref[pl.ds(pl.multiple_of(base, HALF), HALF), :] = first.astype(BF16)
    out_ref[pl.ds(pl.multiple_of(base + HALF, HALF), HALF), :] = second.astype(BF16)
    base = (QUERY_HEADS + KEY_VALUE_HEADS + group) * HEAD_SIZE
    out_ref[pl.ds(pl.multiple_of(base, HEAD_SIZE), HEAD_SIZE), :] = value_grad_ref[...].astype(BF16)


def attention_back(start, cosine, sine, qkv, mix, logsum, mix_grad):
    length = qkv.shape[1]
    rows = GROUP * HEAD_SIZE
    return pl.pallas_call(
        attention_back_kernel,
        grid=(KEY_VALUE_HEADS,),
        in_specs=[
            pl.BlockSpec((1, length), lambda g: (0, 0)),
            pl.BlockSpec((HALF, length), lambda g: (0, 0)),
            pl.BlockSpec((HALF, length), lambda g: (0, 0)),
            pl.BlockSpec((rows, length), lambda g: (g, 0)),
            pl.BlockSpec((HEAD_SIZE, length), lambda g: (QUERY_HEADS + g, 0)),
            pl.BlockSpec((HEAD_SIZE, length), lambda g: (QUERY_HEADS + KEY_VALUE_HEADS + g, 0)),
            pl.BlockSpec((rows, length), lambda g: (g, 0)),
            pl.BlockSpec((1, 8, length), lambda g: (g, 0, 0)),
            pl.BlockSpec((rows, length), lambda g: (g, 0)),
        ],
        out_specs=pl.BlockSpec(qkv.shape, lambda g: (0, 0)),
        out_shape=jax.ShapeDtypeStruct(qkv.shape, BF16),
        scratch_shapes=[
            pltpu.VMEM((length, length), F32),
            pltpu.VMEM((length, HEAD_SIZE), BF16),
            pltpu.VMEM((length, HEAD_SIZE), BF16),
            pltpu.VMEM((HEAD_SIZE, length), F32),
            pltpu.VMEM((HEAD_SIZE, length), F32),
        ],
        compiler_params=pltpu.CompilerParams(vmem_limit_bytes=8 << 20),
        cost_estimate=pl.CostEstimate(flops=9_000_000_000, bytes_accessed=9_000_000, transcendentals=4_500_000),
        name="attention_back",
    )(start, cosine, sine, qkv, qkv, qkv, mix, logsum, mix_grad)


ROWS = 256
CHUNK = 512


def row_tiles(count):
    return [slice(row, row + ROWS) for row in range(0, count, ROWS)]


def whole(shape):
    return pl.BlockSpec(shape, lambda k: (0,) * len(shape))


def by_cols(rows):
    return pl.BlockSpec((rows, CHUNK), lambda k: (0, k))


def ffn_kernel(
    middle_ref, gain_ref, gate_w_ref, up_w_ref, down_w_ref,
    out_ref, normed_t_ref, gate_ref, up_ref, hidden_ref, normed_ref,
):
    tiles = row_tiles(middle_ref.shape[1])

    @pl.when(pl.program_id(0) == 0)
    def _():
        for cols in tiles:
            middle = middle_ref[:, cols]
            inverse = lax.rsqrt(jnp.mean(middle * middle, axis=0, keepdims=True) + EPSILON)
            normed = (middle * inverse * gain_ref[...]).astype(BF16)
            normed_t_ref[:, cols] = normed
            normed_ref[cols, :] = normed.T
            out_ref[:, cols] = middle

    for rows in tiles:
        normed = normed_ref[rows, :]
        gate = dot(normed, gate_w_ref[...], (1, 0))
        up = dot(normed, up_w_ref[...], (1, 0))
        gate_ref[rows, :] = gate.astype(BF16)
        up_ref[rows, :] = up.astype(BF16)
        hidden = (gate * jax.nn.sigmoid(gate) * up).astype(BF16)
        hidden_ref[rows, :] = hidden
    out_ref[...] += dot(down_w_ref[...], hidden_ref[...], (1, 1))


def ffn(middle, gain, w_gate, w_up, w_down_t):
    width, length = middle.shape
    hidden = w_gate.shape[1]
    return pl.pallas_call(
        ffn_kernel,
        grid=(hidden // CHUNK,),
        in_specs=[whole((width, length)), whole((width, 1)), by_cols(width), by_cols(width), by_cols(width)],
        out_specs=[whole((width, length)), whole((width, length)), by_cols(length), by_cols(length), by_cols(length)],
        out_shape=[
            jax.ShapeDtypeStruct((width, length), F32),
            HBM((width, length), BF16),
            HBM((length, hidden), BF16),
            HBM((length, hidden), BF16),
            HBM((length, hidden), BF16),
        ],
        scratch_shapes=[pltpu.VMEM((length, width), BF16)],
        compiler_params=pltpu.CompilerParams(vmem_limit_bytes=FFN_GRANT),
        cost_estimate=pl.CostEstimate(
            flops=6 * length * width * hidden, bytes_accessed=40_000_000, transcendentals=length * hidden
        ),
        name="ffn",
    )(middle, gain, w_gate, w_up, w_down_t)


def ffn_up_kernel(
    middle_ref, gain_ref, gate_w_ref, up_w_ref, normed_t_ref, gate_ref, up_ref, hidden_ref, normed_ref,
):
    tiles = row_tiles(middle_ref.shape[1])

    @pl.when(pl.program_id(0) == 0)
    def _():
        for cols in tiles:
            middle = middle_ref[:, cols]
            inverse = lax.rsqrt(jnp.mean(middle * middle, axis=0, keepdims=True) + EPSILON)
            normed = (middle * inverse * gain_ref[...]).astype(BF16)
            normed_t_ref[:, cols] = normed
            normed_ref[cols, :] = normed.T

    for rows in tiles:
        normed = normed_ref[rows, :]
        gate = dot(normed, gate_w_ref[...], (1, 0))
        up = dot(normed, up_w_ref[...], (1, 0))
        gate_ref[rows, :] = gate.astype(BF16)
        up_ref[rows, :] = up.astype(BF16)
        hidden_ref[rows, :] = (gate * jax.nn.sigmoid(gate) * up).astype(BF16)


def ffn_up(middle, gain, w_gate, w_up):
    width, length = middle.shape
    hidden = w_gate.shape[1]
    return pl.pallas_call(
        ffn_up_kernel,
        grid=(hidden // CHUNK,),
        in_specs=[whole((width, length)), whole((width, 1)), by_cols(width), by_cols(width)],
        out_specs=[whole((width, length)), by_cols(length), by_cols(length), by_cols(length)],
        out_shape=[HBM((width, length), BF16)] + [HBM((length, hidden), BF16)] * 3,
        scratch_shapes=[pltpu.VMEM((length, width), BF16)],
        compiler_params=pltpu.CompilerParams(vmem_limit_bytes=FFN_GRANT),
        cost_estimate=pl.CostEstimate(
            flops=4 * length * width * hidden, bytes_accessed=30_000_000, transcendentals=length * hidden
        ),
        name="ffn_up",
    )(middle, gain, w_gate, w_up)


def ffn_back_kernel(
    grad_ref, middle_ref, gain_ref, gate_ref, up_ref, gate_w_ref, up_w_ref, down_w_ref,
    out_ref, out_narrow_ref, gate_grad_ref, up_grad_ref, gain_grad_ref, branch_t_ref, total_ref, branch_ref,
):
    step = pl.program_id(0)
    tiles = row_tiles(middle_ref.shape[1])

    @pl.when(step == 0)
    def _():
        for cols in tiles:
            branch = grad_ref[:, cols].astype(BF16)
            branch_t_ref[:, cols] = branch
            branch_ref[cols, :] = branch.T

    for rows in tiles:
        hidden_grad = dot(branch_ref[rows, :], down_w_ref[...], (1, 0))
        gate = gate_ref[rows, :].astype(F32)
        up = up_ref[rows, :].astype(F32)
        sigmoid = jax.nn.sigmoid(gate)
        scaled = hidden_grad * sigmoid
        up_grad = (scaled * gate).astype(BF16)
        gate_grad = (scaled * up * (1.0 + gate * (1.0 - sigmoid))).astype(BF16)
        gate_grad_ref[rows, :] = gate_grad
        up_grad_ref[rows, :] = up_grad
    part = dot(gate_w_ref[...], gate_grad_ref[...], (1, 1)) + dot(up_w_ref[...], up_grad_ref[...], (1, 1))

    @pl.when(step == 0)
    def _():
        total_ref[...] = part

    @pl.when(step > 0)
    def _():
        total_ref[...] += part

    @pl.when(step == pl.num_programs(0) - 1)
    def _():
        gain_grad = jnp.zeros(gain_ref.shape, F32)
        for cols in tiles:
            middle = middle_ref[:, cols]
            normed_grad = total_ref[:, cols]
            inverse = lax.rsqrt(jnp.mean(middle * middle, axis=0, keepdims=True) + EPSILON)
            unit = middle * inverse
            gain_grad += jnp.sum(normed_grad * unit, axis=1, keepdims=True)
            scaled = gain_ref[...] * normed_grad
            inner = jnp.mean(scaled * unit, axis=0, keepdims=True)
            out = grad_ref[:, cols] + inverse * (scaled - unit * inner)
            out_ref[:, cols] = out
            out_narrow_ref[:, cols] = out.astype(BF16)
        gain_grad_ref[...] = gain_grad


def ffn_back(grad, middle, gain, gate, up, w_gate, w_up, w_down_t):
    width, length = middle.shape
    hidden = w_gate.shape[1]
    full = whole((width, length))
    return pl.pallas_call(
        ffn_back_kernel,
        grid=(hidden // CHUNK,),
        in_specs=[
            full, full, whole((width, 1)), by_cols(length), by_cols(length), by_cols(width), by_cols(width), by_cols(width),
        ],
        out_specs=[full, full, by_cols(length), by_cols(length), whole((width, 1)), full],
        out_shape=[
            HBM((width, length), F32),
            jax.ShapeDtypeStruct((width, length), BF16),
            HBM((length, hidden), BF16),
            HBM((length, hidden), BF16),
            jax.ShapeDtypeStruct((width, 1), F32),
            HBM((width, length), BF16),
        ],
        scratch_shapes=[pltpu.VMEM((width, length), F32), pltpu.VMEM((length, width), BF16)],
        compiler_params=pltpu.CompilerParams(vmem_limit_bytes=BACK_GRANT),
        cost_estimate=pl.CostEstimate(
            flops=6 * length * width * hidden, bytes_accessed=50_000_000, transcendentals=length * hidden
        ),
        name="ffn_back",
    )(grad, middle, gain, gate, up, w_gate, w_up, w_down_t)


def weight_grad_kernel(left_fsdp, transposed, places_ref, left_ref, right_ref, left2_ref, right2_ref, keep_ref, send_ref):
    step = pl.program_id(0)
    contract = (1, 1) if transposed else (1, 0)
    total = dot(left_ref[...], right_ref[...], contract) + dot(left2_ref[...], right2_ref[...], contract)
    total = total.astype(BF16)
    half = total.shape[0] // 2
    fsdp, core = places_ref[0], places_ref[1]
    if left_fsdp:
        for out_ref, here in ((keep_ref, step < 2), (send_ref, step >= 2)):

            @pl.when(here)
            def _():
                out_ref[fsdp] = total[:half]
                out_ref[1 - fsdp] = total[half:]

    else:
        for out_ref, first in ((keep_ref, core), (send_ref, 1 - core)):

            @pl.when(first == 0)
            def _():
                out_ref[0] = total[:half]

            @pl.when(first == 1)
            def _():
                out_ref[0] = total[half:]


def weight_grad(places, products, more_products, left_fsdp):
    left, right = products
    left2, right2 = more_products
    rows, length = left.shape
    cols = right.shape[1]
    block = cols // 4
    left_spec = pl.BlockSpec((rows, length), lambda j, places: (0, 0))
    if left_fsdp:
        right_spec = pl.BlockSpec((length, block), lambda j, places: (0, (2 * places[1] + j) % 4))
        keep_spec = pl.BlockSpec((2, rows // 2, block), lambda j, places: (0, 0, jnp.minimum(j, 1)))
        send_spec = pl.BlockSpec((2, rows // 2, block), lambda j, places: (0, 0, jnp.maximum(j - 2, 0)))
    else:
        right_spec = pl.BlockSpec((length, block), lambda j, places: (0, (2 * places[0] + j) % 4))
        keep_spec = pl.BlockSpec((1, rows // 2, block), lambda j, places: (j // 2, 0, j % 2))
        send_spec = keep_spec
    return pl.pallas_call(
        partial(weight_grad_kernel, left_fsdp, False),
        grid_spec=pltpu.PrefetchScalarGridSpec(
            num_scalar_prefetch=1,
            grid=(4,),
            in_specs=[left_spec, right_spec, left_spec, right_spec],
            out_specs=[keep_spec, send_spec],
        ),
        out_shape=[jax.ShapeDtypeStruct((2, rows // 2, cols // 2), BF16)] * 2,
        compiler_params=pltpu.CompilerParams(vmem_limit_bytes=GRAD_GRANT),
        cost_estimate=pl.CostEstimate(
            flops=4 * rows * length * cols, bytes_accessed=10 * rows * cols, transcendentals=0
        ),
        name="weight_grad",
    )(places, left, right, left2, right2)


def mixed_grad_kernel(
    places_ref, mix_ref, branch_ref, normed_ref, qkv_ref, mix2_ref, branch2_ref, normed2_ref, qkv2_ref,
    keep_ref, send_ref,
):
    width = branch_ref.shape[0]
    half_cols = keep_ref.shape[2]
    out_part = dot(mix_ref[...], branch_ref[...], (1, 1)) + dot(mix2_ref[...], branch2_ref[...], (1, 1))
    qkv_part = dot(normed_ref[...], qkv_ref[...], (1, 1)) + dot(normed2_ref[...], qkv2_ref[...], (1, 1))
    out_part = out_part.astype(BF16)
    qkv_part = qkv_part.astype(BF16)
    first = half_cols - width
    core = places_ref[1]
    for low_ref, high_ref, here in ((keep_ref, send_ref, core == 0), (send_ref, keep_ref, core == 1)):

        @pl.when(here)
        def _():
            low_ref[0, :, :width] = out_part
            low_ref[0, :, width:] = qkv_part[:, :first]
            high_ref[0] = qkv_part[:, first:]


def mixed_grad(places, products, more_products):
    (mix, branch), (normed, qkv) = products
    (mix2, branch2), (normed2, qkv2) = more_products
    rows, length = mix.shape
    cols = branch.shape[0] + qkv.shape[0]
    left = pl.BlockSpec((rows // 2, length), lambda j, places: ((places[0] + j) % 2, 0))
    fixed = lambda shape: pl.BlockSpec(shape, lambda j, places: (0, 0))
    specs = [left, fixed(branch.shape), left, fixed(qkv.shape)]
    return pl.pallas_call(
        mixed_grad_kernel,
        grid_spec=pltpu.PrefetchScalarGridSpec(
            num_scalar_prefetch=1,
            grid=(2,),
            in_specs=specs + specs,
            out_specs=[pl.BlockSpec((1, rows // 2, cols // 2), lambda j, places: (j, 0, 0))] * 2,
        ),
        out_shape=[jax.ShapeDtypeStruct((2, rows // 2, cols // 2), BF16)] * 2,
        compiler_params=pltpu.CompilerParams(vmem_limit_bytes=MIXED_GRANT),
        cost_estimate=pl.CostEstimate(
            flops=4 * rows * length * cols, bytes_accessed=10 * rows * cols, transcendentals=0
        ),
        name="mixed_grad",
    )(places, mix, branch, normed, qkv, mix2, branch2, normed2, qkv2)


def assemble_kernel(stack_cores, cuts, places_ref, *refs):
    core, side = places_ref[1], places_ref[2]
    inputs, outputs = refs[:4], refs[4:]
    count, cols = inputs[0].shape
    whole_ref = outputs[-1]
    for k, piece_ref in enumerate(inputs):
        at_side = jnp.bitwise_xor(side, k % 2)
        at_core = jnp.bitwise_xor(core, k // 2)
        row = at_side * count + (at_core * (2 * count) if stack_cores else 0)
        rows = pl.ds(pl.multiple_of(row, 8), count)
        value = piece_ref[...].astype(F32)
        if stack_cores:
            whole_ref[rows, :] = value
        else:
            whole_ref[rows, pl.ds(pl.multiple_of(at_core * cols, 128), cols)] = value
    for out_ref, (low, high) in zip(outputs[:-1], cuts):
        out_ref[...] = whole_ref[:, low:high]


def assemble(places, pieces, stack_cores, cuts=()):
    count, cols = pieces[0].shape
    shape = (4 * count, cols) if stack_cores else (2 * count, 2 * cols)
    out_shape = [jax.ShapeDtypeStruct((shape[0], high - low), F32) for low, high in cuts]
    out_shape = out_shape or [jax.ShapeDtypeStruct(shape, F32)]
    return pl.pallas_call(
        partial(assemble_kernel, stack_cores, cuts),
        grid_spec=pltpu.PrefetchScalarGridSpec(
            num_scalar_prefetch=1,
            grid=(1,),
            in_specs=[pl.BlockSpec((count, cols), lambda j, places: (0, 0))] * 4,
            out_specs=[pl.BlockSpec(out.shape, lambda j, places: (0, 0)) for out in out_shape],
            scratch_shapes=[pltpu.VMEM(shape, F32)] if cuts else [],
        ),
        out_shape=out_shape,
        compiler_params=pltpu.CompilerParams(vmem_limit_bytes=24 << 20),
        cost_estimate=pl.CostEstimate(flops=0, bytes_accessed=24 * count * cols, transcendentals=0),
        name="assemble",
    )(places, *pieces)


def doc_tables(doc_row):
    token_index = jnp.arange(doc_row.shape[0])
    start = jnp.sum((doc_row[:, None] < doc_row[None, :]).astype(jnp.int32), axis=0)
    places = (token_index - start).astype(F32)
    frequency = ROPE_BASE ** (-2.0 * jnp.arange(HALF, dtype=F32) / HEAD_SIZE)
    angles = frequency[:, None] * places[None, :]
    return (start[None, :], jnp.cos(angles), jnp.sin(angles))


def norm_forward(inputs, gain):
    inverse = lax.rsqrt(jnp.mean(inputs * inputs, axis=0, keepdims=True) + EPSILON)
    return (inputs * inverse * gain).astype(BF16)


def norm_backward(inputs, gain, grad):
    inverse = lax.rsqrt(jnp.mean(inputs * inputs, axis=0, keepdims=True) + EPSILON)
    scaled = gain * grad
    inner = jnp.mean(scaled * inputs, axis=0, keepdims=True)
    return (inverse * scaled - inputs * inverse**3 * inner, jnp.sum(grad * inputs * inverse, axis=1, keepdims=True))


def project(inputs, w_qkv, gains, tables):
    _, cosine, sine = tables
    length = inputs.shape[1]
    normed = norm_forward(inputs, gains[0])
    raw = dot(w_qkv, normed, (0, 0))
    heads = QUERY_HEADS + KEY_VALUE_HEADS
    pairs = raw[: heads * HEAD_SIZE].reshape(heads, 2, HALF, length)
    first, second = pairs[:, 0], pairs[:, 1]
    rotated = jnp.stack([first * cosine - second * sine, second * cosine + first * sine], axis=1)
    qkv = jnp.concatenate(
        [rotated.reshape(heads * HEAD_SIZE, length).astype(BF16), raw[heads * HEAD_SIZE :].astype(BF16)], axis=0
    )
    return (normed, qkv)


def project_out(inputs, w_out, mix):
    return inputs + dot(w_out, mix, (0, 0))


def attention_backward(kept, attn_grad, weights, tables):
    start, cosine, sine = tables
    _, _, qkv, logsum, mix = kept
    mix_grad = dot(weights[1], attn_grad, (1, 0)).astype(BF16)
    return attention_back(start, cosine, sine, qkv, mix, logsum, mix_grad)


def input_backward(kept, middle_grad, qkv_grad, weights, gains):
    normed_grad = dot(weights[0], qkv_grad, (1, 0))
    inputs_grad, gain_grad = norm_backward(kept[0], gains[0], normed_grad)
    return (inputs_grad + middle_grad, gain_grad)


def after(value, *earlier):
    return lax.optimization_barrier((value,) + earlier)[0]


def swap_fsdp(value):
    return lax.ppermute(value, "fsdp", [(0, 1), (1, 0)])


def swap_dp(value, bit, size=16):
    return lax.ppermute(value, "dp", [(i, i ^ bit) for i in range(size)])


def fetch(parts, axis, index, pieces):
    sent = [cut_piece(part, index, axis, pieces) for part in parts]
    sent = jnp.concatenate(sent, axis=1) if len(sent) > 1 else sent[0]
    return sent


def cut_piece(value, index, axis, pieces):
    count = value.shape[axis] // pieces
    return lax.dynamic_slice_in_dim(value, index * count, count, axis)


def join_kernel(own_count, shard_axis, piece_axis, index_at, places_ref, *refs):
    own, pieces, out_ref = refs[:own_count], refs[own_count:-1], refs[-1]
    rows, cols = out_ref.shape
    fsdp = places_ref[0]
    index = places_ref[index_at]
    if shard_axis == 0:
        half = pl.ds(pl.multiple_of(fsdp * (rows // 2), 16), rows // 2)
        at = 0
        for ref in own:
            out_ref[half, at : at + ref.shape[1]] = ref[...]
            at += ref.shape[1]
    else:
        out_ref[:, pl.ds(pl.multiple_of(fsdp * (cols // 2), 128), cols // 2)] = own[0][...]
    for flip, ref in enumerate(pieces):
        at = jnp.bitwise_xor(index, flip)
        count, width = ref.shape
        row = at * count if piece_axis == 0 else 0
        col = at * width if piece_axis == 1 else 0
        if shard_axis == 0:
            row = row + (1 - fsdp) * (rows // 2)
        else:
            col = col + (1 - fsdp) * (cols // 2)
        row_at = pl.ds(pl.multiple_of(row, 16), count)
        if shard_axis == 0 and piece_axis == 0:
            out_ref[row_at, :] = ref[...]
        else:
            out_ref[row_at, pl.ds(pl.multiple_of(col, 128), width)] = ref[...]


def join(places, own, pieces, shard_axis, piece_axis, index_at):
    rows, cols = own[0].shape[0], sum(part.shape[1] for part in own)
    shape = (2 * rows, cols) if shard_axis == 0 else (rows, 2 * cols)
    full = lambda shape: pl.BlockSpec(shape, lambda j, places: (0, 0))
    return pl.pallas_call(
        partial(join_kernel, len(own), shard_axis, piece_axis, index_at),
        grid_spec=pltpu.PrefetchScalarGridSpec(
            num_scalar_prefetch=1,
            grid=(1,),
            in_specs=[full(part.shape) for part in (*own, *pieces)],
            out_specs=full(shape),
        ),
        out_shape=jax.ShapeDtypeStruct(shape, BF16),
        compiler_params=pltpu.CompilerParams(vmem_limit_bytes=24 << 20),
        cost_estimate=pl.CostEstimate(flops=0, bytes_accessed=4 * shape[0] * shape[1], transcendentals=0),
        name="join",
    )(places, *own, *pieces)


def add(left, right):
    return (left.astype(F32) + right.astype(F32)).astype(BF16)


def add3(first, second, third):
    return ((first.astype(F32) + second.astype(F32)) + third.astype(F32)).astype(BF16)


def reduce_vector(values):
    total = values
    for bit in (1, 2, 4, 8):
        total = add(total, swap_dp(total, bit))
    total = add(total, swap_fsdp(total))
    count = values.shape[1] // 2
    return lax.dynamic_slice_in_dim(total, lax.axis_index("fsdp") * count, count, 1)


def gather_gains(gains):
    other = swap_fsdp(gains)
    first = lax.axis_index("fsdp") == 0
    return jnp.concatenate([jnp.where(first, gains, other), jnp.where(first, other, gains)], axis=1)


def cut(value, which, axis):
    count = value.shape[axis] // 2
    return lax.dynamic_slice_in_dim(value, which * count, count, axis)


class Reduction:
    def __init__(self, halves):
        self.keep, send = halves
        self.received = swap_dp(send, 1)
        place = lax.axis_index("dp")
        self.side, self.lane = (place // 2) % 2, (place // 4) % 2
        self.stage = 0

    def step(self, queue):
        gate = lambda value: after(value, *queue)
        self.stage += 1
        if self.stage == 1:
            mine = add(gate(self.keep)[1], self.received[1])
            self.incoming = swap_fsdp(mine)
        elif self.stage == 2:
            half = add3(gate(self.keep)[0], self.received[0], self.incoming)
            mine, self.own = cut(half, 1 - self.side, 0), cut(half, self.side, 0)
            self.incoming = swap_dp(mine, 2)
        elif self.stage == 3:
            part = add(gate(self.own), self.incoming)
            mine, self.own = cut(part, 1 - self.lane, 1), cut(part, self.lane, 1)
            self.incoming = swap_dp(mine, 4)
        elif self.stage in (4, 5):
            mine = self.own = add(gate(self.own), self.incoming)
            self.incoming = swap_dp(mine, 8 if self.stage == 4 else 4)
        elif self.stage == 6:
            own = gate(self.own)
            low = jnp.where(self.lane == 0, own, self.incoming)
            high = jnp.where(self.lane == 0, self.incoming, own)
            mine = self.own = jnp.concatenate([low, high], axis=1)
            self.across = swap_dp(mine, 2)
            self.beside = swap_dp(mine, 1)
        else:
            mine = gate(self.across)
            self.pieces = (self.own, mine, self.beside, swap_dp(mine, 1))
        queue[:] = [mine]
        return mine


def make_body(fsdp_size, dp_size):
    paired = fsdp_size == 2 and dp_size == 16

    def body(
        activations, doc_ids, w_query, key_projection, value_projection, w_out,
        gain_attn, gain_ffn, w_gate, w_up, w_down, cotangent,
    ):
        if paired:
            place = lax.axis_index("dp")
            core, side, lane = place % 2, (place // 2) % 2, (place // 4) % 2
            index_y, index_z = place % 4, core + 2 * lane
            places = jnp.stack([lax.axis_index("fsdp"), core, side, index_y, index_z]).astype(jnp.int32)
            qkv_own = (w_query, key_projection, value_projection)
            qkv_sent = fetch(qkv_own, 0, core, 2)
            out_sent = fetch((after(w_out, qkv_sent),), 0, core, 2)
            gate_sent = fetch((after(w_gate, out_sent),), 1, index_y, 4)
            up_sent = fetch((after(w_up, gate_sent),), 1, index_z, 4)
            down_sent = fetch((after(w_down.T, up_sent),), 0, index_y, 4)
            qkv_mine = swap_fsdp(qkv_sent)
            gains = gather_gains(after(jnp.stack([gain_attn, gain_ffn]), qkv_sent)).astype(F32)
            out_mine, gate_mine, up_mine, down_mine = [
                swap_fsdp(sent) for sent in (out_sent, gate_sent, up_sent, down_sent)
            ]
            w_qkv = join(places, qkv_own, (qkv_mine, swap_dp(qkv_mine, 1)), 0, 0, 1)
        else:
            collect = lambda shard, axis: lax.all_gather(shard, "fsdp", axis=axis, tiled=True)
            gains = collect(jnp.stack([gain_attn, gain_ffn]), 1).astype(F32)
            places = jnp.zeros((4,), jnp.int32)
            qkv_shard = jnp.concatenate([w_query, key_projection, value_projection], axis=1)
            weights = (
                collect(qkv_shard, 0), collect(w_out, 0), collect(w_gate, 0), collect(w_up, 0), collect(w_down, 0).T,
            )
        gains = (gains[0][:, None], gains[1][:, None])
        tables = doc_tables(doc_ids[0])
        start, cosine, sine = tables
        inputs = activations[0].T.astype(F32)

        if paired:
            normed, qkv = project(inputs, w_qkv, gains, tables)
            out_mine = after(out_mine, qkv)
            gate_mine = after(gate_mine, out_mine)
            out_beside = swap_dp(out_mine, 1)
            gate_across, gate_beside = swap_dp(gate_mine, 2), swap_dp(gate_mine, 1)
            mix, logsum = attention(start, qkv)
            up_mine = after(up_mine, mix)
            up_across, up_beside = swap_dp(up_mine, 4), swap_dp(up_mine, 1)
            gate_across = after(gate_across, up_mine)
            gate_corner = swap_dp(gate_across, 1)
            w_out_full = join(places, (w_out,), (out_mine, out_beside), 0, 0, 1)
            middle = project_out(inputs, w_out_full, mix)
            down_mine = after(down_mine, middle)
            down_across, down_beside = swap_dp(down_mine, 2), swap_dp(down_mine, 1)
            gate_pieces = (after(gate_mine, down_mine), gate_beside, gate_across, gate_corner)
            w_gate_full = join(places, (w_gate,), gate_pieces, 0, 1, 3)
            up_across = after(up_across, w_gate_full)
            w_up_full = join(places, (w_up,), (up_mine, up_beside, up_across, swap_dp(up_across, 1)), 0, 1, 4)
            first_normed, first_gate, first_up, first_hidden = ffn_up(middle, gains[1], w_gate_full, w_up_full)
            down_across = after(down_across, first_hidden)
            w_down_full = join(
                places, (w_down.T,), (down_mine, down_beside, down_across, swap_dp(down_across, 1)), 1, 0, 3
            )
            weights = (w_qkv, w_out_full, w_gate_full, w_up_full, w_down_full)
            ffn_weights = weights[2:]
        else:
            ffn_weights = weights[2:]
            normed, qkv = project(inputs, weights[0], gains, tables)
            mix, logsum = attention(start, qkv)
            middle = project_out(inputs, weights[1], mix)
            first_normed, first_gate, first_up, first_hidden = ffn_up(middle, gains[1], *ffn_weights[:2])
        first = (inputs, normed, qkv, logsum, mix)
        inputs2 = middle + dot(ffn_weights[2], first_hidden, (1, 1))
        normed2, qkv2 = project(inputs2, weights[0], gains, tables)
        mix2, logsum2 = attention(start, qkv2)
        middle2 = project_out(inputs2, weights[1], mix2)
        second = (inputs2, normed2, qkv2, logsum2, mix2)
        outputs, second_normed, second_gate, second_up, second_hidden = ffn(middle2, gains[1], *ffn_weights)

        grad = cotangent[0].T.astype(F32)
        grad, attn_grad2, gate_grad2, up_grad2, ffn_gain2, branch2 = ffn_back(
            grad, middle2, gains[1], second_gate, second_up, *ffn_weights
        )
        qkv_grad2 = attention_backward(second, attn_grad2, weights, tables)
        grad, attn_gain2 = input_backward(second, grad, qkv_grad2, weights, gains)

        down_halves = weight_grad(
            places, (branch2, second_hidden), (grad.astype(BF16), first_hidden), False
        )
        queue = []
        if paired:
            down = Reduction(down_halves)
            grad = after(grad, down.step(queue))
        else:
            grad = after(grad, *down_halves)
        grad, attn_grad, gate_grad, up_grad, ffn_gain, _ = ffn_back(
            grad, middle, gains[1], first_gate, first_up, *ffn_weights
        )
        if paired:
            down.step(queue)
            gate_grad = after(gate_grad, *queue)
        gate_halves = weight_grad(places, (second_normed, gate_grad2), (first_normed, gate_grad), True)
        mix_grad_in = after(attn_grad, *gate_halves)
        mix_grad = dot(weights[1], mix_grad_in, (1, 0)).astype(BF16)
        if paired:
            gate = Reduction(gate_halves)
            queue.append(mix_grad)
            gate.step(queue)
            up_grad = after(up_grad, *queue)
        up_halves = weight_grad(places, (second_normed, up_grad2), (first_normed, up_grad), True)
        if paired:
            queue.append(up_halves[0])
            up = Reduction(up_halves)
            down.step(queue)
            up.step(queue)
            mix_grad = after(mix_grad, *queue)
        qkv_grad = attention_back(start, cosine, sine, first[2], first[4], first[3], mix_grad)
        if paired:
            queue.append(qkv_grad)
            down.step(queue)
            gate.step(queue)
            qkv_grad = after(qkv_grad, *queue)
        mixed_halves = mixed_grad(
            places,
            ((second[4], attn_grad2), (second[1], qkv_grad2)),
            ((first[4], attn_grad), (first[1], qkv_grad)),
        )
        if paired:
            mixed = Reduction(mixed_halves)
            queue.append(mixed_halves[0])
            down.step(queue)
            gate.step(queue)
            up.step(queue)
            mixed.step(queue)
            grad = after(grad, *queue)
        grad, attn_gain = input_backward(first, grad, after(qkv_grad, *mixed_halves), weights, gains)
        gain_grads = jnp.concatenate([attn_gain + attn_gain2, ffn_gain + ffn_gain2], axis=1).T.astype(BF16)

        width = w_query.shape[1]
        key_end = width + key_projection.shape[1]
        value_end = key_end + value_projection.shape[1]
        cuts = ((0, width), (width, 2 * width), (2 * width, width + key_end), (width + key_end, width + value_end))
        if paired:
            queue.append(grad)
            for reduction in (
                down, gate, up, down, gate, up, mixed, gate, up, mixed, gate, up, mixed, mixed, up, mixed, mixed,
            ):
                reduction.step(queue)
            (grad_down,) = assemble(places, down.pieces, True)
            (grad_gate,) = assemble(places, gate.pieces, False)
            (grad_up,) = assemble(places, up.pieces, False)
            grad_out, grad_query, grad_key, grad_value = assemble(places, mixed.pieces, False, cuts)
            gain_grads = reduce_vector(gain_grads).astype(F32)
        else:

            def reduce(value, axis):
                part = lax.psum_scatter(value, "fsdp", scatter_dimension=axis, tiled=True)
                return lax.psum(part, "dp").astype(F32)

            rows = lambda halves: jnp.concatenate([h.reshape(-1, h.shape[2]) for h in halves], axis=1)
            cols = lambda halves: jnp.concatenate([jnp.concatenate([h[0], h[1]], axis=1) for h in halves])
            grad_down = reduce(cols(down_halves).T, 0).T
            grad_gate = reduce(rows(gate_halves), 0)
            grad_up = reduce(rows(up_halves), 0)
            mixed = reduce(rows(mixed_halves), 0)
            grad_out, grad_query, grad_key, grad_value = [mixed[:, low:high] for low, high in cuts]
            gain_grads = reduce(gain_grads, 1)
        return (
            outputs.T.astype(BF16)[None],
            grad.T.astype(BF16)[None],
            grad_query,
            grad_key,
            grad_value,
            grad_out,
            gain_grads[0],
            gain_grads[1],
            grad_gate,
            grad_up,
            grad_down.T,
        )

    return body


def solution(mesh):
    sequences = P(("dp", "fsdp"), None, None)
    rows = P("fsdp", None)
    vector = P("fsdp")
    in_specs = (
        sequences, P(("dp", "fsdp"), None), rows, rows, rows, rows, vector, vector, rows, rows, rows, sequences,
    )
    out_specs = (sequences, sequences, rows, rows, rows, rows, vector, vector, rows, rows, rows)
    body = make_body(mesh.shape["fsdp"], mesh.shape["dp"])
    return jax.shard_map(body, mesh=mesh, in_specs=in_specs, out_specs=out_specs, check_vma=False)
```

time: 788 us -> 488 us (0.62)
  matrix products: 188 us -> 29.7 us
  local copies, waits for them, and re-layouts: 200 us -> 44.9 us
  Pallas kernels: 52.2 us -> 205 us
  waiting for transfers between devices: 216 us -> 125 us
  starting transfers between devices: 67.3 us -> 43.4 us
  other arithmetic: 46.3 us -> 29.5 us
    dot_general x30 -> x9, matrix products: 188 us -> 29.7 us  [dot(): lax.dot_general(left, right, ((contract[:1], contract[1:]), ((), ())), pr...]
    pallas_call x0 -> x17, Pallas kernels: none -> 154 us  [the longest x2 49.3 us: ffn_back(): pl.pallas_call(ffn_back_kernel, grid=(hidden // CHUNK,), in_specs=[full,...]
    dynamic_update_slice x27 -> x0, local copies, waits for them, and re-layouts: 108 us -> none  [the longest x1 44.3 us: reduce_rows(): lax.dynamic_update_slice_in_dim(whole, beside.astype(F32)[None], 1 - core...]
    ppermute x12 -> x11, waiting for transfers between devices: 69.3 us -> 22.3 us  [swap_fsdp(): return lax.ppermute(value, 'fsdp', [(0, 1), (1, 0)])]
    ppermute x49 -> x47, waiting for transfers between devices: 147 us -> 103 us  [swap_dp(): return lax.ppermute(value, 'dp', [(i, i ^ bit) for i in range(size)])]
    ppermute x49 -> x47, starting transfers between devices: 52.3 us -> 29.9 us  [swap_dp(): return lax.ppermute(value, 'dp', [(i, i ^ bit) for i in range(size)])]
    reshape x2 -> x0, local copies, waits for them, and re-layouts: 12.4 us -> none  [the longest x1 11 us: reduce_rows(): parts = grad.reshape(2, 2, count // 2, width)]
    broadcast_in_dim x8 -> x0, local copies, waits for them, and re-layouts: 11.2 us -> none  [the longest x3 4.75 us: gather_rows(): whole = jnp.zeros((2 * count,) + shard.shape[1:], shard.dtype)]
  transfers between devices with their start and end apart: 61 -> 58, of which waited for: 22 -> 24; matrix products, arithmetic and copies ran while one was open for 35% -> 9% of each run, Pallas kernels for 1% -> 20%
where the time goes in v2:
time: 488 us; the launch traced here: 480 us
  Pallas kernels  205 us (42%)
  waiting for transfers between devices  125 us (26%)
  local copies, waits for them, and re-layouts  44.9 us (9%)
  starting transfers between devices  43.4 us (9%)
  matrix products  29.7 us (6%)
  other arithmetic  29.5 us (6%)
    ppermute x47, waiting for transfers between devices, swap_dp(): return lax.ppermute(value, 'dp', [(i, i ^ bit) for i in range(size)])  103 us
    pallas_call x2, Pallas kernels, ffn_back(): pl.pallas_call(ffn_back_kernel, grid=(hidden // CHUNK,), in_specs=[full,...  49.3 us
    pallas_call x3, Pallas kernels, weight_grad(): pl.pallas_call(partial(weight_grad_kernel, left_fsdp, False), grid_spec=p...  37.7 us
    unnamed x182, local copies, waits for them, and re-layouts  30.2 us
    ppermute x47, starting transfers between devices, swap_dp(): return lax.ppermute(value, 'dp', [(i, i ^ bit) for i in range(size)])  29.9 us
    dot_general x9, matrix products, dot(): lax.dot_general(left, right, ((contract[:1], contract[1:]), ((), ())), pr...  29.7 us
    pallas_call x2, Pallas kernels, attention_back(): pl.pallas_call(attention_back_kernel, grid=(KEY_VALUE_HEADS,), in_specs=[...  28.7 us
    pallas_call x2, Pallas kernels, attention(): pl.pallas_call(attention_kernel, grid=(KEY_VALUE_HEADS,), in_specs=[pl.Bl...  22.8 us
  transfers between devices with their start and end apart: 58, of which 24 were waited for; matrix products, arithmetic and copies ran while one was open for 9% of the time, Pallas kernels for 20%

profile of v2, /device:TPU:0, one launch (start us, length us, event | category | flops | bytes accessed | tf_op | source)
XLA Modules:
  0.0 480.3 jit_solution(2418613078585727420)
XLA Ops:
  22.9 6.9 %collective-permute-done.1.refs_3_ = bf16[240,1600]{1,0:T(8,128)(2,1)} collective-permute-done((bf16[240,1600]{1,0:T(8,128)(2,1)}, bf16[240,1600]{1,0:T(8,128)(2,1)}, u32[]{:S(2)}, u32[]{:S(2)}) %collective-permute-start.1) | collective-permute-done | bytes 768032 | tf_op jit(solution)/shard_map/ppermute | solution.py:577
  29.8 10.5 %collective-permute-done.3 = bf16[2,480]{1,0:T(2,128)(2,1)S(1)} collective-permute-done((bf16[2,480]{1,0:T(2,128)(2,1)S(1)}, bf16[2,480]{1,0:T(2,128)(2,1)S(1)}, u32[]{:S(2)}, u32[]{:S(2)}) %collective-permute-start.3) | collective-permute-done | bytes 1952 | tf_op jit(solution)/shard_map/ppermute | solution.py:577
  58.8 11.5 %attention.2 = (bf16[960,768]{1,0:T(8,128)(2,1)S(1)}, f32[5,8,768]{2,1,0:T(8,128)S(1)}) custom-call(s32[1,768]{1,0:T(1,128)S(1)} %reduce_sum.75.start_ref, bf16[1600,768]{1,0:T(8,128)(2,1)S(1)} %pad_maximum_fusion.query_ref.key_ref.value_ref, bf16[1600,768]{1,0:T(8,128)(2,1)S(1)} %pad_maximum_fusion.query_ref.key_ref.value_ref, ...), custom_call_target="tpu_custom_call" | custom-call | flops 6000000000 | bytes 4000000 | tf_op jit(solution)/shard_map/attention/pallas_call | solution.py:80
  74.0 3.4 fusion.3.middle_ref
  83.2 3.9 collective-permute-done.14.refs_3_
  93.7 13.0 %ffn_up.1 = (bf16[960,768]{1,0:T(8,128)(2,1)}, bf16[768,2560]{1,0:T(8,128)(2,1)}, bf16[768,2560]{1,0:T(8,128)(2,1)}, bf16[768,2560]{1,0:T(8,128)(2,1)}) custom-call(f32[960,768]{1,0:T(8,128)S(1)} %copy-done.42, f32[960,1]{1,0:T(8,128)S(1)} %copy.55.gain_ref, bf16[960,2560]{1,0:T(8,128)(2,1)S(1)} %bitcast.117, bf16[960,2560]{1,0:T(8,128)(2,1)S(1)} %join.8.up_w_ref), custom_call_target="tpu_custom_call" | custom-call | flops 7549747200 | bytes 30000000 | tf_op jit(solution)/shard_map/ffn_up/pallas_call | solution.py:280
  109.7 7.9 %multiply_reduce_fusion.2 = (f32[768]{0:T(1024)S(1)}, f32[960,768]{1,0:T(8,128)S(1)}) fusion(f32[960,768]{1,0:T(8,128)S(1)} %copy-done.42, bf16[960,2560]{1,0:T(8,128)(2,1)S(1)} %join.9.down_w_ref, bf16[768,2560]{1,0:T(8,128)(2,1)} %get-tuple-element.108.right2_ref), kind=kOutput, calls=%fused_computation.21 | convolution fusion | flops 3777084672 | bytes 14748672 | tf_op jit(solution)/shard_map/dot_general | solution.py:31
  124.8 11.3 %attention.3 = (bf16[960,768]{1,0:T(8,128)(2,1)S(1)}, f32[5,8,768]{2,1,0:T(8,128)S(1)}) custom-call(s32[1,768]{1,0:T(1,128)S(1)} %reduce_sum.75.start_ref, bf16[1600,768]{1,0:T(8,128)(2,1)S(1)} %pad_maximum_fusion.1.query_ref.key_ref.value_ref, bf16[1600,768]{1,0:T(8,128)(2,1)S(1)} %pad_maximum_fusion.1.query_ref.key_ref.value_ref, ...), custom_call_target="tpu_custom_call" | custom-call | flops 6000000000 | bytes 4000000 | tf_op jit(solution)/shard_map/attention/pallas_call | solution.py:80
  138.7 16.3 %ffn.1 = (f32[960,768]{1,0:T(8,128)S(1)}, bf16[960,768]{1,0:T(8,128)(2,1)}, bf16[768,2560]{1,0:T(8,128)(2,1)}, bf16[768,2560]{1,0:T(8,128)(2,1)}, bf16[768,2560]{1,0:T(8,128)(2,1)}) custom-call(f32[960,768]{1,0:T(8,128)S(1)} %convolution_add_fusion.middle_ref, f32[960,1]{1,0:T(8,128)S(1)} %copy-done.40, bf16[960,2560]{1,0:T(8,128)(2,1)S(1)} %bitcast.117, ...), custom_call_target="tpu_custom_call" | custom-call | flops 11324620800 | bytes 40000000 | tf_op jit(solution)/shard_map/ffn/pallas_call | solution.py:233
  158.7 24.3 %ffn_back.2 = (f32[960,768]{1,0:T(8,128)}, bf16[960,768]{1,0:T(8,128)(2,1)S(1)}, bf16[768,2560]{1,0:T(8,128)(2,1)}, bf16[768,2560]{1,0:T(8,128)(2,1)}, f32[960,1]{1,0:T(8,128)S(1)}, /*index=5*/bf16[960,768]{1,0:T(8,128)(2,1)}) custom-call(f32[960,768]{1,0:T(8,128)S(1)} %convert_bitcast_fusion.grad_ref, f32[960,768]{1,0:T(8,128)S(1)} %convolution_add_fusion.middle_ref, ...), custom_call_target="tpu_custom_call" | custom-call | flops 11324620800 | bytes 50000000 | tf_op jit(solution)/shard_map/ffn_back/pallas_call | solution.py:350
  185.1 14.4 %attention_back.2.qkv_ref = bf16[1600,768]{1,0:T(8,128)(2,1)S(1)} custom-call(s32[1,768]{1,0:T(1,128)S(1)} %reduce_sum.75.start_ref, f32[32,768]{1,0:T(8,128)S(1)} %get-tuple-element.259.cosine_ref, f32[32,768]{1,0:T(8,128)S(1)} %get-tuple-element.260.sine_ref, bf16[1600,768]{1,0:T(8,128)(2,1)S(1)} %pad_maximum_fusion.1.query_ref.key_ref.value_ref, ...), custom_call_target="tpu_custom_call" | custom-call | flops 8999999488 | bytes 9000000 | tf_op jit(solution)/shard_map/attention_back/pallas_call | solution.py:158
  206.4 12.3 %weight_grad.3 = (bf16[2,480,1280]{2,1,0:T(8,128)(2,1)S(1)}, bf16[2,480,1280]{2,1,0:T(8,128)(2,1)S(1)}) custom-call(s32[5]{0:T(128)S(1)} %stack.44.places_ref, bf16[960,768]{1,0:T(8,128)(2,1)S(1)} %copy-done.64, bf16[768,2560]{1,0:T(8,128)(2,1)S(1)} %copy-done.63, bf16[960,768]{1,0:T(8,128)(2,1)S(1)} %get-tuple-element.227.left2_ref, ...), custom_call_target="tpu_custom_call" | custom-call | flops 7549747200 | bytes 24576000 | tf_op jit(solution)/shard_map/weight_grad/pallas_call | solution.py:416
  218.9 4.5 collective-permute-done.17
  230.9 25.0 %ffn_back.3 = (f32[960,768]{1,0:T(8,128)}, bf16[960,768]{1,0:T(8,128)(2,1)S(1)}, bf16[768,2560]{1,0:T(8,128)(2,1)}, bf16[768,2560]{1,0:T(8,128)(2,1)}, f32[960,1]{1,0:T(8,128)S(1)}, /*index=5*/bf16[960,768]{1,0:T(8,128)(2,1)}) custom-call(f32[960,768]{1,0:T(8,128)S(1)} %get-tuple-element.122.grad_ref, f32[960,768]{1,0:T(8,128)S(1)} %copy-done.43, ...), custom_call_target="tpu_custom_call" | custom-call | flops 11324620800 | bytes 50000000 | tf_op jit(solution)/shard_map/ffn_back/pallas_call | solution.py:350
  262.6 12.2 %weight_grad.4 = (bf16[2,480,1280]{2,1,0:T(8,128)(2,1)S(1)}, bf16[2,480,1280]{2,1,0:T(8,128)(2,1)S(1)}) custom-call(s32[5]{0:T(128)S(1)} %stack.44.places_ref, bf16[960,768]{1,0:T(8,128)(2,1)S(1)} %copy-done.66, bf16[768,2560]{1,0:T(8,128)(2,1)S(1)} %copy-done.58, bf16[960,768]{1,0:T(8,128)(2,1)S(1)} %copy-done.65, bf16[768,2560]{1,0:T(8,128)(2,1)S(1)} %copy-done.60), custom_call_target="tpu_custom_call" | custom-call | flops 7549747200 | bytes 24576000 | tf_op jit(solution)/shard_map/weight_grad/pallas_call | solution.py:416
  281.4 13.2 %weight_grad.5 = (bf16[2,480,1280]{2,1,0:T(8,128)(2,1)S(1)}, bf16[2,480,1280]{2,1,0:T(8,128)(2,1)}) custom-call(s32[5]{0:T(128)S(1)} %stack.44.places_ref, bf16[960,768]{1,0:T(8,128)(2,1)S(1)} %copy-done.66, bf16[768,2560]{1,0:T(8,128)(2,1)S(1)} %copy-done.57, bf16[960,768]{1,0:T(8,128)(2,1)S(1)} %copy-done.65, bf16[768,2560]{1,0:T(8,128)(2,1)S(1)} %copy-done.59), custom_call_target="tpu_custom_call" | custom-call | flops 7549747200 | bytes 24576000 | tf_op jit(solution)/shard_map/weight_grad/pallas_call | solution.py:416
  296.8 14.3 %collective-permute-done.20 = bf16[240,1280]{1,0:T(8,128)(2,1)} collective-permute-done((bf16[240,1280]{1,0:T(8,128)(2,1)}, bf16[240,1280]{1,0:T(8,128)(2,1)}, u32[]{:S(2)}, u32[]{:S(2)}) %collective-permute-start.20) | collective-permute-done | bytes 614432 | tf_op jit(solution)/shard_map/ppermute | solution.py:581
  318.4 14.3 %attention_back.3.qkv2_ref = bf16[1600,768]{1,0:T(8,128)(2,1)S(1)} custom-call(s32[1,768]{1,0:T(1,128)S(1)} %reduce_sum.75.start_ref, f32[32,768]{1,0:T(8,128)S(1)} %get-tuple-element.259.cosine_ref, f32[32,768]{1,0:T(8,128)S(1)} %get-tuple-element.260.sine_ref, bf16[1600,768]{1,0:T(8,128)(2,1)S(1)} %copy-done.16, bf16[1600,768]{1,0:T(8,128)(2,1)S(1)} %copy-done.16, ...), custom_call_target="tpu_custom_call" | custom-call | flops 8999999488 | bytes 9000000 | tf_op jit(solution)/shard_map/attention_back/pallas_call | solution.py:158
  336.8 10.8 %mixed_grad.1 = (bf16[2,480,1280]{2,1,0:T(8,128)(2,1)S(1)}, bf16[2,480,1280]{2,1,0:T(8,128)(2,1)S(1)}) custom-call(s32[5]{0:T(128)S(1)} %stack.44.places_ref, bf16[960,768]{1,0:T(8,128)(2,1)S(1)} %copy-done.46, bf16[960,768]{1,0:T(8,128)(2,1)S(1)} %copy-done.52, bf16[960,768]{1,0:T(8,128)(2,1)S(1)} %copy-done.30, bf16[1600,768]{1,0:T(8,128)(2,1)S(1)} %copy-done.50, ...), custom_call_target="tpu_custom_call" | custom-call | flops 7549747200 | bytes 24576000 | tf_op jit(solution)/shard_map/mixed_grad/pallas_call | solution.py:462
  362.8 4.5 collective-permute-done.29
  373.5 11.1 %collective-permute-done.31.refs_1_ = bf16[240,1280]{1,0:T(8,128)(2,1)S(1)} collective-permute-done((bf16[240,1280]{1,0:T(8,128)(2,1)S(1)}, bf16[240,1280]{1,0:T(8,128)(2,1)S(1)}, u32[]{:S(2)}, u32[]{:S(2)}) %collective-permute-start.31) | collective-permute-done | bytes 614432 | tf_op jit(solution)/shard_map/ppermute | solution.py:581
  389.2 12.3 %collective-permute-done.35 = bf16[240,640]{1,0:T(8,128)(2,1)S(1)} collective-permute-done((bf16[240,640]{1,0:T(8,128)(2,1)S(1)}, bf16[240,640]{1,0:T(8,128)(2,1)S(1)}, u32[]{:S(2)}, u32[]{:S(2)}) %collective-permute-start.35) | collective-permute-done | bytes 307232 | tf_op jit(solution)/shard_map/ppermute | solution.py:581
  405.6 10.5 %collective-permute-done.38.refs_1_ = bf16[240,1280]{1,0:T(8,128)(2,1)S(1)} collective-permute-done((bf16[240,1280]{1,0:T(8,128)(2,1)S(1)}, bf16[240,1280]{1,0:T(8,128)(2,1)S(1)}, u32[]{:S(2)}, u32[]{:S(2)}) %collective-permute-start.38) | collective-permute-done | bytes 614432 | tf_op jit(solution)/shard_map/ppermute | solution.py:581
  421.9 10.5 %collective-permute-done.41 = bf16[240,640]{1,0:T(8,128)(2,1)} collective-permute-done((bf16[240,640]{1,0:T(8,128)(2,1)S(1)}, bf16[240,640]{1,0:T(8,128)(2,1)}, u32[]{:S(2)}, u32[]{:S(2)}) %collective-permute-start.41) | collective-permute-done | bytes 307232 | tf_op jit(solution)/shard_map/ppermute | solution.py:581
  436.2 5.9 %collective-permute-done.43 = bf16[240,640]{1,0:T(8,128)(2,1)S(1)} collective-permute-done((bf16[240,640]{1,0:T(8,128)(2,1)S(1)}, bf16[240,640]{1,0:T(8,128)(2,1)S(1)}, u32[]{:S(2)}, u32[]{:S(2)}) %collective-permute-start.43) | collective-permute-done | bytes 307232 | tf_op jit(solution)/shard_map/ppermute | solution.py:581
  444.1 3.3 collective-permute-done.49
  447.6 4.5 collective-permute-done.50
  452.8 4.5 collective-permute-done.44.refs_1_
  460.4 4.4 assemble.7
  464.8 4.2 assemble.5
  469.0 4.2 assemble.6
  473.2 4.7 assemble.4
  (386 shorter events, 163.3 us)
Async XLA Ops:
  7.9 21.9 %collective-permute-start.1 = (bf16[240,1600]{1,0:T(8,128)(2,1)}, bf16[240,1600]{1,0:T(8,128)(2,1)}, u32[]{:S(2)}, u32[]{:S(2)}) collective-permute-start(bf16[240,1600]{1,0:T(8,128)(2,1)} %concatenate.28), channel_id=1, source_target_pairs={{0,1},{1,0},{2,3},{3,2},{4,5},{5,4},{6,7},{7,6},{8,9},{9,8},{10,11... | collective-permute-start | bytes 2304008 | tf_op jit(solution)/shard_map/ppermute | solution.py:577
  12.7 37.5 %collective-permute-start = (bf16[240,960]{1,0:T(8,128)(2,1)}, bf16[240,960]{1,0:T(8,128)(2,1)}, u32[]{:S(2)}, u32[]{:S(2)}) collective-permute-start(bf16[240,960]{1,0:T(8,128)(2,1)} %constant_dynamic-slice_fusion.21), channel_id=1, source_target_pairs={{0,1},{1,0},{2,3},{3,2},{4,5},{5,4},{6,7},{7,6},{8,9},{9,8},{10,11... | collective-permute-start | bytes 1382408 | tf_op jit(solution)/shard_map/ppermute | solution.py:577
  12.8 27.6 %collective-permute-start.3 = (bf16[2,480]{1,0:T(2,128)(2,1)S(1)}, bf16[2,480]{1,0:T(2,128)(2,1)S(1)}, u32[]{:S(2)}, u32[]{:S(2)}) collective-permute-start(bf16[2,480]{1,0:T(2,128)(2,1)S(1)} %pad_maximum_fusion.8), channel_id=1, source_target_pairs={{0,1},{1,0},{2,3},{3,2},{4,5},{5,4},{6,7},{7,6},{8,9},{9,8},{10,11... | collective-permute-start | bytes 5768 | tf_op jit(solution)/shard_map/ppermute | solution.py:577
  15.7 37.8 %collective-permute-start.8 = (bf16[480,640]{1,0:T(8,128)(2,1)}, bf16[480,640]{1,0:T(8,128)(2,1)}, u32[]{:S(2)}, u32[]{:S(2)}) collective-permute-start(bf16[480,640]{1,0:T(8,128)(2,1)} %constant_dynamic-slice_fusion.20), channel_id=1, source_target_pairs={{0,1},{1,0},{2,3},{3,2},{4,5},{5,4},{6,7},{7,6},{8,9},{9,8},{10,11... | collective-permute-start | bytes 1843208 | tf_op jit(solution)/shard_map/ppermute | solution.py:577
  17.7 52.7 %collective-permute-start.11 = (bf16[480,640]{1,0:T(8,128)(2,1)}, bf16[480,640]{1,0:T(8,128)(2,1)}, u32[]{:S(2)}, u32[]{:S(2)}) collective-permute-start(bf16[480,640]{1,0:T(8,128)(2,1)} %constant_dynamic-slice_fusion.19), channel_id=1, source_target_pairs={{0,1},{1,0},{2,3},{3,2},{4,5},{5,4},{6,7},{7,6},{8,9},{9,8},{10,11... | collective-permute-start | bytes 1843208 | tf_op jit(solution)/shard_map/ppermute | solution.py:577
  53.6 16.8 %collective-permute-start.10 = (bf16[480,640]{1,0:T(8,128)(2,1)}, bf16[480,640]{1,0:T(8,128)(2,1)S(1)}, u32[]{:S(2)}, u32[]{:S(2)}) collective-permute-start(bf16[480,640]{1,0:T(8,128)(2,1)} %collective-permute-done.8.refs_1_), channel_id=1, source_target_pairs={{0,4},{2,6},{4,0},{6,2},{8,12},{10,14},{12,8},{14,10},{16,20},{18,... | collective-permute-start | bytes 1843208 | tf_op jit(solution)/shard_map/ppermute | solution.py:581
  56.8 22.2 %collective-permute-start.5 = (bf16[240,1280]{1,0:T(8,128)(2,1)S(1)}, bf16[240,1280]{1,0:T(8,128)(2,1)S(1)}, u32[]{:S(2)}, u32[]{:S(2)}) collective-permute-start(bf16[240,1280]{1,0:T(8,128)(2,1)S(1)} %constant_dynamic-slice_fusion.18), channel_id=1, source_target_pairs={{0,1},{1,0},{2,3},{3,2},{4,5},{5,4},{6,7},{7,6},{8,9},{9,8},{10,11... | collective-permute-start | bytes 1843208 | tf_op jit(solution)/shard_map/ppermute | solution.py:577
  58.3 20.6 %collective-permute-start.9 = (bf16[480,640]{1,0:T(8,128)(2,1)}, bf16[480,640]{1,0:T(8,128)(2,1)S(1)}, u32[]{:S(2)}, u32[]{:S(2)}) collective-permute-start(bf16[480,640]{1,0:T(8,128)(2,1)} %collective-permute-done.8.refs_1_), channel_id=1, source_target_pairs={{0,2},{2,0},{4,6},{6,4},{8,10},{10,8},{12,14},{14,12},{16,18},{18,... | collective-permute-start | bytes 1843208 | tf_op jit(solution)/shard_map/ppermute | solution.py:581
  70.5 16.5 %collective-permute-start.14 = (bf16[480,640]{1,0:T(8,128)(2,1)}, bf16[480,640]{1,0:T(8,128)(2,1)}, u32[]{:S(2)}, u32[]{:S(2)}) collective-permute-start(bf16[480,640]{1,0:T(8,128)(2,1)} %collective-permute-done.11.refs_1_), channel_id=1, source_target_pairs={{0,8},{2,10},{4,12},{6,14},{8,0},{10,2},{12,4},{14,6},{16,24},{18,... | collective-permute-start | bytes 1843208 | tf_op jit(solution)/shard_map/ppermute | solution.py:581
  72.1 16.3 %collective-permute-start.13 = (bf16[480,640]{1,0:T(8,128)(2,1)}, bf16[480,640]{1,0:T(8,128)(2,1)}, u32[]{:S(2)}, u32[]{:S(2)}) collective-permute-start(bf16[480,640]{1,0:T(8,128)(2,1)} %collective-permute-done.11.refs_1_), channel_id=1, source_target_pairs={{0,2},{2,0},{4,6},{6,4},{8,10},{10,8},{12,14},{14,12},{16,18},{18,... | collective-permute-start | bytes 1843208 | tf_op jit(solution)/shard_map/ppermute | solution.py:581
  87.3 19.9 %collective-permute-start.6 = (bf16[240,1280]{1,0:T(8,128)(2,1)S(1)}, bf16[240,1280]{1,0:T(8,128)(2,1)S(1)}, u32[]{:S(2)}, u32[]{:S(2)}) collective-permute-start(bf16[240,1280]{1,0:T(8,128)(2,1)S(1)} %collective-permute-done.5.refs_1_), channel_id=1, source_target_pairs={{0,2},{2,0},{4,6},{6,4},{8,10},{10,8},{12,14},{14,12},{16,18},{18,... | collective-permute-start | bytes 1843208 | tf_op jit(solution)/shard_map/ppermute | solution.py:581
  87.9 18.9 %collective-permute-start.7 = (bf16[240,1280]{1,0:T(8,128)(2,1)S(1)}, bf16[240,1280]{1,0:T(8,128)(2,1)S(1)}, u32[]{:S(2)}, u32[]{:S(2)}) collective-permute-start(bf16[240,1280]{1,0:T(8,128)(2,1)S(1)} %collective-permute-done.5.refs_1_), channel_id=1, source_target_pairs={{0,4},{2,6},{4,0},{6,2},{8,12},{10,14},{12,8},{14,10},{16,20},{18,... | collective-permute-start | bytes 1843208 | tf_op jit(solution)/shard_map/ppermute | solution.py:581
  225.4 30.5 %collective-permute-start.18 = (bf16[480,1280]{1,0:T(8,128)(2,1)}, bf16[480,1280]{1,0:T(8,128)(2,1)}, u32[]{:S(2)}, u32[]{:S(2)}) collective-permute-start(bf16[480,1280]{1,0:T(8,128)(2,1)} %fusion.19), channel_id=1, source_target_pairs={{0,1},{1,0},{2,3},{3,2},{4,5},{5,4},{6,7},{7,6},{8,9},{9,8},{10,11... | collective-permute-start | bytes 3686408 | tf_op jit(solution)/shard_map/ppermute | solution.py:577
  294.5 19.7 %collective-permute-start.21 = (bf16[2,480,1280]{2,1,0:T(8,128)(2,1)}, bf16[2,480,1280]{2,1,0:T(8,128)(2,1)}, u32[]{:S(2)}, u32[]{:S(2)}) collective-permute-start(bf16[2,480,1280]{2,1,0:T(8,128)(2,1)} %get-tuple-element.142), channel_id=1, source_target_pairs={{0,2},{2,0},{4,6},{6,4},{8,10},{10,8},{12,14},{14,12},{16,18},{18,... | collective-permute-start | bytes 7372808 | tf_op jit(solution)/shard_map/ppermute | solution.py:581
  294.7 16.4 %collective-permute-start.20 = (bf16[240,1280]{1,0:T(8,128)(2,1)}, bf16[240,1280]{1,0:T(8,128)(2,1)}, u32[]{:S(2)}, u32[]{:S(2)}) collective-permute-start(bf16[240,1280]{1,0:T(8,128)(2,1)} %get-tuple-element.240), channel_id=1, source_target_pairs={{0,4},{2,6},{4,0},{6,2},{8,12},{10,14},{12,8},{14,10},{16,20},{18,... | collective-permute-start | bytes 1843208 | tf_op jit(solution)/shard_map/ppermute | solution.py:581
  295.3 37.5 %collective-permute-start.23 = (bf16[480,1280]{1,0:T(8,128)(2,1)}, bf16[480,1280]{1,0:T(8,128)(2,1)S(1)}, u32[]{:S(2)}, u32[]{:S(2)}) collective-permute-start(bf16[480,1280]{1,0:T(8,128)(2,1)} %fusion.20), channel_id=1, source_target_pairs={{0,1},{1,0},{2,3},{3,2},{4,5},{5,4},{6,7},{7,6},{8,9},{9,8},{10,11... | collective-permute-start | bytes 3686408 | tf_op jit(solution)/shard_map/ppermute | solution.py:577
  312.6 20.1 %collective-permute-start.22 = (bf16[240,640]{1,0:T(8,128)(2,1)S(1)}, bf16[240,640]{1,0:T(8,128)(2,1)S(1)}, u32[]{:S(2)}, u32[]{:S(2)}) collective-permute-start(bf16[240,640]{1,0:T(8,128)(2,1)S(1)} %get-tuple-element.256), channel_id=1, source_target_pairs={{0,8},{2,10},{4,12},{6,14},{8,0},{10,2},{12,4},{14,6},{16,24},{18,... | collective-permute-start | bytes 921608 | tf_op jit(solution)/shard_map/ppermute | solution.py:581
  316.8 36.6 %collective-permute-start.26 = (bf16[480,1280]{1,0:T(8,128)(2,1)}, bf16[480,1280]{1,0:T(8,128)(2,1)}, u32[]{:S(2)}, u32[]{:S(2)}) collective-permute-start(bf16[480,1280]{1,0:T(8,128)(2,1)} %fusion.21), channel_id=1, source_target_pairs={{0,1},{1,0},{2,3},{3,2},{4,5},{5,4},{6,7},{7,6},{8,9},{9,8},{10,11... | collective-permute-start | bytes 3686408 | tf_op jit(solution)/shard_map/ppermute | solution.py:577
  333.5 18.3 %collective-permute-start.25 = (bf16[240,1280]{1,0:T(8,128)(2,1)S(1)}, bf16[240,1280]{1,0:T(8,128)(2,1)S(1)}, u32[]{:S(2)}, u32[]{:S(2)}) collective-permute-start(bf16[240,1280]{1,0:T(8,128)(2,1)S(1)} %get-tuple-element.238), channel_id=1, source_target_pairs={{0,4},{2,6},{4,0},{6,2},{8,12},{10,14},{12,8},{14,10},{16,20},{18,... | collective-permute-start | bytes 1843208 | tf_op jit(solution)/shard_map/ppermute | solution.py:581
  334.2 16.8 %collective-permute-start.24 = (bf16[240,640]{1,0:T(8,128)(2,1)S(1)}, bf16[240,640]{1,0:T(8,128)(2,1)S(1)}, u32[]{:S(2)}, u32[]{:S(2)}) collective-permute-start(bf16[240,640]{1,0:T(8,128)(2,1)S(1)} %add_convert_fusion.17), channel_id=1, source_target_pairs={{0,16},{2,18},{4,20},{6,22},{8,24},{10,26},{12,28},{14,30},{16,0},... | collective-permute-start | bytes 921608 | tf_op jit(solution)/shard_map/ppermute | solution.py:581
  352.0 15.3 %collective-permute-start.29 = (bf16[240,640]{1,0:T(8,128)(2,1)S(1)}, bf16[240,640]{1,0:T(8,128)(2,1)S(1)}, u32[]{:S(2)}, u32[]{:S(2)}) collective-permute-start(bf16[240,640]{1,0:T(8,128)(2,1)S(1)} %get-tuple-element.254), channel_id=1, source_target_pairs={{0,8},{2,10},{4,12},{6,14},{8,0},{10,2},{12,4},{14,6},{16,24},{18,... | collective-permute-start | bytes 921608 | tf_op jit(solution)/shard_map/ppermute | solution.py:581
  355.6 16.8 %collective-permute-start.30 = (bf16[240,1280]{1,0:T(8,128)(2,1)S(1)}, bf16[240,1280]{1,0:T(8,128)(2,1)S(1)}, u32[]{:S(2)}, u32[]{:S(2)}) collective-permute-start(bf16[240,1280]{1,0:T(8,128)(2,1)S(1)} %get-tuple-element.236), channel_id=1, source_target_pairs={{0,4},{2,6},{4,0},{6,2},{8,12},{10,14},{12,8},{14,10},{16,20},{18,... | collective-permute-start | bytes 1843208 | tf_op jit(solution)/shard_map/ppermute | solution.py:581
  357.4 30.9 %collective-permute-start.34 = (bf16[480,1280]{1,0:T(8,128)(2,1)S(1)}, bf16[480,1280]{1,0:T(8,128)(2,1)S(1)}, u32[]{:S(2)}, u32[]{:S(2)}) collective-permute-start(bf16[480,1280]{1,0:T(8,128)(2,1)S(1)} %fusion.22), channel_id=1, source_target_pairs={{0,1},{1,0},{2,3},{3,2},{4,5},{5,4},{6,7},{7,6},{8,9},{9,8},{10,11... | collective-permute-start | bytes 3686408 | tf_op jit(solution)/shard_map/ppermute | solution.py:577
  361.3 23.3 %collective-permute-start.31 = (bf16[240,1280]{1,0:T(8,128)(2,1)S(1)}, bf16[240,1280]{1,0:T(8,128)(2,1)S(1)}, u32[]{:S(2)}, u32[]{:S(2)}) collective-permute-start(bf16[240,1280]{1,0:T(8,128)(2,1)S(1)} %pad_maximum_fusion.4.refs_0_), channel_id=1, source_target_pairs={{0,4},{2,6},{4,0},{6,2},{8,12},{10,14},{12,8},{14,10},{16,20},{18,... | collective-permute-start | bytes 1843208 | tf_op jit(solution)/shard_map/ppermute | solution.py:581
  367.4 17.1 %collective-permute-start.32 = (bf16[240,640]{1,0:T(8,128)(2,1)S(1)}, bf16[240,640]{1,0:T(8,128)(2,1)S(1)}, u32[]{:S(2)}, u32[]{:S(2)}) collective-permute-start(bf16[240,640]{1,0:T(8,128)(2,1)S(1)} %add_convert_fusion.15), channel_id=1, source_target_pairs={{0,16},{2,18},{4,20},{6,22},{8,24},{10,26},{12,28},{14,30},{16,0},... | collective-permute-start | bytes 921608 | tf_op jit(solution)/shard_map/ppermute | solution.py:581
  386.3 15.5 %collective-permute-start.36 = (bf16[240,640]{1,0:T(8,128)(2,1)S(1)}, bf16[240,640]{1,0:T(8,128)(2,1)S(1)}, u32[]{:S(2)}, u32[]{:S(2)}) collective-permute-start(bf16[240,640]{1,0:T(8,128)(2,1)S(1)} %add_convert_fusion.13), channel_id=1, source_target_pairs={{0,16},{2,18},{4,20},{6,22},{8,24},{10,26},{12,28},{14,30},{16,0},... | collective-permute-start | bytes 921608 | tf_op jit(solution)/shard_map/ppermute | solution.py:581
  388.9 16.2 %collective-permute-start.37 = (bf16[240,1280]{1,0:T(8,128)(2,1)S(1)}, bf16[240,1280]{1,0:T(8,128)(2,1)S(1)}, u32[]{:S(2)}, u32[]{:S(2)}) collective-permute-start(bf16[240,1280]{1,0:T(8,128)(2,1)S(1)} %get-tuple-element.234), channel_id=1, source_target_pairs={{0,4},{2,6},{4,0},{6,2},{8,12},{10,14},{12,8},{14,10},{16,20},{18,... | collective-permute-start | bytes 1843208 | tf_op jit(solution)/shard_map/ppermute | solution.py:581
  417.2 15.3 %collective-permute-start.41 = (bf16[240,640]{1,0:T(8,128)(2,1)S(1)}, bf16[240,640]{1,0:T(8,128)(2,1)}, u32[]{:S(2)}, u32[]{:S(2)}) collective-permute-start(bf16[240,640]{1,0:T(8,128)(2,1)S(1)} %add_convert_fusion.11), channel_id=1, source_target_pairs={{0,16},{2,18},{4,20},{6,22},{8,24},{10,26},{12,28},{14,30},{16,0},... | collective-permute-start | bytes 921608 | tf_op jit(solution)/shard_map/ppermute | solution.py:581
  420.5 15.7 %collective-permute-start.42 = (bf16[240,1280]{1,0:T(8,128)(2,1)}, bf16[240,1280]{1,0:T(8,128)(2,1)}, u32[]{:S(2)}, u32[]{:S(2)}) collective-permute-start(bf16[240,1280]{1,0:T(8,128)(2,1)} %pad_maximum_fusion.6.refs_0_), channel_id=1, source_target_pairs={{0,4},{2,6},{4,0},{6,2},{8,12},{10,14},{12,8},{14,10},{16,20},{18,... | collective-permute-start | bytes 1843208 | tf_op jit(solution)/shard_map/ppermute | solution.py:581
  435.6 22.3 %collective-permute-start.56 = (bf16[240,1280]{1,0:T(8,128)(2,1)}, bf16[240,1280]{1,0:T(8,128)(2,1)}, u32[]{:S(2)}, u32[]{:S(2)}) collective-permute-start(bf16[240,1280]{1,0:T(8,128)(2,1)} %copy-done.17), channel_id=1, source_target_pairs={{0,2},{2,0},{4,6},{6,4},{8,10},{10,8},{12,14},{14,12},{16,18},{18,... | collective-permute-start | bytes 1843208 | tf_op jit(solution)/shard_map/ppermute | solution.py:581
  435.6 22.3 %collective-permute-start.57 = (bf16[240,1280]{1,0:T(8,128)(2,1)}, bf16[240,1280]{1,0:T(8,128)(2,1)}, u32[]{:S(2)}, u32[]{:S(2)}) collective-permute-start(bf16[240,1280]{1,0:T(8,128)(2,1)} %copy-done.31), channel_id=1, source_target_pairs={{0,2},{2,0},{4,6},{6,4},{8,10},{10,8},{12,14},{14,12},{16,18},{18,... | collective-permute-start | bytes 1843208 | tf_op jit(solution)/shard_map/ppermute | solution.py:581
  436.1 22.3 %collective-permute-start.52 = (bf16[240,1280]{1,0:T(8,128)(2,1)}, bf16[240,1280]{1,0:T(8,128)(2,1)}, u32[]{:S(2)}, u32[]{:S(2)}) collective-permute-start(bf16[240,1280]{1,0:T(8,128)(2,1)} %copy-done.19), channel_id=1, source_target_pairs={{0,2},{2,0},{4,6},{6,4},{8,10},{10,8},{12,14},{14,12},{16,18},{18,... | collective-permute-start | bytes 1843208 | tf_op jit(solution)/shard_map/ppermute | solution.py:581
  (115 other events, 990.3 us)

commit v3 on v2

--- a/solution.py
+++ b/solution.py
@@ -492,13 +492,17 @@
         else:
             whole_ref[rows, pl.ds(pl.multiple_of(at_core * cols, 128), cols)] = value
     for out_ref, (low, high) in zip(outputs[:-1], cuts):
-        out_ref[...] = whole_ref[:, low:high]
+        value = whole_ref[:, low:high]
+        out_ref[...] = value.T if out_ref.shape[0] == high - low else value
 
 
 def assemble(places, pieces, stack_cores, cuts=()):
     count, cols = pieces[0].shape
     shape = (4 * count, cols) if stack_cores else (2 * count, 2 * cols)
-    out_shape = [jax.ShapeDtypeStruct((shape[0], high - low), F32) for low, high in cuts]
+    out_shape = [
+        jax.ShapeDtypeStruct((high - low, shape[0]) if high - low < shape[0] else (shape[0], high - low), F32)
+        for low, high in cuts
+    ]
     out_shape = out_shape or [jax.ShapeDtypeStruct(shape, F32)]
     return pl.pallas_call(
         partial(assemble_kernel, stack_cores, cuts),
@@ -668,43 +672,134 @@
     return lax.dynamic_slice_in_dim(value, which * count, count, axis)
 
 
+def sides():
+    place = lax.axis_index("dp")
+    return ((place // 2) % 2, (place // 4) % 2, (place // 8) % 2)
+
+
 class Reduction:
-    def __init__(self, halves):
+    def __init__(self, halves, queue=()):
         self.keep, send = halves
-        self.received = swap_dp(send, 1)
-        place = lax.axis_index("dp")
-        self.side, self.lane = (place // 2) % 2, (place // 4) % 2
-        self.stage = 0
+        self.received = swap_dp(after(send, *queue), 1)
+        self.side, self.lane, _ = sides()
+        self.plan = iter((self.fsdp, self.y, self.z_near, self.z_far, self.z_back, self.y_back, self.finish))
 
     def step(self, queue):
-        gate = lambda value: after(value, *queue)
-        self.stage += 1
-        if self.stage == 1:
-            mine = add(gate(self.keep)[1], self.received[1])
-            self.incoming = swap_fsdp(mine)
-        elif self.stage == 2:
-            half = add3(gate(self.keep)[0], self.received[0], self.incoming)
-            mine, self.own = cut(half, 1 - self.side, 0), cut(half, self.side, 0)
-            self.incoming = swap_dp(mine, 2)
-        elif self.stage == 3:
-            part = add(gate(self.own), self.incoming)
-            mine, self.own = cut(part, 1 - self.lane, 1), cut(part, self.lane, 1)
-            self.incoming = swap_dp(mine, 4)
-        elif self.stage in (4, 5):
-            mine = self.own = add(gate(self.own), self.incoming)
-            self.incoming = swap_dp(mine, 8 if self.stage == 4 else 4)
-        elif self.stage == 6:
-            own = gate(self.own)
-            low = jnp.where(self.lane == 0, own, self.incoming)
-            high = jnp.where(self.lane == 0, self.incoming, own)
-            mine = self.own = jnp.concatenate([low, high], axis=1)
-            self.across = swap_dp(mine, 2)
-            self.beside = swap_dp(mine, 1)
-        else:
-            mine = gate(self.across)
-            self.pieces = (self.own, mine, self.beside, swap_dp(mine, 1))
+        mine = next(self.plan)(lambda value: after(value, *queue))
         queue[:] = [mine]
+
+    def split(self, value, which, axis, bit):
+        mine, self.own = cut(value, 1 - which, axis), cut(value, which, axis)
+        self.incoming = swap_dp(mine, bit)
         return mine
+
+    def fsdp(self, gate):
+        mine = add(gate(self.keep)[1], self.received[1])
+        self.incoming = swap_fsdp(mine)
+        return mine
+
+    def fsdp_sum(self, gate):
+        return add3(gate(self.keep)[0], self.received[0], self.incoming)
+
+    def y(self, gate):
+        return self.split(self.fsdp_sum(gate), self.side, 0, 2)
+
+    def z_near(self, gate):
+        return self.split(add(gate(self.own), self.incoming), self.lane, 1, 4)
+
+    def z_far(self, gate):
+        self.own = add(gate(self.own), self.incoming)
+        self.incoming = swap_dp(self.own, 8)
+        return self.own
+
+    def z_back(self, gate):
+        self.own = add(gate(self.own), self.incoming)
+        self.incoming = swap_dp(self.own, 4)
+        return self.own
+
+    def y_back(self, gate):
+        mine = self.own = put_together(gate(self.own), self.incoming, self.lane, 1)
+        self.across = swap_dp(mine, 2)
+        self.beside = swap_dp(mine, 1)
+        return mine
+
+    def finish(self, gate):
+        mine = gate(self.across)
+        self.pieces = (self.own, mine, self.beside, swap_dp(mine, 1))
+        return mine
+
+
+class ReductionOverZ(Reduction):
+    def __init__(self, halves, queue=()):
+        super().__init__(halves, queue)
+        self.far = sides()[2]
+        self.plan = iter((self.fsdp, self.first, self.second, self.over_y, self.back_far, self.back_near, self.done))
+
+    def first(self, gate):
+        return self.split(self.fsdp_sum(gate), self.lane, 0, 4)
+
+    def second(self, gate):
+        return self.split(add(gate(self.own), self.incoming), self.far, 0, 8)
+
+    def over_y(self, gate):
+        self.own = add(gate(self.own), self.incoming)
+        self.incoming = swap_dp(self.own, 2)
+        return self.own
+
+    def back_far(self, gate):
+        self.own = add(gate(self.own), self.incoming)
+        self.incoming = swap_dp(self.own, 8)
+        return self.own
+
+    def back_near(self, gate):
+        mine = self.own = put_together(gate(self.own), self.incoming, self.far, 0)
+        self.across = swap_dp(mine, 4)
+        self.beside = swap_dp(mine, 1)
+        return mine
+
+    def done(self, gate):
+        mine = gate(self.across)
+        self.pieces = (self.own, mine, self.beside, swap_dp(mine, 1))
+        return mine
+
+
+class ReductionBothWays(Reduction):
+    def __init__(self, halves, queue=()):
+        super().__init__(halves, queue)
+        self.plan = iter((self.one, self.two, self.three, self.z_far, self.z_back, self.y_back, self.finish))
+
+    def one(self, gate):
+        keep = gate(self.keep)
+        half = keep.shape[2] // 2
+        theirs = add(keep[1, :, :half], self.received[1, :, :half])
+        self.over_x = swap_fsdp(theirs)
+        both = add(keep[:, :, half:], self.received[:, :, half:])
+        mine, self.both = cut(both, 1 - self.side, 1), cut(both, self.side, 1)
+        self.over_y = swap_dp(mine, 2)
+        return mine
+
+    def two(self, gate):
+        half = self.keep.shape[2] // 2
+        first = add3(gate(self.keep)[0, :, :half], self.received[0, :, :half], self.over_x)
+        mine, self.first = cut(first, 1 - self.side, 0), cut(first, self.side, 0)
+        self.over_y_too = swap_dp(mine, 2)
+        theirs = add(gate(self.both)[1], self.over_y[1])
+        self.over_x_too = swap_fsdp(theirs)
+        return theirs
+
+    def three(self, gate):
+        first = add(gate(self.first), self.over_y_too)
+        second = add3(gate(self.both)[0], self.over_y[0], self.over_x_too)
+        mine = jnp.where(self.lane == 0, second, first)
+        self.own = jnp.where(self.lane == 0, first, second)
+        self.incoming = swap_dp(mine, 4)
+        return mine
+
+
+def put_together(own, other, which, axis):
+    low = jnp.where(which == 0, own, other)
+    high = jnp.where(which == 0, other, own)
+    return jnp.concatenate([low, high], axis=axis)
 
 
 def make_body(fsdp_size, dp_size):
@@ -797,7 +892,8 @@
         queue = []
         if paired:
             down = Reduction(down_halves)
-            grad = after(grad, down.step(queue))
+            down.step(queue)
+            grad = after(grad, *queue)
         else:
             grad = after(grad, *down_halves)
         grad, attn_grad, gate_grad, up_grad, ffn_gain, _ = ffn_back(
@@ -807,18 +903,21 @@
             down.step(queue)
             gate_grad = after(gate_grad, *queue)
         gate_halves = weight_grad(places, (second_normed, gate_grad2), (first_normed, gate_grad), True)
+        if paired:
+            queue.append(gate_halves[0])
+            down.step(queue)
+            gate = Reduction(gate_halves, queue)
         mix_grad_in = after(attn_grad, *gate_halves)
         mix_grad = dot(weights[1], mix_grad_in, (1, 0)).astype(BF16)
         if paired:
-            gate = Reduction(gate_halves)
             queue.append(mix_grad)
             gate.step(queue)
             up_grad = after(up_grad, *queue)
         up_halves = weight_grad(places, (second_normed, up_grad2), (first_normed, up_grad), True)
         if paired:
             queue.append(up_halves[0])
-            up = Reduction(up_halves)
             down.step(queue)
+            up = Reduction(up_halves, queue)
             up.step(queue)
             mix_grad = after(mix_grad, *queue)
         qkv_grad = attention_back(start, cosine, sine, first[2], first[4], first[3], mix_grad)
@@ -849,14 +948,30 @@
         cuts = ((0, width), (width, 2 * width), (2 * width, width + key_end), (width + key_end, width + value_end))
         if paired:
             queue.append(grad)
-            for reduction in (
-                down, gate, up, down, gate, up, mixed, gate, up, mixed, gate, up, mixed, mixed, up, mixed, mixed,
-            ):
-                reduction.step(queue)
-            (grad_down,) = assemble(places, down.pieces, True)
-            (grad_gate,) = assemble(places, gate.pieces, False)
-            (grad_up,) = assemble(places, up.pieces, False)
+            down.step(queue)
+            gate.step(queue)
+            up.step(queue)
+            mixed.step(queue)
+            gate.step(queue)
+            up.step(queue)
+            gate.step(queue)
+            mixed.step(queue)
+            (grad_down,) = assemble(places, [after(down.pieces[0], *queue), *down.pieces[1:]], True)
+            queue.append(grad_down)
+            up.step(queue)
+            mixed.step(queue)
+            up.step(queue)
+            mixed.step(queue)
+            gate.step(queue)
+            (grad_gate,) = assemble(places, [after(gate.pieces[0], *queue), *gate.pieces[1:]], False)
+            queue.append(grad_gate)
+            mixed.step(queue)
+            up.step(queue)
+            mixed.step(queue)
+            (grad_up,) = assemble(places, [after(up.pieces[0], *queue), *up.pieces[1:]], False)
+            queue.append(grad_up)
             grad_out, grad_query, grad_key, grad_value = assemble(places, mixed.pieces, False, cuts)
+            grad_key, grad_value = grad_key.T, grad_value.T
             gain_grads = reduce_vector(gain_grads).astype(F32)
         else:
 

time: 488 us -> 480 us (0.984)
  waiting for transfers between devices: 125 us -> 102 us
  starting transfers between devices: 43.4 us -> 54.2 us
  local copies, waits for them, and re-layouts: 44.9 us -> 52.5 us
    ppermute x47, waiting for transfers between devices: 103 us -> 61.2 us  [swap_dp(): return lax.ppermute(value, 'dp', [(i, i ^ bit) for i in range(size)])]
    ppermute x11, waiting for transfers between devices: 22.3 us -> 41.2 us  [swap_fsdp(): return lax.ppermute(value, 'fsdp', [(0, 1), (1, 0)])]
    ppermute x47, starting transfers between devices: 29.9 us -> 38.8 us  [swap_dp(): return lax.ppermute(value, 'dp', [(i, i ^ bit) for i in range(size)])]
    unnamed x182 -> x180, local copies, waits for them, and re-layouts: 30.2 us -> 39 us
  transfers between devices with their start and end apart: 58 -> 58, of which waited for: 24 -> 23; matrix products, arithmetic and copies ran while one was open for 9% -> 9% of each run, Pallas kernels for 20% -> 25%
where the time goes in v3:
time: 480 us; the launch traced here: 471 us
  Pallas kernels  204 us (42%)
  waiting for transfers between devices  102 us (21%)
  starting transfers between devices  54.2 us (11%)
  local copies, waits for them, and re-layouts  52.5 us (11%)
  matrix products  29.6 us (6%)
  other arithmetic  26.6 us (6%)
    ppermute x47, waiting for transfers between devices, swap_dp(): return lax.ppermute(value, 'dp', [(i, i ^ bit) for i in range(size)])  61.2 us
    pallas_call x2, Pallas kernels, ffn_back(): pl.pallas_call(ffn_back_kernel, grid=(hidden // CHUNK,), in_specs=[full,...  49.3 us
    ppermute x11, waiting for transfers between devices, swap_fsdp(): return lax.ppermute(value, 'fsdp', [(0, 1), (1, 0)])  41.2 us
    unnamed x180, local copies, waits for them, and re-layouts  39 us
    ppermute x47, starting transfers between devices, swap_dp(): return lax.ppermute(value, 'dp', [(i, i ^ bit) for i in range(size)])  38.8 us
    pallas_call x3, Pallas kernels, weight_grad(): pl.pallas_call(partial(weight_grad_kernel, left_fsdp, False), grid_spec=p...  37.7 us
    dot_general x9, matrix products, dot(): lax.dot_general(left, right, ((contract[:1], contract[1:]), ((), ())), pr...  29.6 us
    pallas_call x2, Pallas kernels, attention_back(): pl.pallas_call(attention_back_kernel, grid=(KEY_VALUE_HEADS,), in_specs=[...  28.8 us
  transfers between devices with their start and end apart: 58, of which 23 were waited for; matrix products, arithmetic and copies ran while one was open for 9% of the time, Pallas kernels for 25%

profile of v3, /device:TPU:0, one launch (start us, length us, event | category | flops | bytes accessed | tf_op | source)
XLA Modules:
  0.0 471.1 jit_solution(12688314589088237203)
XLA Ops:
  22.9 6.9 %collective-permute-done.1.refs_3_ = bf16[240,1600]{1,0:T(8,128)(2,1)} collective-permute-done((bf16[240,1600]{1,0:T(8,128)(2,1)}, bf16[240,1600]{1,0:T(8,128)(2,1)}, u32[]{:S(2)}, u32[]{:S(2)}) %collective-permute-start.1) | collective-permute-done | bytes 768032 | tf_op jit(solution)/shard_map/ppermute | solution.py:581
  29.8 10.5 %collective-permute-done.3 = bf16[2,480]{1,0:T(2,128)(2,1)S(1)} collective-permute-done((bf16[2,480]{1,0:T(2,128)(2,1)S(1)}, bf16[2,480]{1,0:T(2,128)(2,1)S(1)}, u32[]{:S(2)}, u32[]{:S(2)}) %collective-permute-start.3) | collective-permute-done | bytes 1952 | tf_op jit(solution)/shard_map/ppermute | solution.py:581
  50.3 3.3 collective-permute-done.8.refs_1_
  58.8 11.5 %attention.2 = (bf16[960,768]{1,0:T(8,128)(2,1)S(1)}, f32[5,8,768]{2,1,0:T(8,128)S(1)}) custom-call(s32[1,768]{1,0:T(1,128)S(1)} %reduce_sum.75.start_ref, bf16[1600,768]{1,0:T(8,128)(2,1)S(1)} %pad_maximum_fusion.query_ref.key_ref.value_ref, bf16[1600,768]{1,0:T(8,128)(2,1)S(1)} %pad_maximum_fusion.query_ref.key_ref.value_ref, ...), custom_call_target="tpu_custom_call" | custom-call | flops 6000000000 | bytes 4000000 | tf_op jit(solution)/shard_map/attention/pallas_call | solution.py:80
  74.0 3.4 fusion.3.middle_ref
  83.2 3.9 collective-permute-done.14.refs_3_
  93.7 13.0 %ffn_up.1 = (bf16[960,768]{1,0:T(8,128)(2,1)}, bf16[768,2560]{1,0:T(8,128)(2,1)}, bf16[768,2560]{1,0:T(8,128)(2,1)}, bf16[768,2560]{1,0:T(8,128)(2,1)}) custom-call(f32[960,768]{1,0:T(8,128)S(1)} %copy-done.41, f32[960,1]{1,0:T(8,128)S(1)} %copy.49.gain_ref, bf16[960,2560]{1,0:T(8,128)(2,1)S(1)} %bitcast.119, bf16[960,2560]{1,0:T(8,128)(2,1)S(1)} %join.8.up_w_ref), custom_call_target="tpu_custom_call" | custom-call | flops 7549747200 | bytes 30000000 | tf_op jit(solution)/shard_map/ffn_up/pallas_call | solution.py:280
  109.7 7.9 %multiply_reduce_fusion.2 = (f32[768]{0:T(1024)S(1)}, f32[960,768]{1,0:T(8,128)S(1)}) fusion(f32[960,768]{1,0:T(8,128)S(1)} %copy-done.41, bf16[960,2560]{1,0:T(8,128)(2,1)S(1)} %join.9.down_w_ref, bf16[768,2560]{1,0:T(8,128)(2,1)} %get-tuple-element.113.right2_ref), kind=kOutput, calls=%fused_computation.21 | convolution fusion | flops 3777084672 | bytes 14748672 | tf_op jit(solution)/shard_map/dot_general | solution.py:31
  124.8 11.3 %attention.3 = (bf16[960,768]{1,0:T(8,128)(2,1)S(1)}, f32[5,8,768]{2,1,0:T(8,128)S(1)}) custom-call(s32[1,768]{1,0:T(1,128)S(1)} %reduce_sum.75.start_ref, bf16[1600,768]{1,0:T(8,128)(2,1)S(1)} %pad_maximum_fusion.1.query_ref.key_ref.value_ref, bf16[1600,768]{1,0:T(8,128)(2,1)S(1)} %pad_maximum_fusion.1.query_ref.key_ref.value_ref, ...), custom_call_target="tpu_custom_call" | custom-call | flops 6000000000 | bytes 4000000 | tf_op jit(solution)/shard_map/attention/pallas_call | solution.py:80
  138.7 16.3 %ffn.1 = (f32[960,768]{1,0:T(8,128)S(1)}, bf16[960,768]{1,0:T(8,128)(2,1)}, bf16[768,2560]{1,0:T(8,128)(2,1)}, bf16[768,2560]{1,0:T(8,128)(2,1)}, bf16[768,2560]{1,0:T(8,128)(2,1)}) custom-call(f32[960,768]{1,0:T(8,128)S(1)} %convolution_add_fusion.middle_ref, f32[960,1]{1,0:T(8,128)S(1)} %copy-done.39, bf16[960,2560]{1,0:T(8,128)(2,1)S(1)} %bitcast.119, ...), custom_call_target="tpu_custom_call" | custom-call | flops 11324620800 | bytes 40000000 | tf_op jit(solution)/shard_map/ffn/pallas_call | solution.py:233
  158.7 24.3 %ffn_back.2 = (f32[960,768]{1,0:T(8,128)}, bf16[960,768]{1,0:T(8,128)(2,1)S(1)}, bf16[768,2560]{1,0:T(8,128)(2,1)}, bf16[768,2560]{1,0:T(8,128)(2,1)}, f32[960,1]{1,0:T(8,128)S(1)}, /*index=5*/bf16[960,768]{1,0:T(8,128)(2,1)}) custom-call(f32[960,768]{1,0:T(8,128)S(1)} %convert_bitcast_fusion.grad_ref, f32[960,768]{1,0:T(8,128)S(1)} %convolution_add_fusion.middle_ref, ...), custom_call_target="tpu_custom_call" | custom-call | flops 11324620800 | bytes 50000000 | tf_op jit(solution)/shard_map/ffn_back/pallas_call | solution.py:350
  185.1 14.4 %attention_back.2.qkv_ref = bf16[1600,768]{1,0:T(8,128)(2,1)S(1)} custom-call(s32[1,768]{1,0:T(1,128)S(1)} %reduce_sum.75.start_ref, f32[32,768]{1,0:T(8,128)S(1)} %get-tuple-element.225.cosine_ref, f32[32,768]{1,0:T(8,128)S(1)} %get-tuple-element.226.sine_ref, bf16[1600,768]{1,0:T(8,128)(2,1)S(1)} %pad_maximum_fusion.1.query_ref.key_ref.value_ref, ...), custom_call_target="tpu_custom_call" | custom-call | flops 8999999488 | bytes 9000000 | tf_op jit(solution)/shard_map/attention_back/pallas_call | solution.py:158
  206.4 12.3 %weight_grad.3 = (bf16[2,480,1280]{2,1,0:T(8,128)(2,1)S(1)}, bf16[2,480,1280]{2,1,0:T(8,128)(2,1)S(1)}) custom-call(s32[5]{0:T(128)S(1)} %stack.44.places_ref, bf16[960,768]{1,0:T(8,128)(2,1)S(1)} %copy-done.64, bf16[768,2560]{1,0:T(8,128)(2,1)S(1)} %copy-done.63, bf16[960,768]{1,0:T(8,128)(2,1)S(1)} %get-tuple-element.193.left2_ref, ...), custom_call_target="tpu_custom_call" | custom-call | flops 7549747200 | bytes 24576000 | tf_op jit(solution)/shard_map/weight_grad/pallas_call | solution.py:416
  218.9 4.5 collective-permute-done.17
  230.9 25.0 %ffn_back.3 = (f32[960,768]{1,0:T(8,128)}, bf16[960,768]{1,0:T(8,128)(2,1)S(1)}, bf16[768,2560]{1,0:T(8,128)(2,1)}, bf16[768,2560]{1,0:T(8,128)(2,1)}, f32[960,1]{1,0:T(8,128)S(1)}, /*index=5*/bf16[960,768]{1,0:T(8,128)(2,1)}) custom-call(f32[960,768]{1,0:T(8,128)S(1)} %get-tuple-element.127.grad_ref, f32[960,768]{1,0:T(8,128)S(1)} %copy-done.42, ...), custom_call_target="tpu_custom_call" | custom-call | flops 11324620800 | bytes 50000000 | tf_op jit(solution)/shard_map/ffn_back/pallas_call | solution.py:350
  262.3 12.2 %weight_grad.4 = (bf16[2,480,1280]{2,1,0:T(8,128)(2,1)S(1)}, bf16[2,480,1280]{2,1,0:T(8,128)(2,1)S(1)}) custom-call(s32[5]{0:T(128)S(1)} %stack.44.places_ref, bf16[960,768]{1,0:T(8,128)(2,1)S(1)} %copy-done.66, bf16[768,2560]{1,0:T(8,128)(2,1)S(1)} %copy-done.58, bf16[960,768]{1,0:T(8,128)(2,1)S(1)} %copy-done.65, bf16[768,2560]{1,0:T(8,128)(2,1)S(1)} %copy-done.60), custom_call_target="tpu_custom_call" | custom-call | flops 7549747200 | bytes 24576000 | tf_op jit(solution)/shard_map/weight_grad/pallas_call | solution.py:416
  283.2 13.2 %weight_grad.5 = (bf16[2,480,1280]{2,1,0:T(8,128)(2,1)S(1)}, bf16[2,480,1280]{2,1,0:T(8,128)(2,1)}) custom-call(s32[5]{0:T(128)S(1)} %stack.44.places_ref, bf16[960,768]{1,0:T(8,128)(2,1)S(1)} %copy-done.66, bf16[768,2560]{1,0:T(8,128)(2,1)S(1)} %copy-done.57, bf16[960,768]{1,0:T(8,128)(2,1)S(1)} %copy-done.65, bf16[768,2560]{1,0:T(8,128)(2,1)S(1)} %copy-done.59), custom_call_target="tpu_custom_call" | custom-call | flops 7549747200 | bytes 24576000 | tf_op jit(solution)/shard_map/weight_grad/pallas_call | solution.py:416
  307.5 14.3 %attention_back.3.qkv2_ref = bf16[1600,768]{1,0:T(8,128)(2,1)S(1)} custom-call(s32[1,768]{1,0:T(1,128)S(1)} %reduce_sum.75.start_ref, f32[32,768]{1,0:T(8,128)S(1)} %get-tuple-element.225.cosine_ref, f32[32,768]{1,0:T(8,128)S(1)} %get-tuple-element.226.sine_ref, bf16[1600,768]{1,0:T(8,128)(2,1)S(1)} %copy-done.16, bf16[1600,768]{1,0:T(8,128)(2,1)S(1)} %copy-done.16, ...), custom_call_target="tpu_custom_call" | custom-call | flops 8999999488 | bytes 9000000 | tf_op jit(solution)/shard_map/attention_back/pallas_call | solution.py:158
  321.9 4.8 %collective-permute-done.24 = bf16[480,1280]{1,0:T(8,128)(2,1)S(1)} collective-permute-done((bf16[480,1280]{1,0:T(8,128)(2,1)}, bf16[480,1280]{1,0:T(8,128)(2,1)S(1)}, u32[]{:S(2)}, u32[]{:S(2)}) %collective-permute-start.24) | collective-permute-done | bytes 1228832 | tf_op jit(solution)/shard_map/ppermute | solution.py:581
  330.2 10.8 %mixed_grad.1 = (bf16[2,480,1280]{2,1,0:T(8,128)(2,1)S(1)}, bf16[2,480,1280]{2,1,0:T(8,128)(2,1)S(1)}) custom-call(s32[5]{0:T(128)S(1)} %stack.44.places_ref, bf16[960,768]{1,0:T(8,128)(2,1)S(1)} %copy-done.45, bf16[960,768]{1,0:T(8,128)(2,1)S(1)} %copy-done.52, bf16[960,768]{1,0:T(8,128)(2,1)S(1)} %copy-done.27, bf16[1600,768]{1,0:T(8,128)(2,1)S(1)} %copy-done.50, ...), custom_call_target="tpu_custom_call" | custom-call | flops 7549747200 | bytes 24576000 | tf_op jit(solution)/shard_map/mixed_grad/pallas_call | solution.py:462
  341.1 3.2 fusion.14
  347.9 4.7 %collective-permute-done.27 = bf16[480,1280]{1,0:T(8,128)(2,1)} collective-permute-done((bf16[480,1280]{1,0:T(8,128)(2,1)S(1)}, bf16[480,1280]{1,0:T(8,128)(2,1)}, u32[]{:S(2)}, u32[]{:S(2)}) %collective-permute-start.27) | collective-permute-done | bytes 1228832 | tf_op jit(solution)/shard_map/ppermute | solution.py:581
  363.9 10.0 %collective-permute-done.31 = bf16[240,1280]{1,0:T(8,128)(2,1)S(1)} collective-permute-done((bf16[240,1280]{1,0:T(8,128)(2,1)S(1)}, bf16[240,1280]{1,0:T(8,128)(2,1)S(1)}, u32[]{:S(2)}, u32[]{:S(2)}) %collective-permute-start.31) | collective-permute-done | bytes 614432 | tf_op jit(solution)/shard_map/ppermute | solution.py:585
  374.9 9.3 %collective-permute-done.32 = bf16[480,1280]{1,0:T(8,128)(2,1)S(1)} collective-permute-done((bf16[480,1280]{1,0:T(8,128)(2,1)S(1)}, bf16[480,1280]{1,0:T(8,128)(2,1)S(1)}, u32[]{:S(2)}, u32[]{:S(2)}) %collective-permute-start.32) | collective-permute-done | bytes 1228832 | tf_op jit(solution)/shard_map/ppermute | solution.py:581
  390.1 5.6 %collective-permute-done.35 = bf16[240,640]{1,0:T(8,128)(2,1)S(1)} collective-permute-done((bf16[240,640]{1,0:T(8,128)(2,1)S(1)}, bf16[240,640]{1,0:T(8,128)(2,1)S(1)}, u32[]{:S(2)}, u32[]{:S(2)}) %collective-permute-start.35) | collective-permute-done | bytes 307232 | tf_op jit(solution)/shard_map/ppermute | solution.py:585
  395.8 5.9 %collective-permute-done.36 = bf16[240,1280]{1,0:T(8,128)(2,1)S(1)} collective-permute-done((bf16[240,1280]{1,0:T(8,128)(2,1)S(1)}, bf16[240,1280]{1,0:T(8,128)(2,1)S(1)}, u32[]{:S(2)}, u32[]{:S(2)}) %collective-permute-start.36) | collective-permute-done | bytes 614432 | tf_op jit(solution)/shard_map/ppermute | solution.py:585
  408.7 3.5 collective-permute-done.40
  414.9 7.7 %collective-permute-done.41 = bf16[240,640]{1,0:T(8,128)(2,1)S(1)} collective-permute-done((bf16[240,640]{1,0:T(8,128)(2,1)S(1)}, bf16[240,640]{1,0:T(8,128)(2,1)S(1)}, u32[]{:S(2)}, u32[]{:S(2)}) %collective-permute-start.41) | collective-permute-done | bytes 307232 | tf_op jit(solution)/shard_map/ppermute | solution.py:585
  423.5 3.1 collective-permute-done.42
  452.8 6.7 %collective-permute-done.47.refs_1_ = bf16[240,1280]{1,0:T(8,128)(2,1)} collective-permute-done((bf16[240,1280]{1,0:T(8,128)(2,1)}, bf16[240,1280]{1,0:T(8,128)(2,1)}, u32[]{:S(2)}, u32[]{:S(2)}) %collective-permute-start.47) | collective-permute-done | bytes 614432 | tf_op jit(solution)/shard_map/ppermute | solution.py:585
  461.4 4.4 assemble.7
  465.8 5.0 %assemble.6 = (f32[480,960]{1,0:T(8,128)}, f32[480,960]{1,0:T(8,128)}, f32[320,480]{1,0:T(8,128)}, f32[320,480]{1,0:T(8,128)}) custom-call(s32[5]{0:T(128)S(1)} %stack.44.places_ref, bf16[240,1280]{1,0:T(8,128)(2,1)} %pad_maximum_fusion.7.refs_0_, bf16[240,1280]{1,0:T(8,128)(2,1)} %collective-permute-done.47.refs_1_, ...), custom_call_target="tpu_custom_call" | custom-call | bytes 7372800 | tf_op jit(solution)/shard_map/assemble/pallas_call | solution.py:507
  (384 shorter events, 175.9 us)
Async XLA Ops:
  7.9 21.9 %collective-permute-start.1 = (bf16[240,1600]{1,0:T(8,128)(2,1)}, bf16[240,1600]{1,0:T(8,128)(2,1)}, u32[]{:S(2)}, u32[]{:S(2)}) collective-permute-start(bf16[240,1600]{1,0:T(8,128)(2,1)} %concatenate.28), channel_id=1, source_target_pairs={{0,1},{1,0},{2,3},{3,2},{4,5},{5,4},{6,7},{7,6},{8,9},{9,8},{10,11... | collective-permute-start | bytes 2304008 | tf_op jit(solution)/shard_map/ppermute | solution.py:581
  12.7 37.5 %collective-permute-start = (bf16[240,960]{1,0:T(8,128)(2,1)}, bf16[240,960]{1,0:T(8,128)(2,1)}, u32[]{:S(2)}, u32[]{:S(2)}) collective-permute-start(bf16[240,960]{1,0:T(8,128)(2,1)} %constant_dynamic-slice_fusion.21), channel_id=1, source_target_pairs={{0,1},{1,0},{2,3},{3,2},{4,5},{5,4},{6,7},{7,6},{8,9},{9,8},{10,11... | collective-permute-start | bytes 1382408 | tf_op jit(solution)/shard_map/ppermute | solution.py:581
  12.8 27.6 %collective-permute-start.3 = (bf16[2,480]{1,0:T(2,128)(2,1)S(1)}, bf16[2,480]{1,0:T(2,128)(2,1)S(1)}, u32[]{:S(2)}, u32[]{:S(2)}) collective-permute-start(bf16[2,480]{1,0:T(2,128)(2,1)S(1)} %pad_maximum_fusion.8), channel_id=1, source_target_pairs={{0,1},{1,0},{2,3},{3,2},{4,5},{5,4},{6,7},{7,6},{8,9},{9,8},{10,11... | collective-permute-start | bytes 5768 | tf_op jit(solution)/shard_map/ppermute | solution.py:581
  15.7 37.8 %collective-permute-start.8 = (bf16[480,640]{1,0:T(8,128)(2,1)}, bf16[480,640]{1,0:T(8,128)(2,1)}, u32[]{:S(2)}, u32[]{:S(2)}) collective-permute-start(bf16[480,640]{1,0:T(8,128)(2,1)} %constant_dynamic-slice_fusion.20), channel_id=1, source_target_pairs={{0,1},{1,0},{2,3},{3,2},{4,5},{5,4},{6,7},{7,6},{8,9},{9,8},{10,11... | collective-permute-start | bytes 1843208 | tf_op jit(solution)/shard_map/ppermute | solution.py:581
  17.7 52.7 %collective-permute-start.11 = (bf16[480,640]{1,0:T(8,128)(2,1)}, bf16[480,640]{1,0:T(8,128)(2,1)}, u32[]{:S(2)}, u32[]{:S(2)}) collective-permute-start(bf16[480,640]{1,0:T(8,128)(2,1)} %constant_dynamic-slice_fusion.19), channel_id=1, source_target_pairs={{0,1},{1,0},{2,3},{3,2},{4,5},{5,4},{6,7},{7,6},{8,9},{9,8},{10,11... | collective-permute-start | bytes 1843208 | tf_op jit(solution)/shard_map/ppermute | solution.py:581
  53.6 16.8 %collective-permute-start.10 = (bf16[480,640]{1,0:T(8,128)(2,1)}, bf16[480,640]{1,0:T(8,128)(2,1)S(1)}, u32[]{:S(2)}, u32[]{:S(2)}) collective-permute-start(bf16[480,640]{1,0:T(8,128)(2,1)} %collective-permute-done.8.refs_1_), channel_id=1, source_target_pairs={{0,4},{2,6},{4,0},{6,2},{8,12},{10,14},{12,8},{14,10},{16,20},{18,... | collective-permute-start | bytes 1843208 | tf_op jit(solution)/shard_map/ppermute | solution.py:585
  56.8 22.2 %collective-permute-start.5 = (bf16[240,1280]{1,0:T(8,128)(2,1)S(1)}, bf16[240,1280]{1,0:T(8,128)(2,1)S(1)}, u32[]{:S(2)}, u32[]{:S(2)}) collective-permute-start(bf16[240,1280]{1,0:T(8,128)(2,1)S(1)} %constant_dynamic-slice_fusion.18), channel_id=1, source_target_pairs={{0,1},{1,0},{2,3},{3,2},{4,5},{5,4},{6,7},{7,6},{8,9},{9,8},{10,11... | collective-permute-start | bytes 1843208 | tf_op jit(solution)/shard_map/ppermute | solution.py:581
  58.3 20.6 %collective-permute-start.9 = (bf16[480,640]{1,0:T(8,128)(2,1)}, bf16[480,640]{1,0:T(8,128)(2,1)S(1)}, u32[]{:S(2)}, u32[]{:S(2)}) collective-permute-start(bf16[480,640]{1,0:T(8,128)(2,1)} %collective-permute-done.8.refs_1_), channel_id=1, source_target_pairs={{0,2},{2,0},{4,6},{6,4},{8,10},{10,8},{12,14},{14,12},{16,18},{18,... | collective-permute-start | bytes 1843208 | tf_op jit(solution)/shard_map/ppermute | solution.py:585
  70.5 16.5 %collective-permute-start.14 = (bf16[480,640]{1,0:T(8,128)(2,1)}, bf16[480,640]{1,0:T(8,128)(2,1)}, u32[]{:S(2)}, u32[]{:S(2)}) collective-permute-start(bf16[480,640]{1,0:T(8,128)(2,1)} %collective-permute-done.11.refs_1_), channel_id=1, source_target_pairs={{0,8},{2,10},{4,12},{6,14},{8,0},{10,2},{12,4},{14,6},{16,24},{18,... | collective-permute-start | bytes 1843208 | tf_op jit(solution)/shard_map/ppermute | solution.py:585
  72.1 16.3 %collective-permute-start.13 = (bf16[480,640]{1,0:T(8,128)(2,1)}, bf16[480,640]{1,0:T(8,128)(2,1)}, u32[]{:S(2)}, u32[]{:S(2)}) collective-permute-start(bf16[480,640]{1,0:T(8,128)(2,1)} %collective-permute-done.11.refs_1_), channel_id=1, source_target_pairs={{0,2},{2,0},{4,6},{6,4},{8,10},{10,8},{12,14},{14,12},{16,18},{18,... | collective-permute-start | bytes 1843208 | tf_op jit(solution)/shard_map/ppermute | solution.py:585
  87.3 19.9 %collective-permute-start.6 = (bf16[240,1280]{1,0:T(8,128)(2,1)S(1)}, bf16[240,1280]{1,0:T(8,128)(2,1)S(1)}, u32[]{:S(2)}, u32[]{:S(2)}) collective-permute-start(bf16[240,1280]{1,0:T(8,128)(2,1)S(1)} %collective-permute-done.5.refs_1_), channel_id=1, source_target_pairs={{0,2},{2,0},{4,6},{6,4},{8,10},{10,8},{12,14},{14,12},{16,18},{18,... | collective-permute-start | bytes 1843208 | tf_op jit(solution)/shard_map/ppermute | solution.py:585
  87.9 18.9 %collective-permute-start.7 = (bf16[240,1280]{1,0:T(8,128)(2,1)S(1)}, bf16[240,1280]{1,0:T(8,128)(2,1)S(1)}, u32[]{:S(2)}, u32[]{:S(2)}) collective-permute-start(bf16[240,1280]{1,0:T(8,128)(2,1)S(1)} %collective-permute-done.5.refs_1_), channel_id=1, source_target_pairs={{0,4},{2,6},{4,0},{6,2},{8,12},{10,14},{12,8},{14,10},{16,20},{18,... | collective-permute-start | bytes 1843208 | tf_op jit(solution)/shard_map/ppermute | solution.py:585
  225.4 30.5 %collective-permute-start.18 = (bf16[480,1280]{1,0:T(8,128)(2,1)}, bf16[480,1280]{1,0:T(8,128)(2,1)}, u32[]{:S(2)}, u32[]{:S(2)}) collective-permute-start(bf16[480,1280]{1,0:T(8,128)(2,1)} %fusion.19), channel_id=1, source_target_pairs={{0,1},{1,0},{2,3},{3,2},{4,5},{5,4},{6,7},{7,6},{8,9},{9,8},{10,11... | collective-permute-start | bytes 3686408 | tf_op jit(solution)/shard_map/ppermute | solution.py:581
  258.5 16.0 %collective-permute-start.19 = (bf16[240,1280]{1,0:T(8,128)(2,1)S(1)}, bf16[240,1280]{1,0:T(8,128)(2,1)S(1)}, u32[]{:S(2)}, u32[]{:S(2)}) collective-permute-start(bf16[240,1280]{1,0:T(8,128)(2,1)S(1)} %get-tuple-element.206), channel_id=1, source_target_pairs={{0,4},{2,6},{4,0},{6,2},{8,12},{10,14},{12,8},{14,10},{16,20},{18,... | collective-permute-start | bytes 1843208 | tf_op jit(solution)/shard_map/ppermute | solution.py:585
  279.8 16.6 %collective-permute-start.21 = (bf16[240,640]{1,0:T(8,128)(2,1)S(1)}, bf16[240,640]{1,0:T(8,128)(2,1)S(1)}, u32[]{:S(2)}, u32[]{:S(2)}) collective-permute-start(bf16[240,640]{1,0:T(8,128)(2,1)S(1)} %get-tuple-element.222), channel_id=1, source_target_pairs={{0,8},{2,10},{4,12},{6,14},{8,0},{10,2},{12,4},{14,6},{16,24},{18,... | collective-permute-start | bytes 921608 | tf_op jit(solution)/shard_map/ppermute | solution.py:585
  296.6 30.1 %collective-permute-start.24 = (bf16[480,1280]{1,0:T(8,128)(2,1)}, bf16[480,1280]{1,0:T(8,128)(2,1)S(1)}, u32[]{:S(2)}, u32[]{:S(2)}) collective-permute-start(bf16[480,1280]{1,0:T(8,128)(2,1)} %fusion.20), channel_id=1, source_target_pairs={{0,1},{1,0},{2,3},{3,2},{4,5},{5,4},{6,7},{7,6},{8,9},{9,8},{10,11... | collective-permute-start | bytes 3686408 | tf_op jit(solution)/shard_map/ppermute | solution.py:581
  298.1 23.6 %collective-permute-start.23 = (bf16[240,640]{1,0:T(8,128)(2,1)S(1)}, bf16[240,640]{1,0:T(8,128)(2,1)S(1)}, u32[]{:S(2)}, u32[]{:S(2)}) collective-permute-start(bf16[240,640]{1,0:T(8,128)(2,1)S(1)} %add_convert_fusion.17), channel_id=1, source_target_pairs={{0,16},{2,18},{4,20},{6,22},{8,24},{10,26},{12,28},{14,30},{16,0},... | collective-permute-start | bytes 921608 | tf_op jit(solution)/shard_map/ppermute | solution.py:585
  303.1 49.5 %collective-permute-start.27 = (bf16[480,1280]{1,0:T(8,128)(2,1)S(1)}, bf16[480,1280]{1,0:T(8,128)(2,1)}, u32[]{:S(2)}, u32[]{:S(2)}) collective-permute-start(bf16[480,1280]{1,0:T(8,128)(2,1)S(1)} %fusion.21), channel_id=1, source_target_pairs={{0,1},{1,0},{2,3},{3,2},{4,5},{5,4},{6,7},{7,6},{8,9},{9,8},{10,11... | collective-permute-start | bytes 3686408 | tf_op jit(solution)/shard_map/ppermute | solution.py:581
  328.2 16.9 %collective-permute-start.26 = (bf16[240,1280]{1,0:T(8,128)(2,1)}, bf16[240,1280]{1,0:T(8,128)(2,1)}, u32[]{:S(2)}, u32[]{:S(2)}) collective-permute-start(bf16[240,1280]{1,0:T(8,128)(2,1)} %get-tuple-element.204), channel_id=1, source_target_pairs={{0,4},{2,6},{4,0},{6,2},{8,12},{10,14},{12,8},{14,10},{16,20},{18,... | collective-permute-start | bytes 1843208 | tf_op jit(solution)/shard_map/ppermute | solution.py:585
  344.4 16.7 %collective-permute-start.29 = (bf16[240,1280]{1,0:T(8,128)(2,1)S(1)}, bf16[240,1280]{1,0:T(8,128)(2,1)S(1)}, u32[]{:S(2)}, u32[]{:S(2)}) collective-permute-start(bf16[240,1280]{1,0:T(8,128)(2,1)S(1)} %pad_maximum_fusion.4.refs_0_), channel_id=1, source_target_pairs={{0,4},{2,6},{4,0},{6,2},{8,12},{10,14},{12,8},{14,10},{16,20},{18,... | collective-permute-start | bytes 1843208 | tf_op jit(solution)/shard_map/ppermute | solution.py:585
  354.9 19.0 %collective-permute-start.31 = (bf16[240,1280]{1,0:T(8,128)(2,1)S(1)}, bf16[240,1280]{1,0:T(8,128)(2,1)S(1)}, u32[]{:S(2)}, u32[]{:S(2)}) collective-permute-start(bf16[240,1280]{1,0:T(8,128)(2,1)S(1)} %get-tuple-element.202), channel_id=1, source_target_pairs={{0,4},{2,6},{4,0},{6,2},{8,12},{10,14},{12,8},{14,10},{16,20},{18,... | collective-permute-start | bytes 1843208 | tf_op jit(solution)/shard_map/ppermute | solution.py:585
  355.8 28.3 %collective-permute-start.32 = (bf16[480,1280]{1,0:T(8,128)(2,1)S(1)}, bf16[480,1280]{1,0:T(8,128)(2,1)S(1)}, u32[]{:S(2)}, u32[]{:S(2)}) collective-permute-start(bf16[480,1280]{1,0:T(8,128)(2,1)S(1)} %fusion.22), channel_id=1, source_target_pairs={{0,1},{1,0},{2,3},{3,2},{4,5},{5,4},{6,7},{7,6},{8,9},{9,8},{10,11... | collective-permute-start | bytes 3686408 | tf_op jit(solution)/shard_map/ppermute | solution.py:581
  361.2 23.6 %collective-permute-start.33 = (bf16[240,640]{1,0:T(8,128)(2,1)S(1)}, bf16[240,640]{1,0:T(8,128)(2,1)S(1)}, u32[]{:S(2)}, u32[]{:S(2)}) collective-permute-start(bf16[240,640]{1,0:T(8,128)(2,1)S(1)} %add_convert_fusion.15), channel_id=1, source_target_pairs={{0,16},{2,18},{4,20},{6,22},{8,24},{10,26},{12,28},{14,30},{16,0},... | collective-permute-start | bytes 921608 | tf_op jit(solution)/shard_map/ppermute | solution.py:585
  385.4 18.2 %collective-permute-start.37 = (bf16[240,1280]{1,0:T(8,128)(2,1)S(1)}, bf16[240,1280]{1,0:T(8,128)(2,1)S(1)}, u32[]{:S(2)}, u32[]{:S(2)}) collective-permute-start(bf16[240,1280]{1,0:T(8,128)(2,1)S(1)} %pad_maximum_fusion.4.refs_0_), channel_id=1, source_target_pairs={{0,2},{2,0},{4,6},{6,4},{8,10},{10,8},{12,14},{14,12},{16,18},{18,... | collective-permute-start | bytes 1843208 | tf_op jit(solution)/shard_map/ppermute | solution.py:585
  385.4 18.2 %collective-permute-start.38 = (bf16[240,1280]{1,0:T(8,128)(2,1)S(1)}, bf16[240,1280]{1,0:T(8,128)(2,1)S(1)}, u32[]{:S(2)}, u32[]{:S(2)}) collective-permute-start(bf16[240,1280]{1,0:T(8,128)(2,1)S(1)} %collective-permute-done.29.refs_1_), channel_id=1, source_target_pairs={{0,2},{2,0},{4,6},{6,4},{8,10},{10,8},{12,14},{14,12},{16,18},{18,... | collective-permute-start | bytes 1843208 | tf_op jit(solution)/shard_map/ppermute | solution.py:585
  385.9 15.8 %collective-permute-start.36 = (bf16[240,1280]{1,0:T(8,128)(2,1)S(1)}, bf16[240,1280]{1,0:T(8,128)(2,1)S(1)}, u32[]{:S(2)}, u32[]{:S(2)}) collective-permute-start(bf16[240,1280]{1,0:T(8,128)(2,1)S(1)} %get-tuple-element.200), channel_id=1, source_target_pairs={{0,4},{2,6},{4,0},{6,2},{8,12},{10,14},{12,8},{14,10},{16,20},{18,... | collective-permute-start | bytes 1843208 | tf_op jit(solution)/shard_map/ppermute | solution.py:585
  387.4 19.3 %collective-permute-start.39 = (bf16[240,640]{1,0:T(8,128)(2,1)S(1)}, bf16[240,640]{1,0:T(8,128)(2,1)S(1)}, u32[]{:S(2)}, u32[]{:S(2)}) collective-permute-start(bf16[240,640]{1,0:T(8,128)(2,1)S(1)} %add_convert_fusion.13), channel_id=1, source_target_pairs={{0,16},{2,18},{4,20},{6,22},{8,24},{10,26},{12,28},{14,30},{16,0},... | collective-permute-start | bytes 921608 | tf_op jit(solution)/shard_map/ppermute | solution.py:585
  406.8 15.8 %collective-permute-start.41 = (bf16[240,640]{1,0:T(8,128)(2,1)S(1)}, bf16[240,640]{1,0:T(8,128)(2,1)S(1)}, u32[]{:S(2)}, u32[]{:S(2)}) collective-permute-start(bf16[240,640]{1,0:T(8,128)(2,1)S(1)} %add_convert_fusion.12), channel_id=1, source_target_pairs={{0,8},{2,10},{4,12},{6,14},{8,0},{10,2},{12,4},{14,6},{16,24},{18,... | collective-permute-start | bytes 921608 | tf_op jit(solution)/shard_map/ppermute | solution.py:585
  407.3 19.5 %collective-permute-start.43 = (bf16[240,1280]{1,0:T(8,128)(2,1)S(1)}, bf16[240,1280]{1,0:T(8,128)(2,1)S(1)}, u32[]{:S(2)}, u32[]{:S(2)}) collective-permute-start(bf16[240,1280]{1,0:T(8,128)(2,1)S(1)} %pad_maximum_fusion.5.refs_0_), channel_id=1, source_target_pairs={{0,4},{2,6},{4,0},{6,2},{8,12},{10,14},{12,8},{14,10},{16,20},{18,... | collective-permute-start | bytes 1843208 | tf_op jit(solution)/shard_map/ppermute | solution.py:585
  408.7 22.3 %collective-permute-start.44 = (bf16[240,1280]{1,0:T(8,128)(2,1)S(1)}, bf16[240,1280]{1,0:T(8,128)(2,1)S(1)}, u32[]{:S(2)}, u32[]{:S(2)}) collective-permute-start(bf16[240,1280]{1,0:T(8,128)(2,1)S(1)} %pad_maximum_fusion.5.refs_0_), channel_id=1, source_target_pairs={{0,2},{2,0},{4,6},{6,4},{8,10},{10,8},{12,14},{14,12},{16,18},{18,... | collective-permute-start | bytes 1843208 | tf_op jit(solution)/shard_map/ppermute | solution.py:585
  430.4 22.4 %collective-permute-start.48 = (bf16[240,1280]{1,0:T(8,128)(2,1)}, bf16[240,1280]{1,0:T(8,128)(2,1)}, u32[]{:S(2)}, u32[]{:S(2)}) collective-permute-start(bf16[240,1280]{1,0:T(8,128)(2,1)} %pad_maximum_fusion.6.refs_0_), channel_id=1, source_target_pairs={{0,4},{2,6},{4,0},{6,2},{8,12},{10,14},{12,8},{14,10},{16,20},{18,... | collective-permute-start | bytes 1843208 | tf_op jit(solution)/shard_map/ppermute | solution.py:585
  441.0 18.5 %collective-permute-start.47 = (bf16[240,1280]{1,0:T(8,128)(2,1)}, bf16[240,1280]{1,0:T(8,128)(2,1)}, u32[]{:S(2)}, u32[]{:S(2)}) collective-permute-start(bf16[240,1280]{1,0:T(8,128)(2,1)} %pad_maximum_fusion.7.refs_0_), channel_id=1, source_target_pairs={{0,4},{2,6},{4,0},{6,2},{8,12},{10,14},{12,8},{14,10},{16,20},{18,... | collective-permute-start | bytes 1843208 | tf_op jit(solution)/shard_map/ppermute | solution.py:585
  (115 other events, 929.4 us)

commit v4 on v3

--- a/solution.py
+++ b/solution.py
@@ -947,7 +947,8 @@
         value_end = key_end + value_projection.shape[1]
         cuts = ((0, width), (width, 2 * width), (2 * width, width + key_end), (width + key_end, width + value_end))
         if paired:
-            queue.append(grad)
+            grad_narrow = grad.T.astype(BF16)[None]
+            queue.append(grad_narrow)
             down.step(queue)
             gate.step(queue)
             up.step(queue)
@@ -963,17 +964,18 @@
             up.step(queue)
             mixed.step(queue)
             gate.step(queue)
+            mixed.step(queue)
             (grad_gate,) = assemble(places, [after(gate.pieces[0], *queue), *gate.pieces[1:]], False)
             queue.append(grad_gate)
-            mixed.step(queue)
             up.step(queue)
-            mixed.step(queue)
             (grad_up,) = assemble(places, [after(up.pieces[0], *queue), *up.pieces[1:]], False)
             queue.append(grad_up)
+            mixed.step(queue)
             grad_out, grad_query, grad_key, grad_value = assemble(places, mixed.pieces, False, cuts)
             grad_key, grad_value = grad_key.T, grad_value.T
             gain_grads = reduce_vector(gain_grads).astype(F32)
         else:
+            grad_narrow = grad.T.astype(BF16)[None]
 
             def reduce(value, axis):
                 part = lax.psum_scatter(value, "fsdp", scatter_dimension=axis, tiled=True)
@@ -989,7 +991,7 @@
             gain_grads = reduce(gain_grads, 1)
         return (
             outputs.T.astype(BF16)[None],
-            grad.T.astype(BF16)[None],
+            grad_narrow,
             grad_query,
             grad_key,
             grad_value,

time: 480 us -> 476 us (level)
    unnamed x180 -> x168, local copies, waits for them, and re-layouts: 39 us -> 33.1 us
  transfers between devices with their start and end apart: 58 -> 58, of which waited for: 23 -> 25; matrix products, arithmetic and copies ran while one was open for 9% -> 9% of each run, Pallas kernels for 25% -> 25%
where the time goes in v4:
time: 476 us; the launch traced here: 468 us
  Pallas kernels  202 us (42%)
  waiting for transfers between devices  105 us (22%)
  starting transfers between devices  54.5 us (11%)
  local copies, waits for them, and re-layouts  48.1 us (10%)
  matrix products  29.6 us (6%)
  other arithmetic  26 us (5%)
    ppermute x47, waiting for transfers between devices, swap_dp(): return lax.ppermute(value, 'dp', [(i, i ^ bit) for i in range(size)])  64.5 us
    pallas_call x2, Pallas kernels, ffn_back(): pl.pallas_call(ffn_back_kernel, grid=(hidden // CHUNK,), in_specs=[full,...  49.3 us
    ppermute x11, waiting for transfers between devices, swap_fsdp(): return lax.ppermute(value, 'fsdp', [(0, 1), (1, 0)])  40.6 us
    ppermute x47, starting transfers between devices, swap_dp(): return lax.ppermute(value, 'dp', [(i, i ^ bit) for i in range(size)])  39.2 us
    pallas_call x3, Pallas kernels, weight_grad(): pl.pallas_call(partial(weight_grad_kernel, left_fsdp, False), grid_spec=p...  37.7 us
    unnamed x168, local copies, waits for them, and re-layouts  33.1 us
    dot_general x9, matrix products, dot(): lax.dot_general(left, right, ((contract[:1], contract[1:]), ((), ())), pr...  29.6 us
    pallas_call x2, Pallas kernels, attention_back(): pl.pallas_call(attention_back_kernel, grid=(KEY_VALUE_HEADS,), in_specs=[...  28.7 us
  transfers between devices with their start and end apart: 58, of which 25 were waited for; matrix products, arithmetic and copies ran while one was open for 9% of the time, Pallas kernels for 25%

profile of v4, /device:TPU:0, one launch (start us, length us, event | category | flops | bytes accessed | tf_op | source)
XLA Modules:
  0.0 467.7 jit_solution(15266522781960809671)
XLA Ops:
  22.9 6.9 %collective-permute-done.1.refs_3_ = bf16[240,1600]{1,0:T(8,128)(2,1)} collective-permute-done((bf16[240,1600]{1,0:T(8,128)(2,1)}, bf16[240,1600]{1,0:T(8,128)(2,1)}, u32[]{:S(2)}, u32[]{:S(2)}) %collective-permute-start.1) | collective-permute-done | bytes 768032 | tf_op jit(solution)/shard_map/ppermute | solution.py:581
  29.8 10.5 %collective-permute-done.3 = bf16[2,480]{1,0:T(2,128)(2,1)S(1)} collective-permute-done((bf16[2,480]{1,0:T(2,128)(2,1)S(1)}, bf16[2,480]{1,0:T(2,128)(2,1)S(1)}, u32[]{:S(2)}, u32[]{:S(2)}) %collective-permute-start.3) | collective-permute-done | bytes 1952 | tf_op jit(solution)/shard_map/ppermute | solution.py:581
  50.3 3.3 collective-permute-done.8.refs_1_
  58.8 11.5 %attention.2 = (bf16[960,768]{1,0:T(8,128)(2,1)S(1)}, f32[5,8,768]{2,1,0:T(8,128)S(1)}) custom-call(s32[1,768]{1,0:T(1,128)S(1)} %reduce_sum.75.start_ref, bf16[1600,768]{1,0:T(8,128)(2,1)S(1)} %pad_maximum_fusion.query_ref.key_ref.value_ref, bf16[1600,768]{1,0:T(8,128)(2,1)S(1)} %pad_maximum_fusion.query_ref.key_ref.value_ref, ...), custom_call_target="tpu_custom_call" | custom-call | flops 6000000000 | bytes 4000000 | tf_op jit(solution)/shard_map/attention/pallas_call | solution.py:80
  74.0 3.4 fusion.3.middle_ref
  83.2 3.9 collective-permute-done.14.refs_3_
  93.7 13.1 %ffn_up.1 = (bf16[960,768]{1,0:T(8,128)(2,1)}, bf16[768,2560]{1,0:T(8,128)(2,1)}, bf16[768,2560]{1,0:T(8,128)(2,1)}, bf16[768,2560]{1,0:T(8,128)(2,1)}) custom-call(f32[960,768]{1,0:T(8,128)S(1)} %copy-done.35, f32[960,1]{1,0:T(8,128)S(1)} %copy.49.gain_ref, bf16[960,2560]{1,0:T(8,128)(2,1)S(1)} %bitcast.122, bf16[960,2560]{1,0:T(8,128)(2,1)S(1)} %join.8.up_w_ref), custom_call_target="tpu_custom_call" | custom-call | flops 7549747200 | bytes 30000000 | tf_op jit(solution)/shard_map/ffn_up/pallas_call | solution.py:280
  109.8 7.9 %multiply_reduce_fusion.2 = (f32[768]{0:T(1024)S(1)}, f32[960,768]{1,0:T(8,128)S(1)}) fusion(f32[960,768]{1,0:T(8,128)S(1)} %copy-done.35, bf16[960,2560]{1,0:T(8,128)(2,1)S(1)} %join.9.down_w_ref, bf16[768,2560]{1,0:T(8,128)(2,1)} %get-tuple-element.113.right2_ref), kind=kOutput, calls=%fused_computation.22 | convolution fusion | flops 3777084672 | bytes 14748672 | tf_op jit(solution)/shard_map/dot_general | solution.py:31
  124.9 11.3 %attention.3 = (bf16[960,768]{1,0:T(8,128)(2,1)S(1)}, f32[5,8,768]{2,1,0:T(8,128)S(1)}) custom-call(s32[1,768]{1,0:T(1,128)S(1)} %reduce_sum.75.start_ref, bf16[1600,768]{1,0:T(8,128)(2,1)S(1)} %pad_maximum_fusion.1.query_ref.key_ref.value_ref, bf16[1600,768]{1,0:T(8,128)(2,1)S(1)} %pad_maximum_fusion.1.query_ref.key_ref.value_ref, ...), custom_call_target="tpu_custom_call" | custom-call | flops 6000000000 | bytes 4000000 | tf_op jit(solution)/shard_map/attention/pallas_call | solution.py:80
  138.8 16.3 %ffn.1 = (f32[960,768]{1,0:T(8,128)S(1)}, bf16[960,768]{1,0:T(8,128)(2,1)}, bf16[768,2560]{1,0:T(8,128)(2,1)}, bf16[768,2560]{1,0:T(8,128)(2,1)}, bf16[768,2560]{1,0:T(8,128)(2,1)}) custom-call(f32[960,768]{1,0:T(8,128)S(1)} %convolution_add_fusion.middle_ref, f32[960,1]{1,0:T(8,128)S(1)} %copy-done.33, bf16[960,2560]{1,0:T(8,128)(2,1)S(1)} %bitcast.122, ...), custom_call_target="tpu_custom_call" | custom-call | flops 11324620800 | bytes 40000000 | tf_op jit(solution)/shard_map/ffn/pallas_call | solution.py:233
  158.7 24.3 %ffn_back.2 = (f32[960,768]{1,0:T(8,128)}, bf16[960,768]{1,0:T(8,128)(2,1)S(1)}, bf16[768,2560]{1,0:T(8,128)(2,1)}, bf16[768,2560]{1,0:T(8,128)(2,1)}, f32[960,1]{1,0:T(8,128)S(1)}, /*index=5*/bf16[960,768]{1,0:T(8,128)(2,1)}) custom-call(f32[960,768]{1,0:T(8,128)S(1)} %convert_bitcast_fusion.grad_ref, f32[960,768]{1,0:T(8,128)S(1)} %convolution_add_fusion.middle_ref, ...), custom_call_target="tpu_custom_call" | custom-call | flops 11324620800 | bytes 50000000 | tf_op jit(solution)/shard_map/ffn_back/pallas_call | solution.py:350
  185.1 14.4 %attention_back.2.qkv_ref = bf16[1600,768]{1,0:T(8,128)(2,1)S(1)} custom-call(s32[1,768]{1,0:T(1,128)S(1)} %reduce_sum.75.start_ref, f32[32,768]{1,0:T(8,128)S(1)} %get-tuple-element.225.cosine_ref, f32[32,768]{1,0:T(8,128)S(1)} %get-tuple-element.226.sine_ref, bf16[1600,768]{1,0:T(8,128)(2,1)S(1)} %pad_maximum_fusion.1.query_ref.key_ref.value_ref, ...), custom_call_target="tpu_custom_call" | custom-call | flops 8999999488 | bytes 9000000 | tf_op jit(solution)/shard_map/attention_back/pallas_call | solution.py:158
  206.4 12.3 %weight_grad.3 = (bf16[2,480,1280]{2,1,0:T(8,128)(2,1)S(1)}, bf16[2,480,1280]{2,1,0:T(8,128)(2,1)S(1)}) custom-call(s32[5]{0:T(128)S(1)} %stack.44.places_ref, bf16[960,768]{1,0:T(8,128)(2,1)S(1)} %copy-done.58, bf16[768,2560]{1,0:T(8,128)(2,1)S(1)} %copy-done.57, bf16[960,768]{1,0:T(8,128)(2,1)S(1)} %get-tuple-element.193.left2_ref, ...), custom_call_target="tpu_custom_call" | custom-call | flops 7549747200 | bytes 24576000 | tf_op jit(solution)/shard_map/weight_grad/pallas_call | solution.py:416
  218.9 4.6 collective-permute-done.17
  230.9 25.0 %ffn_back.3 = (f32[960,768]{1,0:T(8,128)}, bf16[960,768]{1,0:T(8,128)(2,1)S(1)}, bf16[768,2560]{1,0:T(8,128)(2,1)}, bf16[768,2560]{1,0:T(8,128)(2,1)}, f32[960,1]{1,0:T(8,128)S(1)}, /*index=5*/bf16[960,768]{1,0:T(8,128)(2,1)}) custom-call(f32[960,768]{1,0:T(8,128)S(1)} %get-tuple-element.127.grad_ref, f32[960,768]{1,0:T(8,128)S(1)} %copy-done.36, ...), custom_call_target="tpu_custom_call" | custom-call | flops 11324620800 | bytes 50000000 | tf_op jit(solution)/shard_map/ffn_back/pallas_call | solution.py:350
  262.3 12.2 %weight_grad.4 = (bf16[2,480,1280]{2,1,0:T(8,128)(2,1)S(1)}, bf16[2,480,1280]{2,1,0:T(8,128)(2,1)S(1)}) custom-call(s32[5]{0:T(128)S(1)} %stack.44.places_ref, bf16[960,768]{1,0:T(8,128)(2,1)S(1)} %copy-done.60, bf16[768,2560]{1,0:T(8,128)(2,1)S(1)} %copy-done.52, bf16[960,768]{1,0:T(8,128)(2,1)S(1)} %copy-done.59, bf16[768,2560]{1,0:T(8,128)(2,1)S(1)} %copy-done.54), custom_call_target="tpu_custom_call" | custom-call | flops 7549747200 | bytes 24576000 | tf_op jit(solution)/shard_map/weight_grad/pallas_call | solution.py:416
  283.2 13.2 %weight_grad.5 = (bf16[2,480,1280]{2,1,0:T(8,128)(2,1)S(1)}, bf16[2,480,1280]{2,1,0:T(8,128)(2,1)}) custom-call(s32[5]{0:T(128)S(1)} %stack.44.places_ref, bf16[960,768]{1,0:T(8,128)(2,1)S(1)} %copy-done.60, bf16[768,2560]{1,0:T(8,128)(2,1)S(1)} %copy-done.51, bf16[960,768]{1,0:T(8,128)(2,1)S(1)} %copy-done.59, bf16[768,2560]{1,0:T(8,128)(2,1)S(1)} %copy-done.53), custom_call_target="tpu_custom_call" | custom-call | flops 7549747200 | bytes 24576000 | tf_op jit(solution)/shard_map/weight_grad/pallas_call | solution.py:416
  308.5 14.3 %attention_back.3.qkv2_ref = bf16[1600,768]{1,0:T(8,128)(2,1)S(1)} custom-call(s32[1,768]{1,0:T(1,128)S(1)} %reduce_sum.75.start_ref, f32[32,768]{1,0:T(8,128)S(1)} %get-tuple-element.225.cosine_ref, f32[32,768]{1,0:T(8,128)S(1)} %get-tuple-element.226.sine_ref, bf16[1600,768]{1,0:T(8,128)(2,1)S(1)} %copy-done.16, bf16[1600,768]{1,0:T(8,128)(2,1)S(1)} %copy-done.16, ...), custom_call_target="tpu_custom_call" | custom-call | flops 8999999488 | bytes 9000000 | tf_op jit(solution)/shard_map/attention_back/pallas_call | solution.py:158
  322.9 3.8 collective-permute-done.24
  330.2 10.8 %mixed_grad.1 = (bf16[2,480,1280]{2,1,0:T(8,128)(2,1)S(1)}, bf16[2,480,1280]{2,1,0:T(8,128)(2,1)S(1)}) custom-call(s32[5]{0:T(128)S(1)} %stack.44.places_ref, bf16[960,768]{1,0:T(8,128)(2,1)S(1)} %copy-done.39, bf16[960,768]{1,0:T(8,128)(2,1)S(1)} %copy-done.46, bf16[960,768]{1,0:T(8,128)(2,1)S(1)} %copy-done.25, bf16[1600,768]{1,0:T(8,128)(2,1)S(1)} %copy-done.44, ...), custom_call_target="tpu_custom_call" | custom-call | flops 7549747200 | bytes 24576000 | tf_op jit(solution)/shard_map/mixed_grad/pallas_call | solution.py:462
  346.8 5.8 %collective-permute-done.27 = bf16[480,1280]{1,0:T(8,128)(2,1)} collective-permute-done((bf16[480,1280]{1,0:T(8,128)(2,1)}, bf16[480,1280]{1,0:T(8,128)(2,1)}, u32[]{:S(2)}, u32[]{:S(2)}) %collective-permute-start.27) | collective-permute-done | bytes 1228832 | tf_op jit(solution)/shard_map/ppermute | solution.py:581
  363.9 10.0 %collective-permute-done.31 = bf16[240,1280]{1,0:T(8,128)(2,1)S(1)} collective-permute-done((bf16[240,1280]{1,0:T(8,128)(2,1)S(1)}, bf16[240,1280]{1,0:T(8,128)(2,1)S(1)}, u32[]{:S(2)}, u32[]{:S(2)}) %collective-permute-start.31) | collective-permute-done | bytes 614432 | tf_op jit(solution)/shard_map/ppermute | solution.py:585
  375.5 8.8 %collective-permute-done.32 = bf16[480,1280]{1,0:T(8,128)(2,1)S(1)} collective-permute-done((bf16[480,1280]{1,0:T(8,128)(2,1)S(1)}, bf16[480,1280]{1,0:T(8,128)(2,1)S(1)}, u32[]{:S(2)}, u32[]{:S(2)}) %collective-permute-start.32) | collective-permute-done | bytes 1228832 | tf_op jit(solution)/shard_map/ppermute | solution.py:581
  395.4 7.7 %collective-permute-done.36 = bf16[240,1280]{1,0:T(8,128)(2,1)S(1)} collective-permute-done((bf16[240,1280]{1,0:T(8,128)(2,1)}, bf16[240,1280]{1,0:T(8,128)(2,1)S(1)}, u32[]{:S(2)}, u32[]{:S(2)}) %collective-permute-start.36) | collective-permute-done | bytes 614432 | tf_op jit(solution)/shard_map/ppermute | solution.py:585
  410.2 3.4 collective-permute-done.40
  416.3 7.9 %collective-permute-done.41 = bf16[240,640]{1,0:T(8,128)(2,1)S(1)} collective-permute-done((bf16[240,640]{1,0:T(8,128)(2,1)S(1)}, bf16[240,640]{1,0:T(8,128)(2,1)S(1)}, u32[]{:S(2)}, u32[]{:S(2)}) %collective-permute-start.41) | collective-permute-done | bytes 307232 | tf_op jit(solution)/shard_map/ppermute | solution.py:585
  424.3 4.5 collective-permute-done.42
  432.1 3.8 collective-permute-done.44
  439.9 6.7 %collective-permute-done.46.refs_1_ = bf16[240,1280]{1,0:T(8,128)(2,1)S(1)} collective-permute-done((bf16[240,1280]{1,0:T(8,128)(2,1)S(1)}, bf16[240,1280]{1,0:T(8,128)(2,1)S(1)}, u32[]{:S(2)}, u32[]{:S(2)}) %collective-permute-start.46) | collective-permute-done | bytes 614432 | tf_op jit(solution)/shard_map/ppermute | solution.py:585
  450.4 3.4 collective-permute-start.56
  457.0 4.2 assemble.6
  463.7 3.8 assemble.7
  (372 shorter events, 172.6 us)
Async XLA Ops:
  7.9 21.9 %collective-permute-start.1 = (bf16[240,1600]{1,0:T(8,128)(2,1)}, bf16[240,1600]{1,0:T(8,128)(2,1)}, u32[]{:S(2)}, u32[]{:S(2)}) collective-permute-start(bf16[240,1600]{1,0:T(8,128)(2,1)} %concatenate.28), channel_id=1, source_target_pairs={{0,1},{1,0},{2,3},{3,2},{4,5},{5,4},{6,7},{7,6},{8,9},{9,8},{10,11... | collective-permute-start | bytes 2304008 | tf_op jit(solution)/shard_map/ppermute | solution.py:581
  12.7 37.6 %collective-permute-start = (bf16[240,960]{1,0:T(8,128)(2,1)}, bf16[240,960]{1,0:T(8,128)(2,1)}, u32[]{:S(2)}, u32[]{:S(2)}) collective-permute-start(bf16[240,960]{1,0:T(8,128)(2,1)} %constant_dynamic-slice_fusion.21), channel_id=1, source_target_pairs={{0,1},{1,0},{2,3},{3,2},{4,5},{5,4},{6,7},{7,6},{8,9},{9,8},{10,11... | collective-permute-start | bytes 1382408 | tf_op jit(solution)/shard_map/ppermute | solution.py:581
  12.8 27.6 %collective-permute-start.3 = (bf16[2,480]{1,0:T(2,128)(2,1)S(1)}, bf16[2,480]{1,0:T(2,128)(2,1)S(1)}, u32[]{:S(2)}, u32[]{:S(2)}) collective-permute-start(bf16[2,480]{1,0:T(2,128)(2,1)S(1)} %pad_maximum_fusion.8), channel_id=1, source_target_pairs={{0,1},{1,0},{2,3},{3,2},{4,5},{5,4},{6,7},{7,6},{8,9},{9,8},{10,11... | collective-permute-start | bytes 5768 | tf_op jit(solution)/shard_map/ppermute | solution.py:581
  15.7 37.8 %collective-permute-start.8 = (bf16[480,640]{1,0:T(8,128)(2,1)}, bf16[480,640]{1,0:T(8,128)(2,1)}, u32[]{:S(2)}, u32[]{:S(2)}) collective-permute-start(bf16[480,640]{1,0:T(8,128)(2,1)} %constant_dynamic-slice_fusion.20), channel_id=1, source_target_pairs={{0,1},{1,0},{2,3},{3,2},{4,5},{5,4},{6,7},{7,6},{8,9},{9,8},{10,11... | collective-permute-start | bytes 1843208 | tf_op jit(solution)/shard_map/ppermute | solution.py:581
  17.7 52.7 %collective-permute-start.11 = (bf16[480,640]{1,0:T(8,128)(2,1)}, bf16[480,640]{1,0:T(8,128)(2,1)}, u32[]{:S(2)}, u32[]{:S(2)}) collective-permute-start(bf16[480,640]{1,0:T(8,128)(2,1)} %constant_dynamic-slice_fusion.19), channel_id=1, source_target_pairs={{0,1},{1,0},{2,3},{3,2},{4,5},{5,4},{6,7},{7,6},{8,9},{9,8},{10,11... | collective-permute-start | bytes 1843208 | tf_op jit(solution)/shard_map/ppermute | solution.py:581
  53.6 16.8 %collective-permute-start.10 = (bf16[480,640]{1,0:T(8,128)(2,1)}, bf16[480,640]{1,0:T(8,128)(2,1)S(1)}, u32[]{:S(2)}, u32[]{:S(2)}) collective-permute-start(bf16[480,640]{1,0:T(8,128)(2,1)} %collective-permute-done.8.refs_1_), channel_id=1, source_target_pairs={{0,4},{2,6},{4,0},{6,2},{8,12},{10,14},{12,8},{14,10},{16,20},{18,... | collective-permute-start | bytes 1843208 | tf_op jit(solution)/shard_map/ppermute | solution.py:585
  56.8 22.2 %collective-permute-start.5 = (bf16[240,1280]{1,0:T(8,128)(2,1)S(1)}, bf16[240,1280]{1,0:T(8,128)(2,1)S(1)}, u32[]{:S(2)}, u32[]{:S(2)}) collective-permute-start(bf16[240,1280]{1,0:T(8,128)(2,1)S(1)} %constant_dynamic-slice_fusion.18), channel_id=1, source_target_pairs={{0,1},{1,0},{2,3},{3,2},{4,5},{5,4},{6,7},{7,6},{8,9},{9,8},{10,11... | collective-permute-start | bytes 1843208 | tf_op jit(solution)/shard_map/ppermute | solution.py:581
  58.3 20.6 %collective-permute-start.9 = (bf16[480,640]{1,0:T(8,128)(2,1)}, bf16[480,640]{1,0:T(8,128)(2,1)S(1)}, u32[]{:S(2)}, u32[]{:S(2)}) collective-permute-start(bf16[480,640]{1,0:T(8,128)(2,1)} %collective-permute-done.8.refs_1_), channel_id=1, source_target_pairs={{0,2},{2,0},{4,6},{6,4},{8,10},{10,8},{12,14},{14,12},{16,18},{18,... | collective-permute-start | bytes 1843208 | tf_op jit(solution)/shard_map/ppermute | solution.py:585
  70.5 16.5 %collective-permute-start.14 = (bf16[480,640]{1,0:T(8,128)(2,1)}, bf16[480,640]{1,0:T(8,128)(2,1)}, u32[]{:S(2)}, u32[]{:S(2)}) collective-permute-start(bf16[480,640]{1,0:T(8,128)(2,1)} %collective-permute-done.11.refs_1_), channel_id=1, source_target_pairs={{0,8},{2,10},{4,12},{6,14},{8,0},{10,2},{12,4},{14,6},{16,24},{18,... | collective-permute-start | bytes 1843208 | tf_op jit(solution)/shard_map/ppermute | solution.py:585
  72.1 16.3 %collective-permute-start.13 = (bf16[480,640]{1,0:T(8,128)(2,1)}, bf16[480,640]{1,0:T(8,128)(2,1)}, u32[]{:S(2)}, u32[]{:S(2)}) collective-permute-start(bf16[480,640]{1,0:T(8,128)(2,1)} %collective-permute-done.11.refs_1_), channel_id=1, source_target_pairs={{0,2},{2,0},{4,6},{6,4},{8,10},{10,8},{12,14},{14,12},{16,18},{18,... | collective-permute-start | bytes 1843208 | tf_op jit(solution)/shard_map/ppermute | solution.py:585
  87.3 19.9 %collective-permute-start.6 = (bf16[240,1280]{1,0:T(8,128)(2,1)S(1)}, bf16[240,1280]{1,0:T(8,128)(2,1)S(1)}, u32[]{:S(2)}, u32[]{:S(2)}) collective-permute-start(bf16[240,1280]{1,0:T(8,128)(2,1)S(1)} %collective-permute-done.5.refs_1_), channel_id=1, source_target_pairs={{0,2},{2,0},{4,6},{6,4},{8,10},{10,8},{12,14},{14,12},{16,18},{18,... | collective-permute-start | bytes 1843208 | tf_op jit(solution)/shard_map/ppermute | solution.py:585
  87.9 18.9 %collective-permute-start.7 = (bf16[240,1280]{1,0:T(8,128)(2,1)S(1)}, bf16[240,1280]{1,0:T(8,128)(2,1)S(1)}, u32[]{:S(2)}, u32[]{:S(2)}) collective-permute-start(bf16[240,1280]{1,0:T(8,128)(2,1)S(1)} %collective-permute-done.5.refs_1_), channel_id=1, source_target_pairs={{0,4},{2,6},{4,0},{6,2},{8,12},{10,14},{12,8},{14,10},{16,20},{18,... | collective-permute-start | bytes 1843208 | tf_op jit(solution)/shard_map/ppermute | solution.py:585
  225.4 30.5 %collective-permute-start.18 = (bf16[480,1280]{1,0:T(8,128)(2,1)}, bf16[480,1280]{1,0:T(8,128)(2,1)}, u32[]{:S(2)}, u32[]{:S(2)}) collective-permute-start(bf16[480,1280]{1,0:T(8,128)(2,1)} %fusion.21), channel_id=1, source_target_pairs={{0,1},{1,0},{2,3},{3,2},{4,5},{5,4},{6,7},{7,6},{8,9},{9,8},{10,11... | collective-permute-start | bytes 3686408 | tf_op jit(solution)/shard_map/ppermute | solution.py:581
  258.5 16.0 %collective-permute-start.19 = (bf16[240,1280]{1,0:T(8,128)(2,1)S(1)}, bf16[240,1280]{1,0:T(8,128)(2,1)S(1)}, u32[]{:S(2)}, u32[]{:S(2)}) collective-permute-start(bf16[240,1280]{1,0:T(8,128)(2,1)S(1)} %get-tuple-element.206), channel_id=1, source_target_pairs={{0,4},{2,6},{4,0},{6,2},{8,12},{10,14},{12,8},{14,10},{16,20},{18,... | collective-permute-start | bytes 1843208 | tf_op jit(solution)/shard_map/ppermute | solution.py:585
  279.8 16.6 %collective-permute-start.21 = (bf16[240,640]{1,0:T(8,128)(2,1)S(1)}, bf16[240,640]{1,0:T(8,128)(2,1)S(1)}, u32[]{:S(2)}, u32[]{:S(2)}) collective-permute-start(bf16[240,640]{1,0:T(8,128)(2,1)S(1)} %get-tuple-element.222), channel_id=1, source_target_pairs={{0,8},{2,10},{4,12},{6,14},{8,0},{10,2},{12,4},{14,6},{16,24},{18,... | collective-permute-start | bytes 921608 | tf_op jit(solution)/shard_map/ppermute | solution.py:585
  296.6 30.1 %collective-permute-start.24 = (bf16[480,1280]{1,0:T(8,128)(2,1)}, bf16[480,1280]{1,0:T(8,128)(2,1)S(1)}, u32[]{:S(2)}, u32[]{:S(2)}) collective-permute-start(bf16[480,1280]{1,0:T(8,128)(2,1)} %fusion.22), channel_id=1, source_target_pairs={{0,1},{1,0},{2,3},{3,2},{4,5},{5,4},{6,7},{7,6},{8,9},{9,8},{10,11... | collective-permute-start | bytes 3686408 | tf_op jit(solution)/shard_map/ppermute | solution.py:581
  298.1 24.6 %collective-permute-start.23 = (bf16[240,640]{1,0:T(8,128)(2,1)S(1)}, bf16[240,640]{1,0:T(8,128)(2,1)S(1)}, u32[]{:S(2)}, u32[]{:S(2)}) collective-permute-start(bf16[240,640]{1,0:T(8,128)(2,1)S(1)} %add_convert_fusion.17), channel_id=1, source_target_pairs={{0,16},{2,18},{4,20},{6,22},{8,24},{10,26},{12,28},{14,30},{16,0},... | collective-permute-start | bytes 921608 | tf_op jit(solution)/shard_map/ppermute | solution.py:585
  304.2 48.4 %collective-permute-start.27 = (bf16[480,1280]{1,0:T(8,128)(2,1)}, bf16[480,1280]{1,0:T(8,128)(2,1)}, u32[]{:S(2)}, u32[]{:S(2)}) collective-permute-start(bf16[480,1280]{1,0:T(8,128)(2,1)} %fusion.23), channel_id=1, source_target_pairs={{0,1},{1,0},{2,3},{3,2},{4,5},{5,4},{6,7},{7,6},{8,9},{9,8},{10,11... | collective-permute-start | bytes 3686408 | tf_op jit(solution)/shard_map/ppermute | solution.py:581
  328.1 16.9 %collective-permute-start.26 = (bf16[240,1280]{1,0:T(8,128)(2,1)}, bf16[240,1280]{1,0:T(8,128)(2,1)S(1)}, u32[]{:S(2)}, u32[]{:S(2)}) collective-permute-start(bf16[240,1280]{1,0:T(8,128)(2,1)} %get-tuple-element.204), channel_id=1, source_target_pairs={{0,4},{2,6},{4,0},{6,2},{8,12},{10,14},{12,8},{14,10},{16,20},{18,... | collective-permute-start | bytes 1843208 | tf_op jit(solution)/shard_map/ppermute | solution.py:585
  344.4 16.7 %collective-permute-start.29 = (bf16[240,1280]{1,0:T(8,128)(2,1)S(1)}, bf16[240,1280]{1,0:T(8,128)(2,1)S(1)}, u32[]{:S(2)}, u32[]{:S(2)}) collective-permute-start(bf16[240,1280]{1,0:T(8,128)(2,1)S(1)} %pad_maximum_fusion.4.refs_0_), channel_id=1, source_target_pairs={{0,4},{2,6},{4,0},{6,2},{8,12},{10,14},{12,8},{14,10},{16,20},{18,... | collective-permute-start | bytes 1843208 | tf_op jit(solution)/shard_map/ppermute | solution.py:585
  354.9 18.9 %collective-permute-start.31 = (bf16[240,1280]{1,0:T(8,128)(2,1)S(1)}, bf16[240,1280]{1,0:T(8,128)(2,1)S(1)}, u32[]{:S(2)}, u32[]{:S(2)}) collective-permute-start(bf16[240,1280]{1,0:T(8,128)(2,1)S(1)} %get-tuple-element.202), channel_id=1, source_target_pairs={{0,4},{2,6},{4,0},{6,2},{8,12},{10,14},{12,8},{14,10},{16,20},{18,... | collective-permute-start | bytes 1843208 | tf_op jit(solution)/shard_map/ppermute | solution.py:585
  355.9 28.3 %collective-permute-start.32 = (bf16[480,1280]{1,0:T(8,128)(2,1)S(1)}, bf16[480,1280]{1,0:T(8,128)(2,1)S(1)}, u32[]{:S(2)}, u32[]{:S(2)}) collective-permute-start(bf16[480,1280]{1,0:T(8,128)(2,1)S(1)} %fusion.24), channel_id=1, source_target_pairs={{0,1},{1,0},{2,3},{3,2},{4,5},{5,4},{6,7},{7,6},{8,9},{9,8},{10,11... | collective-permute-start | bytes 3686408 | tf_op jit(solution)/shard_map/ppermute | solution.py:581
  361.2 24.5 %collective-permute-start.33 = (bf16[240,640]{1,0:T(8,128)(2,1)S(1)}, bf16[240,640]{1,0:T(8,128)(2,1)S(1)}, u32[]{:S(2)}, u32[]{:S(2)}) collective-permute-start(bf16[240,640]{1,0:T(8,128)(2,1)S(1)} %add_convert_fusion.15), channel_id=1, source_target_pairs={{0,16},{2,18},{4,20},{6,22},{8,24},{10,26},{12,28},{14,30},{16,0},... | collective-permute-start | bytes 921608 | tf_op jit(solution)/shard_map/ppermute | solution.py:585
  386.5 18.5 %collective-permute-start.37 = (bf16[240,1280]{1,0:T(8,128)(2,1)S(1)}, bf16[240,1280]{1,0:T(8,128)(2,1)S(1)}, u32[]{:S(2)}, u32[]{:S(2)}) collective-permute-start(bf16[240,1280]{1,0:T(8,128)(2,1)S(1)} %pad_maximum_fusion.4.refs_0_), channel_id=1, source_target_pairs={{0,2},{2,0},{4,6},{6,4},{8,10},{10,8},{12,14},{14,12},{16,18},{18,... | collective-permute-start | bytes 1843208 | tf_op jit(solution)/shard_map/ppermute | solution.py:585
  386.5 18.4 %collective-permute-start.38 = (bf16[240,1280]{1,0:T(8,128)(2,1)}, bf16[240,1280]{1,0:T(8,128)(2,1)S(1)}, u32[]{:S(2)}, u32[]{:S(2)}) collective-permute-start(bf16[240,1280]{1,0:T(8,128)(2,1)} %copy-done.26), channel_id=1, source_target_pairs={{0,2},{2,0},{4,6},{6,4},{8,10},{10,8},{12,14},{14,12},{16,18},{18,... | collective-permute-start | bytes 1843208 | tf_op jit(solution)/shard_map/ppermute | solution.py:585
  387.0 16.0 %collective-permute-start.36 = (bf16[240,1280]{1,0:T(8,128)(2,1)}, bf16[240,1280]{1,0:T(8,128)(2,1)S(1)}, u32[]{:S(2)}, u32[]{:S(2)}) collective-permute-start(bf16[240,1280]{1,0:T(8,128)(2,1)} %get-tuple-element.200), channel_id=1, source_target_pairs={{0,4},{2,6},{4,0},{6,2},{8,12},{10,14},{12,8},{14,10},{16,20},{18,... | collective-permute-start | bytes 1843208 | tf_op jit(solution)/shard_map/ppermute | solution.py:585
  389.5 18.6 %collective-permute-start.39 = (bf16[240,640]{1,0:T(8,128)(2,1)S(1)}, bf16[240,640]{1,0:T(8,128)(2,1)S(1)}, u32[]{:S(2)}, u32[]{:S(2)}) collective-permute-start(bf16[240,640]{1,0:T(8,128)(2,1)S(1)} %add_convert_fusion.13), channel_id=1, source_target_pairs={{0,16},{2,18},{4,20},{6,22},{8,24},{10,26},{12,28},{14,30},{16,0},... | collective-permute-start | bytes 921608 | tf_op jit(solution)/shard_map/ppermute | solution.py:585
  408.7 21.7 %collective-permute-start.43 = (bf16[240,1280]{1,0:T(8,128)(2,1)S(1)}, bf16[240,1280]{1,0:T(8,128)(2,1)S(1)}, u32[]{:S(2)}, u32[]{:S(2)}) collective-permute-start(bf16[240,1280]{1,0:T(8,128)(2,1)S(1)} %pad_maximum_fusion.5.refs_0_), channel_id=1, source_target_pairs={{0,4},{2,6},{4,0},{6,2},{8,12},{10,14},{12,8},{14,10},{16,20},{18,... | collective-permute-start | bytes 1843208 | tf_op jit(solution)/shard_map/ppermute | solution.py:585
  429.9 16.7 %collective-permute-start.46 = (bf16[240,1280]{1,0:T(8,128)(2,1)S(1)}, bf16[240,1280]{1,0:T(8,128)(2,1)S(1)}, u32[]{:S(2)}, u32[]{:S(2)}) collective-permute-start(bf16[240,1280]{1,0:T(8,128)(2,1)S(1)} %pad_maximum_fusion.6.refs_0_), channel_id=1, source_target_pairs={{0,4},{2,6},{4,0},{6,2},{8,12},{10,14},{12,8},{14,10},{16,20},{18,... | collective-permute-start | bytes 1843208 | tf_op jit(solution)/shard_map/ppermute | solution.py:585
  430.6 16.1 %collective-permute-start.54 = (bf16[2,960]{1,0:T(2,128)(2,1)S(1)}, bf16[2,960]{1,0:T(2,128)(2,1)S(1)}, u32[]{:S(2)}, u32[]{:S(2)}) collective-permute-start(bf16[2,960]{1,0:T(2,128)(2,1)S(1)} %add_convert_fusion.21), channel_id=1, source_target_pairs={{0,4},{2,6},{4,0},{6,2},{8,12},{10,14},{12,8},{14,10},{16,20},{18,... | collective-permute-start | bytes 11528 | tf_op jit(solution)/shard_map/ppermute | solution.py:585
  435.8 21.2 %collective-permute-start.49 = (bf16[240,1280]{1,0:T(8,128)(2,1)S(1)}, bf16[240,1280]{1,0:T(8,128)(2,1)S(1)}, u32[]{:S(2)}, u32[]{:S(2)}) collective-permute-start(bf16[240,1280]{1,0:T(8,128)(2,1)S(1)} %pad_maximum_fusion.6.refs_0_), channel_id=1, source_target_pairs={{0,2},{2,0},{4,6},{6,4},{8,10},{10,8},{12,14},{14,12},{16,18},{18,... | collective-permute-start | bytes 1843208 | tf_op jit(solution)/shard_map/ppermute | solution.py:585
  435.9 25.3 %collective-permute-start.45 = (bf16[240,1280]{1,0:T(8,128)(2,1)S(1)}, bf16[240,1280]{1,0:T(8,128)(2,1)S(1)}, u32[]{:S(2)}, u32[]{:S(2)}) collective-permute-start(bf16[240,1280]{1,0:T(8,128)(2,1)S(1)} %pad_maximum_fusion.7.refs_0_), channel_id=1, source_target_pairs={{0,4},{2,6},{4,0},{6,2},{8,12},{10,14},{12,8},{14,10},{16,20},{18,... | collective-permute-start | bytes 1843208 | tf_op jit(solution)/shard_map/ppermute | solution.py:585
  (109 other events, 867.9 us)

commit v5 on v4

--- a/solution.py
+++ b/solution.py
@@ -965,9 +965,9 @@
             mixed.step(queue)
             gate.step(queue)
             mixed.step(queue)
+            up.step(queue)
             (grad_gate,) = assemble(places, [after(gate.pieces[0], *queue), *gate.pieces[1:]], False)
             queue.append(grad_gate)
-            up.step(queue)
             (grad_up,) = assemble(places, [after(up.pieces[0], *queue), *up.pieces[1:]], False)
             queue.append(grad_up)
             mixed.step(queue)

time: 476 us -> 481 us (1.011)
  waiting for transfers between devices: 105 us -> 111 us
    unnamed x168 -> x164, local copies, waits for them, and re-layouts: 33.1 us -> 33.1 us
  transfers between devices with their start and end apart: 58 -> 58, of which waited for: 25 -> 22; matrix products, arithmetic and copies ran while one was open for 9% -> 9% of each run, Pallas kernels for 25% -> 26%
where the time goes in v5:
time: 481 us; the launch traced here: 473 us
  Pallas kernels  204 us (42%)
  waiting for transfers between devices  111 us (23%)
  starting transfers between devices  51.2 us (11%)
  local copies, waits for them, and re-layouts  47.6 us (10%)
  matrix products  29.7 us (6%)
  other arithmetic  27.4 us (6%)
    ppermute x47, waiting for transfers between devices, swap_dp(): return lax.ppermute(value, 'dp', [(i, i ^ bit) for i in range(size)])  67.8 us
    pallas_call x2, Pallas kernels, ffn_back(): pl.pallas_call(ffn_back_kernel, grid=(hidden // CHUNK,), in_specs=[full,...  49.3 us
    ppermute x11, waiting for transfers between devices, swap_fsdp(): return lax.ppermute(value, 'fsdp', [(0, 1), (1, 0)])  43.1 us
    pallas_call x3, Pallas kernels, weight_grad(): pl.pallas_call(partial(weight_grad_kernel, left_fsdp, False), grid_spec=p...  37.7 us
    ppermute x47, starting transfers between devices, swap_dp(): return lax.ppermute(value, 'dp', [(i, i ^ bit) for i in range(size)])  36.8 us
    unnamed x164, local copies, waits for them, and re-layouts  33.1 us
    dot_general x9, matrix products, dot(): lax.dot_general(left, right, ((contract[:1], contract[1:]), ((), ())), pr...  29.7 us
    pallas_call x2, Pallas kernels, attention_back(): pl.pallas_call(attention_back_kernel, grid=(KEY_VALUE_HEADS,), in_specs=[...  28.7 us
  transfers between devices with their start and end apart: 58, of which 22 were waited for; matrix products, arithmetic and copies ran while one was open for 9% of the time, Pallas kernels for 26%

profile of v5, /device:TPU:0, one launch (start us, length us, event | category | flops | bytes accessed | tf_op | source)
XLA Modules:
  0.0 473.1 jit_solution(11155950571562037967)
XLA Ops:
  22.9 6.9 %collective-permute-done.1.refs_3_ = bf16[240,1600]{1,0:T(8,128)(2,1)} collective-permute-done((bf16[240,1600]{1,0:T(8,128)(2,1)}, bf16[240,1600]{1,0:T(8,128)(2,1)}, u32[]{:S(2)}, u32[]{:S(2)}) %collective-permute-start.1) | collective-permute-done | bytes 768032 | tf_op jit(solution)/shard_map/ppermute | solution.py:581
  29.8 10.5 %collective-permute-done.3 = bf16[2,480]{1,0:T(2,128)(2,1)S(1)} collective-permute-done((bf16[2,480]{1,0:T(2,128)(2,1)S(1)}, bf16[2,480]{1,0:T(2,128)(2,1)S(1)}, u32[]{:S(2)}, u32[]{:S(2)}) %collective-permute-start.3) | collective-permute-done | bytes 1952 | tf_op jit(solution)/shard_map/ppermute | solution.py:581
  58.8 11.5 %attention.2 = (bf16[960,768]{1,0:T(8,128)(2,1)S(1)}, f32[5,8,768]{2,1,0:T(8,128)S(1)}) custom-call(s32[1,768]{1,0:T(1,128)S(1)} %reduce_sum.75.start_ref, bf16[1600,768]{1,0:T(8,128)(2,1)S(1)} %pad_maximum_fusion.query_ref.key_ref.value_ref, bf16[1600,768]{1,0:T(8,128)(2,1)S(1)} %pad_maximum_fusion.query_ref.key_ref.value_ref, ...), custom_call_target="tpu_custom_call" | custom-call | flops 6000000000 | bytes 4000000 | tf_op jit(solution)/shard_map/attention/pallas_call | solution.py:80
  83.2 3.9 collective-permute-done.14.refs_3_
  93.7 13.1 %ffn_up.1 = (bf16[960,768]{1,0:T(8,128)(2,1)}, bf16[768,2560]{1,0:T(8,128)(2,1)}, bf16[768,2560]{1,0:T(8,128)(2,1)}, bf16[768,2560]{1,0:T(8,128)(2,1)}) custom-call(f32[960,768]{1,0:T(8,128)S(1)} %copy-done.32, f32[960,1]{1,0:T(8,128)S(1)} %copy.49.gain_ref, bf16[960,2560]{1,0:T(8,128)(2,1)S(1)} %bitcast.122, bf16[960,2560]{1,0:T(8,128)(2,1)S(1)} %join.8.up_w_ref), custom_call_target="tpu_custom_call" | custom-call | flops 7549747200 | bytes 30000000 | tf_op jit(solution)/shard_map/ffn_up/pallas_call | solution.py:280
  109.8 7.9 %multiply_reduce_fusion.2 = (f32[768]{0:T(1024)S(1)}, f32[960,768]{1,0:T(8,128)S(1)}) fusion(f32[960,768]{1,0:T(8,128)S(1)} %copy-done.32, bf16[960,2560]{1,0:T(8,128)(2,1)S(1)} %join.9.down_w_ref, bf16[768,2560]{1,0:T(8,128)(2,1)} %get-tuple-element.113.right2_ref), kind=kOutput, calls=%fused_computation.22 | convolution fusion | flops 3777084672 | bytes 14748672 | tf_op jit(solution)/shard_map/dot_general | solution.py:31
  124.9 11.3 %attention.3 = (bf16[960,768]{1,0:T(8,128)(2,1)S(1)}, f32[5,8,768]{2,1,0:T(8,128)S(1)}) custom-call(s32[1,768]{1,0:T(1,128)S(1)} %reduce_sum.75.start_ref, bf16[1600,768]{1,0:T(8,128)(2,1)S(1)} %pad_maximum_fusion.1.query_ref.key_ref.value_ref, bf16[1600,768]{1,0:T(8,128)(2,1)S(1)} %pad_maximum_fusion.1.query_ref.key_ref.value_ref, ...), custom_call_target="tpu_custom_call" | custom-call | flops 6000000000 | bytes 4000000 | tf_op jit(solution)/shard_map/attention/pallas_call | solution.py:80
  138.8 16.3 %ffn.1 = (f32[960,768]{1,0:T(8,128)S(1)}, bf16[960,768]{1,0:T(8,128)(2,1)}, bf16[768,2560]{1,0:T(8,128)(2,1)}, bf16[768,2560]{1,0:T(8,128)(2,1)}, bf16[768,2560]{1,0:T(8,128)(2,1)}) custom-call(f32[960,768]{1,0:T(8,128)S(1)} %convolution_add_fusion.middle_ref, f32[960,1]{1,0:T(8,128)S(1)} %copy-done.27, bf16[960,2560]{1,0:T(8,128)(2,1)S(1)} %bitcast.122, ...), custom_call_target="tpu_custom_call" | custom-call | flops 11324620800 | bytes 40000000 | tf_op jit(solution)/shard_map/ffn/pallas_call | solution.py:233
  158.8 24.3 %ffn_back.2 = (f32[960,768]{1,0:T(8,128)}, bf16[960,768]{1,0:T(8,128)(2,1)S(1)}, bf16[768,2560]{1,0:T(8,128)(2,1)}, bf16[768,2560]{1,0:T(8,128)(2,1)}, f32[960,1]{1,0:T(8,128)S(1)}, /*index=5*/bf16[960,768]{1,0:T(8,128)(2,1)}) custom-call(f32[960,768]{1,0:T(8,128)S(1)} %convert_bitcast_fusion.grad_ref, f32[960,768]{1,0:T(8,128)S(1)} %convolution_add_fusion.middle_ref, ...), custom_call_target="tpu_custom_call" | custom-call | flops 11324620800 | bytes 50000000 | tf_op jit(solution)/shard_map/ffn_back/pallas_call | solution.py:350
  185.2 14.4 %attention_back.2.qkv_ref = bf16[1600,768]{1,0:T(8,128)(2,1)S(1)} custom-call(s32[1,768]{1,0:T(1,128)S(1)} %reduce_sum.75.start_ref, f32[32,768]{1,0:T(8,128)S(1)} %get-tuple-element.225.cosine_ref, f32[32,768]{1,0:T(8,128)S(1)} %get-tuple-element.226.sine_ref, bf16[1600,768]{1,0:T(8,128)(2,1)S(1)} %pad_maximum_fusion.1.query_ref.key_ref.value_ref, ...), custom_call_target="tpu_custom_call" | custom-call | flops 8999999488 | bytes 9000000 | tf_op jit(solution)/shard_map/attention_back/pallas_call | solution.py:158
  206.5 12.3 %weight_grad.3 = (bf16[2,480,1280]{2,1,0:T(8,128)(2,1)S(1)}, bf16[2,480,1280]{2,1,0:T(8,128)(2,1)S(1)}) custom-call(s32[5]{0:T(128)S(1)} %stack.44.places_ref, bf16[960,768]{1,0:T(8,128)(2,1)S(1)} %copy-done.55, bf16[768,2560]{1,0:T(8,128)(2,1)S(1)} %copy-done.54, bf16[960,768]{1,0:T(8,128)(2,1)S(1)} %get-tuple-element.193.left2_ref, ...), custom_call_target="tpu_custom_call" | custom-call | flops 7549747200 | bytes 24576000 | tf_op jit(solution)/shard_map/weight_grad/pallas_call | solution.py:416
  219.0 4.6 collective-permute-done.17
  231.0 25.0 %ffn_back.3 = (f32[960,768]{1,0:T(8,128)}, bf16[960,768]{1,0:T(8,128)(2,1)S(1)}, bf16[768,2560]{1,0:T(8,128)(2,1)}, bf16[768,2560]{1,0:T(8,128)(2,1)}, f32[960,1]{1,0:T(8,128)S(1)}, /*index=5*/bf16[960,768]{1,0:T(8,128)(2,1)}) custom-call(f32[960,768]{1,0:T(8,128)S(1)} %get-tuple-element.127.grad_ref, f32[960,768]{1,0:T(8,128)S(1)} %copy-done.33, ...), custom_call_target="tpu_custom_call" | custom-call | flops 11324620800 | bytes 50000000 | tf_op jit(solution)/shard_map/ffn_back/pallas_call | solution.py:350
  262.4 12.2 %weight_grad.4 = (bf16[2,480,1280]{2,1,0:T(8,128)(2,1)S(1)}, bf16[2,480,1280]{2,1,0:T(8,128)(2,1)S(1)}) custom-call(s32[5]{0:T(128)S(1)} %stack.44.places_ref, bf16[960,768]{1,0:T(8,128)(2,1)S(1)} %copy-done.57, bf16[768,2560]{1,0:T(8,128)(2,1)S(1)} %copy-done.49, bf16[960,768]{1,0:T(8,128)(2,1)S(1)} %copy-done.56, bf16[768,2560]{1,0:T(8,128)(2,1)S(1)} %copy-done.51), custom_call_target="tpu_custom_call" | custom-call | flops 7549747200 | bytes 24576000 | tf_op jit(solution)/shard_map/weight_grad/pallas_call | solution.py:416
  283.3 13.2 %weight_grad.5 = (bf16[2,480,1280]{2,1,0:T(8,128)(2,1)S(1)}, bf16[2,480,1280]{2,1,0:T(8,128)(2,1)}) custom-call(s32[5]{0:T(128)S(1)} %stack.44.places_ref, bf16[960,768]{1,0:T(8,128)(2,1)S(1)} %copy-done.57, bf16[768,2560]{1,0:T(8,128)(2,1)S(1)} %copy-done.48, bf16[960,768]{1,0:T(8,128)(2,1)S(1)} %copy-done.56, bf16[768,2560]{1,0:T(8,128)(2,1)S(1)} %copy-done.50), custom_call_target="tpu_custom_call" | custom-call | flops 7549747200 | bytes 24576000 | tf_op jit(solution)/shard_map/weight_grad/pallas_call | solution.py:416
  309.2 14.3 %attention_back.3.qkv2_ref = bf16[1600,768]{1,0:T(8,128)(2,1)S(1)} custom-call(s32[1,768]{1,0:T(1,128)S(1)} %reduce_sum.75.start_ref, f32[32,768]{1,0:T(8,128)S(1)} %get-tuple-element.225.cosine_ref, f32[32,768]{1,0:T(8,128)S(1)} %get-tuple-element.226.sine_ref, bf16[1600,768]{1,0:T(8,128)(2,1)S(1)} %copy-done.16, bf16[1600,768]{1,0:T(8,128)(2,1)S(1)} %copy-done.16, ...), custom_call_target="tpu_custom_call" | custom-call | flops 8999999488 | bytes 9000000 | tf_op jit(solution)/shard_map/attention_back/pallas_call | solution.py:158
  323.6 6.6 %collective-permute-done.24 = bf16[480,1280]{1,0:T(8,128)(2,1)S(1)} collective-permute-done((bf16[480,1280]{1,0:T(8,128)(2,1)}, bf16[480,1280]{1,0:T(8,128)(2,1)S(1)}, u32[]{:S(2)}, u32[]{:S(2)}) %collective-permute-start.24) | collective-permute-done | bytes 1228832 | tf_op jit(solution)/shard_map/ppermute | solution.py:581
  333.7 10.8 %mixed_grad.1 = (bf16[2,480,1280]{2,1,0:T(8,128)(2,1)S(1)}, bf16[2,480,1280]{2,1,0:T(8,128)(2,1)S(1)}) custom-call(s32[5]{0:T(128)S(1)} %stack.44.places_ref, bf16[960,768]{1,0:T(8,128)(2,1)S(1)} %copy-done.36, bf16[960,768]{1,0:T(8,128)(2,1)S(1)} %copy-done.43, bf16[960,768]{1,0:T(8,128)(2,1)S(1)} %copy-done.25, bf16[1600,768]{1,0:T(8,128)(2,1)S(1)} %copy-done.41, ...), custom_call_target="tpu_custom_call" | custom-call | flops 7549747200 | bytes 24576000 | tf_op jit(solution)/shard_map/mixed_grad/pallas_call | solution.py:462
  351.5 4.8 %collective-permute-done.27 = bf16[480,1280]{1,0:T(8,128)(2,1)} collective-permute-done((bf16[480,1280]{1,0:T(8,128)(2,1)S(1)}, bf16[480,1280]{1,0:T(8,128)(2,1)}, u32[]{:S(2)}, u32[]{:S(2)}) %collective-permute-start.27) | collective-permute-done | bytes 1228832 | tf_op jit(solution)/shard_map/ppermute | solution.py:581
  367.4 10.0 %collective-permute-done.31 = bf16[240,1280]{1,0:T(8,128)(2,1)S(1)} collective-permute-done((bf16[240,1280]{1,0:T(8,128)(2,1)S(1)}, bf16[240,1280]{1,0:T(8,128)(2,1)S(1)}, u32[]{:S(2)}, u32[]{:S(2)}) %collective-permute-start.31) | collective-permute-done | bytes 614432 | tf_op jit(solution)/shard_map/ppermute | solution.py:585
  378.4 9.5 %collective-permute-done.32 = bf16[480,1280]{1,0:T(8,128)(2,1)S(1)} collective-permute-done((bf16[480,1280]{1,0:T(8,128)(2,1)S(1)}, bf16[480,1280]{1,0:T(8,128)(2,1)S(1)}, u32[]{:S(2)}, u32[]{:S(2)}) %collective-permute-start.32) | collective-permute-done | bytes 1228832 | tf_op jit(solution)/shard_map/ppermute | solution.py:581
  391.3 5.1 %collective-permute-done.35 = bf16[240,640]{1,0:T(8,128)(2,1)S(1)} collective-permute-done((bf16[240,640]{1,0:T(8,128)(2,1)S(1)}, bf16[240,640]{1,0:T(8,128)(2,1)S(1)}, u32[]{:S(2)}, u32[]{:S(2)}) %collective-permute-start.35) | collective-permute-done | bytes 307232 | tf_op jit(solution)/shard_map/ppermute | solution.py:585
  400.1 5.9 %collective-permute-done.36 = bf16[240,1280]{1,0:T(8,128)(2,1)S(1)} collective-permute-done((bf16[240,1280]{1,0:T(8,128)(2,1)S(1)}, bf16[240,1280]{1,0:T(8,128)(2,1)S(1)}, u32[]{:S(2)}, u32[]{:S(2)}) %collective-permute-start.36) | collective-permute-done | bytes 614432 | tf_op jit(solution)/shard_map/ppermute | solution.py:585
  413.7 3.6 collective-permute-done.40
  419.2 7.5 %collective-permute-done.41 = bf16[240,640]{1,0:T(8,128)(2,1)S(1)} collective-permute-done((bf16[240,640]{1,0:T(8,128)(2,1)S(1)}, bf16[240,640]{1,0:T(8,128)(2,1)S(1)}, u32[]{:S(2)}, u32[]{:S(2)}) %collective-permute-start.41) | collective-permute-done | bytes 307232 | tf_op jit(solution)/shard_map/ppermute | solution.py:585
  426.9 7.2 %collective-permute-done.42 = bf16[240,640]{1,0:T(8,128)(2,1)S(1)} collective-permute-done((bf16[240,640]{1,0:T(8,128)(2,1)S(1)}, bf16[240,640]{1,0:T(8,128)(2,1)S(1)}, u32[]{:S(2)}, u32[]{:S(2)}) %collective-permute-start.42) | collective-permute-done | bytes 307232 | tf_op jit(solution)/shard_map/ppermute | solution.py:585
  437.7 4.8 %collective-permute-done.55 = bf16[2,960]{1,0:T(2,128)(2,1)S(1)} collective-permute-done((bf16[2,960]{1,0:T(2,128)(2,1)S(1)}, bf16[2,960]{1,0:T(2,128)(2,1)S(1)}, u32[]{:S(2)}, u32[]{:S(2)}) %collective-permute-start.55) | collective-permute-done | bytes 3872 | tf_op jit(solution)/shard_map/ppermute | solution.py:585
  444.0 6.7 %collective-permute-done.46.refs_1_ = bf16[240,1280]{1,0:T(8,128)(2,1)} collective-permute-done((bf16[240,1280]{1,0:T(8,128)(2,1)S(1)}, bf16[240,1280]{1,0:T(8,128)(2,1)}, u32[]{:S(2)}, u32[]{:S(2)}) %collective-permute-start.46) | collective-permute-done | bytes 614432 | tf_op jit(solution)/shard_map/ppermute | solution.py:585
  453.7 4.4 assemble.5
  458.1 4.8 %assemble.6 = f32[480,2560]{1,0:T(8,128)} custom-call(s32[5]{0:T(128)S(1)} %stack.44.places_ref, bf16[240,1280]{1,0:T(8,128)(2,1)S(1)} %pad_maximum_fusion.6.refs_0_, bf16[240,1280]{1,0:T(8,128)(2,1)} %collective-permute-done.46.refs_1_, bf16[240,1280]{1,0:T(8,128)(2,1)} %collective-permute-done.49.refs_2_, bf16[240,1280]{1,0:T(8,128)(2,1)} %collective-permute-done.50.refs_3_), custom_call_target="tpu_custom_call" | custom-call | bytes 7372800 | tf_op jit(solution)/shard_map/assemble/pallas_call | solution.py:507
  463.0 4.0 collective-permute-done.45.refs_1_
  469.0 3.8 assemble.7
  (368 shorter events, 169.6 us)
Async XLA Ops:
  7.9 21.9 %collective-permute-start.1 = (bf16[240,1600]{1,0:T(8,128)(2,1)}, bf16[240,1600]{1,0:T(8,128)(2,1)}, u32[]{:S(2)}, u32[]{:S(2)}) collective-permute-start(bf16[240,1600]{1,0:T(8,128)(2,1)} %concatenate.28), channel_id=1, source_target_pairs={{0,1},{1,0},{2,3},{3,2},{4,5},{5,4},{6,7},{7,6},{8,9},{9,8},{10,11... | collective-permute-start | bytes 2304008 | tf_op jit(solution)/shard_map/ppermute | solution.py:581
  12.7 37.6 %collective-permute-start = (bf16[240,960]{1,0:T(8,128)(2,1)}, bf16[240,960]{1,0:T(8,128)(2,1)}, u32[]{:S(2)}, u32[]{:S(2)}) collective-permute-start(bf16[240,960]{1,0:T(8,128)(2,1)} %constant_dynamic-slice_fusion.21), channel_id=1, source_target_pairs={{0,1},{1,0},{2,3},{3,2},{4,5},{5,4},{6,7},{7,6},{8,9},{9,8},{10,11... | collective-permute-start | bytes 1382408 | tf_op jit(solution)/shard_map/ppermute | solution.py:581
  12.8 27.6 %collective-permute-start.3 = (bf16[2,480]{1,0:T(2,128)(2,1)S(1)}, bf16[2,480]{1,0:T(2,128)(2,1)S(1)}, u32[]{:S(2)}, u32[]{:S(2)}) collective-permute-start(bf16[2,480]{1,0:T(2,128)(2,1)S(1)} %pad_maximum_fusion.8), channel_id=1, source_target_pairs={{0,1},{1,0},{2,3},{3,2},{4,5},{5,4},{6,7},{7,6},{8,9},{9,8},{10,11... | collective-permute-start | bytes 5768 | tf_op jit(solution)/shard_map/ppermute | solution.py:581
  15.7 37.8 %collective-permute-start.8 = (bf16[480,640]{1,0:T(8,128)(2,1)}, bf16[480,640]{1,0:T(8,128)(2,1)}, u32[]{:S(2)}, u32[]{:S(2)}) collective-permute-start(bf16[480,640]{1,0:T(8,128)(2,1)} %constant_dynamic-slice_fusion.20), channel_id=1, source_target_pairs={{0,1},{1,0},{2,3},{3,2},{4,5},{5,4},{6,7},{7,6},{8,9},{9,8},{10,11... | collective-permute-start | bytes 1843208 | tf_op jit(solution)/shard_map/ppermute | solution.py:581
  17.7 52.7 %collective-permute-start.11 = (bf16[480,640]{1,0:T(8,128)(2,1)}, bf16[480,640]{1,0:T(8,128)(2,1)}, u32[]{:S(2)}, u32[]{:S(2)}) collective-permute-start(bf16[480,640]{1,0:T(8,128)(2,1)} %constant_dynamic-slice_fusion.19), channel_id=1, source_target_pairs={{0,1},{1,0},{2,3},{3,2},{4,5},{5,4},{6,7},{7,6},{8,9},{9,8},{10,11... | collective-permute-start | bytes 1843208 | tf_op jit(solution)/shard_map/ppermute | solution.py:581
  53.6 16.8 %collective-permute-start.10 = (bf16[480,640]{1,0:T(8,128)(2,1)}, bf16[480,640]{1,0:T(8,128)(2,1)S(1)}, u32[]{:S(2)}, u32[]{:S(2)}) collective-permute-start(bf16[480,640]{1,0:T(8,128)(2,1)} %collective-permute-done.8.refs_1_), channel_id=1, source_target_pairs={{0,4},{2,6},{4,0},{6,2},{8,12},{10,14},{12,8},{14,10},{16,20},{18,... | collective-permute-start | bytes 1843208 | tf_op jit(solution)/shard_map/ppermute | solution.py:585
  56.8 22.2 %collective-permute-start.5 = (bf16[240,1280]{1,0:T(8,128)(2,1)S(1)}, bf16[240,1280]{1,0:T(8,128)(2,1)S(1)}, u32[]{:S(2)}, u32[]{:S(2)}) collective-permute-start(bf16[240,1280]{1,0:T(8,128)(2,1)S(1)} %constant_dynamic-slice_fusion.18), channel_id=1, source_target_pairs={{0,1},{1,0},{2,3},{3,2},{4,5},{5,4},{6,7},{7,6},{8,9},{9,8},{10,11... | collective-permute-start | bytes 1843208 | tf_op jit(solution)/shard_map/ppermute | solution.py:581
  58.3 20.6 %collective-permute-start.9 = (bf16[480,640]{1,0:T(8,128)(2,1)}, bf16[480,640]{1,0:T(8,128)(2,1)S(1)}, u32[]{:S(2)}, u32[]{:S(2)}) collective-permute-start(bf16[480,640]{1,0:T(8,128)(2,1)} %collective-permute-done.8.refs_1_), channel_id=1, source_target_pairs={{0,2},{2,0},{4,6},{6,4},{8,10},{10,8},{12,14},{14,12},{16,18},{18,... | collective-permute-start | bytes 1843208 | tf_op jit(solution)/shard_map/ppermute | solution.py:585
  70.5 16.5 %collective-permute-start.14 = (bf16[480,640]{1,0:T(8,128)(2,1)}, bf16[480,640]{1,0:T(8,128)(2,1)}, u32[]{:S(2)}, u32[]{:S(2)}) collective-permute-start(bf16[480,640]{1,0:T(8,128)(2,1)} %collective-permute-done.11.refs_1_), channel_id=1, source_target_pairs={{0,8},{2,10},{4,12},{6,14},{8,0},{10,2},{12,4},{14,6},{16,24},{18,... | collective-permute-start | bytes 1843208 | tf_op jit(solution)/shard_map/ppermute | solution.py:585
  72.1 16.3 %collective-permute-start.13 = (bf16[480,640]{1,0:T(8,128)(2,1)}, bf16[480,640]{1,0:T(8,128)(2,1)}, u32[]{:S(2)}, u32[]{:S(2)}) collective-permute-start(bf16[480,640]{1,0:T(8,128)(2,1)} %collective-permute-done.11.refs_1_), channel_id=1, source_target_pairs={{0,2},{2,0},{4,6},{6,4},{8,10},{10,8},{12,14},{14,12},{16,18},{18,... | collective-permute-start | bytes 1843208 | tf_op jit(solution)/shard_map/ppermute | solution.py:585
  87.3 19.9 %collective-permute-start.6 = (bf16[240,1280]{1,0:T(8,128)(2,1)S(1)}, bf16[240,1280]{1,0:T(8,128)(2,1)S(1)}, u32[]{:S(2)}, u32[]{:S(2)}) collective-permute-start(bf16[240,1280]{1,0:T(8,128)(2,1)S(1)} %collective-permute-done.5.refs_1_), channel_id=1, source_target_pairs={{0,2},{2,0},{4,6},{6,4},{8,10},{10,8},{12,14},{14,12},{16,18},{18,... | collective-permute-start | bytes 1843208 | tf_op jit(solution)/shard_map/ppermute | solution.py:585
  87.9 18.9 %collective-permute-start.7 = (bf16[240,1280]{1,0:T(8,128)(2,1)S(1)}, bf16[240,1280]{1,0:T(8,128)(2,1)S(1)}, u32[]{:S(2)}, u32[]{:S(2)}) collective-permute-start(bf16[240,1280]{1,0:T(8,128)(2,1)S(1)} %collective-permute-done.5.refs_1_), channel_id=1, source_target_pairs={{0,4},{2,6},{4,0},{6,2},{8,12},{10,14},{12,8},{14,10},{16,20},{18,... | collective-permute-start | bytes 1843208 | tf_op jit(solution)/shard_map/ppermute | solution.py:585
  225.5 30.5 %collective-permute-start.18 = (bf16[480,1280]{1,0:T(8,128)(2,1)}, bf16[480,1280]{1,0:T(8,128)(2,1)}, u32[]{:S(2)}, u32[]{:S(2)}) collective-permute-start(bf16[480,1280]{1,0:T(8,128)(2,1)} %fusion.21), channel_id=1, source_target_pairs={{0,1},{1,0},{2,3},{3,2},{4,5},{5,4},{6,7},{7,6},{8,9},{9,8},{10,11... | collective-permute-start | bytes 3686408 | tf_op jit(solution)/shard_map/ppermute | solution.py:581
  258.6 16.1 %collective-permute-start.19 = (bf16[240,1280]{1,0:T(8,128)(2,1)S(1)}, bf16[240,1280]{1,0:T(8,128)(2,1)S(1)}, u32[]{:S(2)}, u32[]{:S(2)}) collective-permute-start(bf16[240,1280]{1,0:T(8,128)(2,1)S(1)} %get-tuple-element.206), channel_id=1, source_target_pairs={{0,4},{2,6},{4,0},{6,2},{8,12},{10,14},{12,8},{14,10},{16,20},{18,... | collective-permute-start | bytes 1843208 | tf_op jit(solution)/shard_map/ppermute | solution.py:585
  279.9 16.6 %collective-permute-start.21 = (bf16[240,640]{1,0:T(8,128)(2,1)S(1)}, bf16[240,640]{1,0:T(8,128)(2,1)S(1)}, u32[]{:S(2)}, u32[]{:S(2)}) collective-permute-start(bf16[240,640]{1,0:T(8,128)(2,1)S(1)} %get-tuple-element.222), channel_id=1, source_target_pairs={{0,8},{2,10},{4,12},{6,14},{8,0},{10,2},{12,4},{14,6},{16,24},{18,... | collective-permute-start | bytes 921608 | tf_op jit(solution)/shard_map/ppermute | solution.py:585
  300.1 30.1 %collective-permute-start.24 = (bf16[480,1280]{1,0:T(8,128)(2,1)}, bf16[480,1280]{1,0:T(8,128)(2,1)S(1)}, u32[]{:S(2)}, u32[]{:S(2)}) collective-permute-start(bf16[480,1280]{1,0:T(8,128)(2,1)} %fusion.22), channel_id=1, source_target_pairs={{0,1},{1,0},{2,3},{3,2},{4,5},{5,4},{6,7},{7,6},{8,9},{9,8},{10,11... | collective-permute-start | bytes 3686408 | tf_op jit(solution)/shard_map/ppermute | solution.py:581
  301.7 21.9 %collective-permute-start.23 = (bf16[240,640]{1,0:T(8,128)(2,1)}, bf16[240,640]{1,0:T(8,128)(2,1)S(1)}, u32[]{:S(2)}, u32[]{:S(2)}) collective-permute-start(bf16[240,640]{1,0:T(8,128)(2,1)} %add_convert_fusion.17), channel_id=1, source_target_pairs={{0,16},{2,18},{4,20},{6,22},{8,24},{10,26},{12,28},{14,30},{16,0},... | collective-permute-start | bytes 921608 | tf_op jit(solution)/shard_map/ppermute | solution.py:585
  305.8 50.4 %collective-permute-start.27 = (bf16[480,1280]{1,0:T(8,128)(2,1)S(1)}, bf16[480,1280]{1,0:T(8,128)(2,1)}, u32[]{:S(2)}, u32[]{:S(2)}) collective-permute-start(bf16[480,1280]{1,0:T(8,128)(2,1)S(1)} %fusion.23), channel_id=1, source_target_pairs={{0,1},{1,0},{2,3},{3,2},{4,5},{5,4},{6,7},{7,6},{8,9},{9,8},{10,11... | collective-permute-start | bytes 3686408 | tf_op jit(solution)/shard_map/ppermute | solution.py:581
  331.7 16.9 %collective-permute-start.26 = (bf16[240,1280]{1,0:T(8,128)(2,1)}, bf16[240,1280]{1,0:T(8,128)(2,1)}, u32[]{:S(2)}, u32[]{:S(2)}) collective-permute-start(bf16[240,1280]{1,0:T(8,128)(2,1)} %get-tuple-element.204), channel_id=1, source_target_pairs={{0,4},{2,6},{4,0},{6,2},{8,12},{10,14},{12,8},{14,10},{16,20},{18,... | collective-permute-start | bytes 1843208 | tf_op jit(solution)/shard_map/ppermute | solution.py:585
  348.0 16.7 %collective-permute-start.29 = (bf16[240,1280]{1,0:T(8,128)(2,1)S(1)}, bf16[240,1280]{1,0:T(8,128)(2,1)S(1)}, u32[]{:S(2)}, u32[]{:S(2)}) collective-permute-start(bf16[240,1280]{1,0:T(8,128)(2,1)S(1)} %pad_maximum_fusion.4.refs_0_), channel_id=1, source_target_pairs={{0,4},{2,6},{4,0},{6,2},{8,12},{10,14},{12,8},{14,10},{16,20},{18,... | collective-permute-start | bytes 1843208 | tf_op jit(solution)/shard_map/ppermute | solution.py:585
  358.5 18.9 %collective-permute-start.31 = (bf16[240,1280]{1,0:T(8,128)(2,1)S(1)}, bf16[240,1280]{1,0:T(8,128)(2,1)S(1)}, u32[]{:S(2)}, u32[]{:S(2)}) collective-permute-start(bf16[240,1280]{1,0:T(8,128)(2,1)S(1)} %get-tuple-element.202), channel_id=1, source_target_pairs={{0,4},{2,6},{4,0},{6,2},{8,12},{10,14},{12,8},{14,10},{16,20},{18,... | collective-permute-start | bytes 1843208 | tf_op jit(solution)/shard_map/ppermute | solution.py:585
  359.5 28.4 %collective-permute-start.32 = (bf16[480,1280]{1,0:T(8,128)(2,1)S(1)}, bf16[480,1280]{1,0:T(8,128)(2,1)S(1)}, u32[]{:S(2)}, u32[]{:S(2)}) collective-permute-start(bf16[480,1280]{1,0:T(8,128)(2,1)S(1)} %fusion.24), channel_id=1, source_target_pairs={{0,1},{1,0},{2,3},{3,2},{4,5},{5,4},{6,7},{7,6},{8,9},{9,8},{10,11... | collective-permute-start | bytes 3686408 | tf_op jit(solution)/shard_map/ppermute | solution.py:581
  364.8 23.7 %collective-permute-start.33 = (bf16[240,640]{1,0:T(8,128)(2,1)S(1)}, bf16[240,640]{1,0:T(8,128)(2,1)S(1)}, u32[]{:S(2)}, u32[]{:S(2)}) collective-permute-start(bf16[240,640]{1,0:T(8,128)(2,1)S(1)} %add_convert_fusion.15), channel_id=1, source_target_pairs={{0,16},{2,18},{4,20},{6,22},{8,24},{10,26},{12,28},{14,30},{16,0},... | collective-permute-start | bytes 921608 | tf_op jit(solution)/shard_map/ppermute | solution.py:585
  389.1 22.5 %collective-permute-start.53 = (bf16[2,960]{1,0:T(2,128)(2,1)S(1)}, bf16[2,960]{1,0:T(2,128)(2,1)S(1)}, u32[]{:S(2)}, u32[]{:S(2)}) collective-permute-start(bf16[2,960]{1,0:T(2,128)(2,1)S(1)} %maximum_bitcast_fusion), channel_id=1, source_target_pairs={{0,2},{2,0},{4,6},{6,4},{8,10},{10,8},{12,14},{14,12},{16,18},{18,... | collective-permute-start | bytes 11528 | tf_op jit(solution)/shard_map/ppermute | solution.py:585
  389.2 18.7 %collective-permute-start.37 = (bf16[240,1280]{1,0:T(8,128)(2,1)S(1)}, bf16[240,1280]{1,0:T(8,128)(2,1)S(1)}, u32[]{:S(2)}, u32[]{:S(2)}) collective-permute-start(bf16[240,1280]{1,0:T(8,128)(2,1)S(1)} %pad_maximum_fusion.4.refs_0_), channel_id=1, source_target_pairs={{0,2},{2,0},{4,6},{6,4},{8,10},{10,8},{12,14},{14,12},{16,18},{18,... | collective-permute-start | bytes 1843208 | tf_op jit(solution)/shard_map/ppermute | solution.py:585
  389.7 18.2 %collective-permute-start.38 = (bf16[240,1280]{1,0:T(8,128)(2,1)S(1)}, bf16[240,1280]{1,0:T(8,128)(2,1)S(1)}, u32[]{:S(2)}, u32[]{:S(2)}) collective-permute-start(bf16[240,1280]{1,0:T(8,128)(2,1)S(1)} %collective-permute-done.29.refs_1_), channel_id=1, source_target_pairs={{0,2},{2,0},{4,6},{6,4},{8,10},{10,8},{12,14},{14,12},{16,18},{18,... | collective-permute-start | bytes 1843208 | tf_op jit(solution)/shard_map/ppermute | solution.py:585
  389.8 16.2 %collective-permute-start.36 = (bf16[240,1280]{1,0:T(8,128)(2,1)S(1)}, bf16[240,1280]{1,0:T(8,128)(2,1)S(1)}, u32[]{:S(2)}, u32[]{:S(2)}) collective-permute-start(bf16[240,1280]{1,0:T(8,128)(2,1)S(1)} %get-tuple-element.200), channel_id=1, source_target_pairs={{0,4},{2,6},{4,0},{6,2},{8,12},{10,14},{12,8},{14,10},{16,20},{18,... | collective-permute-start | bytes 1843208 | tf_op jit(solution)/shard_map/ppermute | solution.py:585
  411.6 22.6 %collective-permute-start.54 = (bf16[2,960]{1,0:T(2,128)(2,1)S(1)}, bf16[2,960]{1,0:T(2,128)(2,1)S(1)}, u32[]{:S(2)}, u32[]{:S(2)}) collective-permute-start(bf16[2,960]{1,0:T(2,128)(2,1)S(1)} %add_convert_fusion.21), channel_id=1, source_target_pairs={{0,4},{2,6},{4,0},{6,2},{8,12},{10,14},{12,8},{14,10},{16,20},{18,... | collective-permute-start | bytes 11528 | tf_op jit(solution)/shard_map/ppermute | solution.py:585
  413.1 30.2 %collective-permute-start.43 = (bf16[240,1280]{1,0:T(8,128)(2,1)S(1)}, bf16[240,1280]{1,0:T(8,128)(2,1)S(1)}, u32[]{:S(2)}, u32[]{:S(2)}) collective-permute-start(bf16[240,1280]{1,0:T(8,128)(2,1)S(1)} %pad_maximum_fusion.5.refs_0_), channel_id=1, source_target_pairs={{0,4},{2,6},{4,0},{6,2},{8,12},{10,14},{12,8},{14,10},{16,20},{18,... | collective-permute-start | bytes 1843208 | tf_op jit(solution)/shard_map/ppermute | solution.py:585
  417.4 16.7 %collective-permute-start.42 = (bf16[240,640]{1,0:T(8,128)(2,1)S(1)}, bf16[240,640]{1,0:T(8,128)(2,1)S(1)}, u32[]{:S(2)}, u32[]{:S(2)}) collective-permute-start(bf16[240,640]{1,0:T(8,128)(2,1)S(1)} %add_convert_fusion.11), channel_id=1, source_target_pairs={{0,16},{2,18},{4,20},{6,22},{8,24},{10,26},{12,28},{14,30},{16,0},... | collective-permute-start | bytes 921608 | tf_op jit(solution)/shard_map/ppermute | solution.py:585
  450.7 16.3 %collective-permute-start.45 = (bf16[240,1280]{1,0:T(8,128)(2,1)S(1)}, bf16[240,1280]{1,0:T(8,128)(2,1)S(1)}, u32[]{:S(2)}, u32[]{:S(2)}) collective-permute-start(bf16[240,1280]{1,0:T(8,128)(2,1)S(1)} %pad_maximum_fusion.7.refs_0_), channel_id=1, source_target_pairs={{0,4},{2,6},{4,0},{6,2},{8,12},{10,14},{12,8},{14,10},{16,20},{18,... | collective-permute-start | bytes 1843208 | tf_op jit(solution)/shard_map/ppermute | solution.py:585
  452.2 16.1 %collective-permute-start.57 = (bf16[2,960]{1,0:T(2,128)(2,1)S(1)}, bf16[2,960]{1,0:T(2,128)(2,1)S(1)}, u32[]{:S(2)}, u32[]{:S(2)}) collective-permute-start(bf16[2,960]{1,0:T(2,128)(2,1)S(1)} %add_convert_fusion.18), channel_id=1, source_target_pairs={{0,1},{1,0},{2,3},{3,2},{4,5},{5,4},{6,7},{7,6},{8,9},{9,8},{10,11... | collective-permute-start | bytes 11528 | tf_op jit(solution)/shard_map/ppermute | solution.py:581
  (107 other events, 926.6 us)
